TPU v7x, 128 devices: a whole 4x4x4 slice. The times are simulated.
128 devices in a mesh: gx: 8 (over y, core), gy: 16 (over x, z).
Axes of the slice: x: 4, y: 4, z: 4, core: 2. Of those that a mesh axis runs over, the one named last changes fastest.
Arguments:
- right_side: float32 [8, 16, 176, 1152], P('gx', 'gy'), may hold values from -6 to 6
- flex: bfloat16 [8, 16, 1152, 1152], P('gx', 'gy'), as said below
- stiff: bfloat16 [8, 16, 1152, 1152], P('gx', 'gy')
- coarse_inv: float32 [3072, 3072], P('gx', 'gy'), as said below
- corner_map: int32 [8, 16, 24], P('gx', 'gy'), may hold values from 0 to 3071
- side_rows: int32 [8, 16, 2], P('gx', 'gy'), may hold values from 1 to 288, as said below
Outputs:
- solution: float32 [8, 16, 176, 1152], P('gx', 'gy')
- residual: float32 [8, 16, 176, 1152], P('gx', 'gy')
- resid_norm: float32 [3, 176], replicated
Inputs may be any that keep to these rules, and one draw needn't show every extreme that they name: Entry 0 of side_rows at the first subdomain equals 288. flex and stiff are near one on the diagonal plus small full off-diagonal parts. coarse_inv is a dense matrix.
All inputs are finite; a program needn't handle non-finite values.
Results may differ from a plain program's by a relative error of at most 0.0056.
Values sent between devices are 32-bit elements; how exact they have to be, the bound alone decides.
No kernel may reach another device: no remote copies, remote signals or barrier semaphores. Data moves between devices by JAX's collectives and lax.ppermute only.
A program may use at most 64 MiB of HBM per device.

v0:
```python
import functools

import jax
import jax.numpy as jnp
from jax import lax
from jax.experimental import pallas as pl
from jax.experimental.pallas import tpu as pltpu
from jax.sharding import Mesh
from jax.sharding import PartitionSpec as P

ITERS = 3
GX = ("y", "c")
GY = ("x", "z")
ALL = ("y", "c", "x", "z")
NY, NC, NX, NZ = 4, 2, 4, 4
N_GX, N_GY = NY * NC, NX * NZ
SIDES = 4
TOP = 128
LANES = 128
TILE = 8
VMEM_BYTES = 16 * 2**20

cheb_center = 1.15
cheb_half = 0.85
cheb_sigma = cheb_center / cheb_half
F32 = jnp.float32
BF16 = jnp.bfloat16


def turned(array, axes, count, by):
    return lax.ppermute(array, axes, [(i, (i + by) % count) for i in range(count)])


def swapped(array, axes, count, shift):
    pairs = [(i, (((i + shift) ^ 1) - shift) % count) for i in range(count)]
    return lax.ppermute(array, axes, pairs)


def to_all(copies, axes):
    return lax.all_to_all(copies, axes, split_axis=0, concat_axis=0, tiled=True)


def vm():
    return pl.BlockSpec(memory_space=pltpu.VMEM)


def sm():
    return pl.BlockSpec(memory_space=pltpu.SMEM)


def call(body, outs, scalars=0, scratch=()):
    def run(*operands):
        held = [pltpu.with_memory_space_constraint(o, pltpu.VMEM) for o in operands[scalars:]]
        return pl.pallas_call(
            body,
            out_shape=outs,
            in_specs=[sm()] * scalars + [vm()] * len(held),
            out_specs=[vm() for _ in outs],
            scratch_shapes=scratch,
            compiler_params=pltpu.CompilerParams(vmem_limit_bytes=VMEM_BYTES),
        )(*operands[:scalars], *held)

    return run


def shape(*dims, dtype=F32):
    return pltpu.VMEM(dims, dtype)


def dot(a, b, contract=((1,), (0,))):
    return lax.dot_general(a, b, (contract, ((), ())), preferred_element_type=F32)


def split(a):
    high = a.astype(BF16)
    return high, (a - high.astype(F32)).astype(BF16)


def mark(pick, columns, held):
    corners = columns[0].shape[0]
    at = lax.broadcasted_iota(jnp.int32, (2 * corners, held), 1).astype(F32)
    for n in range(0, len(columns), 2):
        ids = jnp.concatenate(columns[n : n + 2], axis=0)
        pick[n * corners : (n + 2) * corners, :] = jnp.where(at == ids, 1.0, 0.0).astype(BF16)


def rows_kernel(where, ids_own, ids_other, *refs):
    blocks, own, other, pick = refs[:-3], refs[-3], refs[-2], refs[-1]
    my_y, my_c = where[0], where[1]
    held = blocks[0].shape[1]
    half = own.shape[1]
    corners = half // N_GY
    lists = [ids[...].T[:corners] for ids in (ids_own, ids_other)]
    total = 0.0
    for k, block in enumerate(blocks):
        base = ((((my_y + NY - k) % NY) * NC + my_c) * held).astype(F32)
        shifted = [ids - base for ids in lists]
        mark(pick, [ids[:, n : n + 1] for ids in shifted for n in range(N_GY)], held)
        for part in split(block[...]):
            total = total + dot(part, pick[...], ((1,), (1,)))
    own[...] = total[:, :half]
    other[...] = total[:, half:]


def cols_kernel(where, own, other, *refs):
    blocks, outs, pick = refs[:-5], refs[-5:-1], refs[-1]
    my_x, my_z = where[2], where[3]
    held = blocks[0].shape[0]
    half = outs[0].shape[1]
    last = own.shape[2] - 1
    columns = [v[n, :, last:] for v in (own, other) for n in range(v.shape[0])]
    total = 0.0
    for k, block in enumerate(blocks):
        base = ((my_x * NZ + (my_z + NZ - k) % NZ) * held).astype(F32)
        mark(pick, [ids - base for ids in columns], held)
        for part in split(block[...]):
            total = total + dot(pick[...], part)
    total = total.T
    for n in range(2):
        outs[2 * n][...], outs[2 * n + 1][...] = split(total[:, n * half : (n + 1) * half])


def pack(out, main, rest, count):
    side, wide = main.shape[0], rest.shape[1]
    half = side // 2
    out[0:side, :] = main
    out[side : side + half, 0:wide] = rest[:half]
    out[side : side + half, wide : 2 * wide] = rest[half:]
    out[side : side + half, 2 * wide :] = jnp.full((half, LANES - 2 * wide), count.astype(F32))


def first_kernel(where, ids, right, flex, flexed, extra, *sends):
    step = pl.program_id(0)

    @pl.when(step == 0)
    def _():
        column = jnp.broadcast_to(ids[...], (LANES, LANES)).T
        extra[...] = jnp.zeros_like(extra)
        extra[:, extra.shape[1] - LANES :] = column[: extra.shape[0]]

    side = flex.shape[0]
    odd_b, odd_a = where[3] % 2, where[1]
    direction = (right[...] / cheb_center).astype(BF16)
    part = dot(flex[...], direction, ((1,), (1,)))
    flexed[pl.ds(pl.multiple_of(step * side, side), side), :] = part
    for k, wanted in enumerate((1 - odd_b, odd_b, 3 - odd_a, 2 + odd_a)):

        @pl.when(step == wanted)
        def _():
            pack(sends[k], part[:, :LANES], part[:, LANES:], where[4 + k // 2])


def send_sides(where, flexed, *sends):
    side = flexed.shape[0] // SIDES
    odd_b, odd_a = where[3] % 2, where[1]
    for k, wanted in enumerate((1 - odd_b, odd_b, 3 - odd_a, 2 + odd_a)):
        rows = pl.ds(pl.multiple_of(wanted * side, 32), side)
        pack(sends[k], flexed[rows, 0:LANES], flexed[rows, LANES:], where[4 + k // 2])


def balance_kernel(where, flexed, in_a, in_b, in_c, in_y, stiff, extra, *refs):
    balanced, told, message = refs[-3:]
    side = flexed.shape[0] // SIDES
    loads = flexed.shape[1]
    wide = loads - LANES
    half = side // 2
    row = where[0] * NC + where[1]
    col = where[2] * NZ + where[3]
    odd_b, odd_a = where[3] % 2 == 1, where[1] == 1
    spot = (slice(side, side + 1), slice(2 * wide, 2 * wide + 1))
    count_west = jnp.where(odd_b, in_a[spot], in_b[spot])
    count_north = jnp.where(odd_a, in_c[spot], in_y[spot])
    count_east = jnp.full((1, 1), where[4].astype(F32))
    count_south = jnp.full((1, 1), where[5].astype(F32))

    for rows, lanes, there in (
        ((0, side), (0, LANES), ((0, side), (0, LANES))),
        ((0, half), (LANES, loads), ((side, side + half), (0, wide))),
        ((half, side), (LANES, loads), ((side, side + half), (wide, 2 * wide))),
    ):
        size = (rows[1] - rows[0], lanes[1] - lanes[0])
        at = (lax.broadcasted_iota(jnp.int32, size, 0) + rows[0]).astype(F32)
        a, b, c, y = (m[there[0][0] : there[0][1], there[1][0] : there[1][1]] for m in (in_a, in_b, in_c, in_y))
        west, east, north, south = (
            flexed[k * side + rows[0] : k * side + rows[1], lanes[0] : lanes[1]] for k in range(SIDES)
        )

        def half_jump(count, inside, ahead, behind):
            return jnp.where(jnp.logical_and(at < count, inside), 0.5 * (ahead - behind), 0.0)

        results = (
            west + half_jump(count_west, col > 0, jnp.where(odd_b, a, b), west),
            east - half_jump(count_east, col < N_GY - 1, east, jnp.where(odd_b, b, a)),
            north + half_jump(count_north, row > 0, jnp.where(odd_a, c, y), north),
            south - half_jump(count_south, row < N_GX - 1, south, jnp.where(odd_a, y, c)),
        )
        for k, result in enumerate(results):
            balanced[k * side + rows[0] : k * side + rows[1], lanes[0] : lanes[1]] = result.astype(BF16)
    corners = told.shape[1]
    message[...] = extra[...]
    message[:, 0:loads] = dot(stiff[0:32, :], balanced[...])[:corners]
    for k in range(told.shape[0]):
        told[k] = message[...]


def step_on(steps, flex, dir_low, low, new_dir_low, flex_base):
    new_dir = steps[0] * dir_low + steps[1] * low
    new_dir_low[...] = new_dir
    flex_base[...] = dot(flex[:, TOP:], new_dir.astype(BF16))


def first_bulk_kernel(steps, after, balanced, stiff, flex, right, *outs):
    right = right[...].T
    res_top, res_low, sol_top, sol_low, squares = outs[:5]
    stiffed = dot(stiff[...], balanced[...])
    direction = right / cheb_center
    low = right[TOP:, :] - stiffed[TOP:]
    res_top[...] = right[:TOP, :] - stiffed[:TOP]
    res_low[...] = low
    sol_top[...] = direction[:TOP]
    sol_low[...] = direction[TOP:]
    squares[...] = jnp.sum(low * low, axis=0, keepdims=True)
    step_on(steps, flex, direction[TOP:], low, *outs[5:])


def bulk_kernel(steps, after, balanced, stiff, flex, res_top, res_low, dir_top, dir_low, sol_top, sol_low, *outs):
    new_res_top, new_res_low, new_sol_top, new_sol_low, squares = outs[:5]
    stiffed = dot(stiff[...], balanced[...])
    low = res_low[...] - stiffed[TOP:]
    new_res_top[...] = res_top[...] - stiffed[:TOP]
    new_res_low[...] = low
    new_sol_top[...] = sol_top[...] + dir_top[...]
    new_sol_low[...] = sol_low[...] + dir_low[...]
    squares[...] = jnp.sum(low * low, axis=0, keepdims=True)
    if steps is not None:
        step_on(steps, flex, dir_low[...], low, *outs[5:])


def split_dot(high, low, values):
    values_high, values_low = split(values[...].reshape(-1, values.shape[2]))
    return dot(high[...], values_high) + (dot(high[...], values_low) + dot(low[...], values_high))


def tree_sum(parts):
    while len(parts) > 1:
        parts = [p + q for p, q in zip(parts[::2], parts[1::2])]
    return parts[0]


def riders(values):
    return tree_sum([values[k, 0:TILE, :] for k in range(values.shape[0])])


def half_product_kernel(high, low, values, total, ride):
    total[...] = split_dot(high, low, values)
    ride[...] = riders(values)


def product_kernel(loads, after, high, low, values, half, ride, total):
    result = (half[...] + split_dot(high, low, values)).reshape(total.shape)
    both = ride[...] + riders(values)
    lane = lax.broadcasted_iota(jnp.int32, both.shape, 1)
    for k in range(total.shape[0]):
        total[k] = result[k]
        total[k, 0:TILE, :] = jnp.where(lane < loads, result[k, 0:TILE, :], both)


def correction_of(terms, squares, res_top, new_res_top, earlier):
    corners = terms.shape[1]
    total = tree_sum([terms[k] for k in range(terms.shape[0])])
    earlier[...] = total[0:TILE, :] * (1.0 / NX)
    new_res_top[...] = res_top[...]
    new_res_top[:corners, :] = res_top[:corners, :] - total[:, : res_top.shape[1]]
    top = new_res_top[...]
    return top, squares[...] + jnp.sum(top * top, axis=0, keepdims=True)


def last_kernel(terms, squares, res_top, new_res_top, earlier, told):
    _, norm = correction_of(terms, squares, res_top, new_res_top, earlier)
    padded = jnp.concatenate([norm, jnp.zeros((1, told.shape[2] - norm.shape[1]), F32)], axis=1)
    told[...] = jnp.broadcast_to(padded[None], told.shape)


def correct_kernel(steps, where, terms, squares, res_top, dir_top, flex, flex_base, *outs):
    new_res_top, earlier, extra, new_dir_top, flexed = outs[:5]
    top, norm = correction_of(terms, squares, res_top, new_res_top, earlier)
    new_dir = steps[0] * dir_top[...] + steps[1] * top
    new_dir_top[...] = new_dir
    flexed[...] = flex_base[...] + dot(flex[:, :TOP], new_dir.astype(BF16))
    send_sides(where, flexed, *outs[5:])
    loads, width = norm.shape[1], extra.shape[1]
    spare = width - loads
    padded = jnp.concatenate([norm, jnp.zeros((1, spare), F32)], axis=1)
    padded = jnp.broadcast_to(padded, (TILE, width))
    line = lax.broadcasted_iota(jnp.int32, padded.shape, 0)
    ride = jnp.zeros_like(padded)
    for n in range(-(-loads // spare)):
        ride = jnp.where(line == n, pltpu.roll(padded, (loads - n * spare) % width, 1), ride)
    extra[...] = jnp.zeros_like(extra)
    extra[0:TILE, :] = ride


def rider_values(earlier, loads):
    spare = earlier.shape[1] - loads
    lines = -(-loads // spare)
    return earlier[:lines, loads:].reshape(-1)[:loads]


def local(right_side, flex, stiff, coarse_inv, corner_map, side_rows):
    right = right_side[0, 0]
    flex_block = flex[0, 0]
    stiff_block = stiff[0, 0]
    order = flex_block.shape[0]
    side = order // SIDES
    loads = right.shape[0]
    width = -(-loads // LANES) * LANES
    corners = corner_map.shape[2]
    rows_held, cols_held = coarse_inv.shape
    half = N_GY * corners
    ids = corner_map[0, 0]
    where = jnp.concatenate([jnp.stack([lax.axis_index(a) for a in ALL]), side_rows[0, 0]])
    where = where.astype(jnp.int32)

    inv_t = coarse_inv.T
    inv_blocks = [inv_t]
    for k in range(1, NY):
        inv_blocks.append(turned(inv_t, "y", NY, k))

    sides = [shape(side + side // 2, LANES)] * SIDES
    ids_line = jnp.pad(ids.astype(F32), (0, LANES - corners))[None]
    from_hbm = [pltpu.with_memory_space_constraint(a, pltpu.HBM) for a in (right, flex_block)]
    flexed, extra, *sends = pl.pallas_call(
        first_kernel,
        grid=(SIDES,),
        out_shape=[shape(order, loads), shape(corners, width)] + sides,
        in_specs=[
            sm(),
            vm(),
            pl.BlockSpec((loads, order), lambda i: (0, 0)),
            pl.BlockSpec((side, order), lambda i: (i, 0)),
        ],
        out_specs=[vm() for _ in range(2 + SIDES)],
        compiler_params=pltpu.CompilerParams(vmem_limit_bytes=VMEM_BYTES),
        name="first",
    )(where, ids_line, *from_hbm)

    own_ids, *sends = lax.optimization_barrier((ids_line, *sends))
    own_ids = jnp.broadcast_to(own_ids[None], (N_GY, 1, LANES))
    own_ids = to_all(own_ids, GY).reshape(N_GY, LANES)
    other_ids = turned(own_ids, "c", NC, 1)
    own_rows, other_rows = call(
        rows_kernel,
        [shape(cols_held, half)] * 2,
        scalars=1,
        scratch=[pltpu.VMEM((2 * half, rows_held), BF16)],
    )(where, own_ids, other_ids, *inv_blocks)
    own_rows = own_rows + turned(other_rows, "c", NC, 1)

    row_parts = [own_rows]
    for k in range(1, NZ):
        row_parts.append(turned(own_rows, "z", NZ, k))

    tops, lows = shape(TOP, loads), shape(order - TOP, loads)
    told_shape = shape(NY * NX, corners, width)
    ride_shape = shape(TILE, width)
    ordering = (own_rows,)
    rho_prev = 1.0 / cheb_sigma
    norms = []
    for iteration in range(ITERS):
        last = iteration + 1 == ITERS
        ins = []
        for k in range(SIDES):
            axes, count = (GY, N_GY) if k < 2 else (GX, N_GX)
            ins.append(swapped(sends[k], axes, count, k % 2))
        balanced, told = call(
            balance_kernel,
            [shape(order, loads, dtype=BF16), told_shape],
            scalars=1,
            scratch=[pltpu.VMEM((corners, width), F32)],
        )(where, flexed, *ins, stiff_block, extra, *ordering)
        ordering = ()
        values = to_all(told, ("y", "x"))
        steps = None
        if not last:
            rho_next = 1.0 / (2.0 * cheb_sigma - rho_prev)
            steps = (rho_next * rho_prev, 2.0 * rho_next / cheb_half)
            rho_prev = rho_next
        if iteration == 0:
            kernel, state = first_bulk_kernel, (right,)
        else:
            kernel, state = bulk_kernel, (res_top, res_low, dir_top, dir_low, sol_top, sol_low)
        outs = call(
            functools.partial(kernel, steps),
            [tops, lows, tops, lows, shape(1, loads)] + ([] if last else [lows, shape(order, loads)]),
        )(values, balanced, stiff_block, flex_block, *state)
        res_top, res_low, sol_top, sol_low, squares = outs[:5]
        values_other = turned(values, "c", NC, 1)
        if iteration == 0:
            dir_top = sol_top
            own_high, own_low, other_high, other_low = call(
                cols_kernel,
                [shape(half, half, dtype=BF16)] * 4,
                scalars=1,
                scratch=[pltpu.VMEM((2 * half, cols_held), BF16)],
            )(where, values, values_other, *row_parts)
        partial, ride = call(half_product_kernel, [shape(half, width), ride_shape])(
            own_high, own_low, values
        )
        (partial,) = call(
            functools.partial(product_kernel, loads), [shape(N_GY, corners, width)]
        )(squares, other_high, other_low, values_other, partial, ride)
        terms = to_all(partial, GY)
        if last:
            res_top, earlier, told = call(
                last_kernel, [tops, ride_shape, shape(N_GX * N_GY, 1, width)]
            )(terms, squares, res_top)
        else:
            dir_low, flex_base = outs[5:]
            res_top, earlier, extra, dir_top, flexed, *sends = call(
                functools.partial(correct_kernel, steps),
                [tops, ride_shape, shape(corners, width), tops, shape(order, loads)] + sides,
                scalars=1,
            )(where, terms, squares, res_top, dir_top, flex_block, flex_base)
        if iteration > 0:
            norms.append(rider_values(earlier, loads))
    norms.append(to_all(told, ALL).sum(axis=0)[0, :loads])
    resid_norm = jnp.sqrt(jnp.stack(norms) / (N_GX * N_GY * order))
    solution = jnp.concatenate([sol_top, sol_low]).T
    residual = jnp.concatenate([res_top, res_low]).T
    return (solution[None, None], residual[None, None], resid_norm)


def solution(mesh):
    torus = Mesh(mesh.devices.reshape(NY, NC, NX, NZ), ALL)
    return jax.shard_map(
        local,
        mesh=torus,
        in_specs=(
            P(GX, GY, None, None),
            P(GX, GY, None, None),
            P(GX, GY, None, None),
            P(GX, GY),
            P(GX, GY, None),
            P(GX, GY, None),
        ),
        out_specs=(P(GX, GY, None, None), P(GX, GY, None, None), P()),
        check_vma=False,
    )
```

profile of v0, /device:TPU:0, one launch (start us, length us, event | category | flops | bytes accessed | tf_op | source)
XLA Modules:
  0.0 193.7 jit_solution(16058125918377692713)
XLA Ops:
  2.4 2.9 %collective-permute-start.6 = (f32[192,384]{1,0:T(8,128)}, f32[192,384]{1,0:T(8,128)S(1)}, u32[]{:S(2)}, u32[]{:S(2)}) collective-permute-start(f32[192,384]{1,0:T(8,128)} %bitcast.44), channel_id=1, source_target_pairs={{0,64},{32,96},{64,0},{96,32},{1,65},{33,97},{65,1},{97,33},{2,66}... | collective-permute-start | bytes 884744 | tf_op jit(solution)/shard_map/ppermute | solution.py:31
  8.0 4.2 %first.1 = (f32[1152,176]{1,0:T(8,128)S(1)}, f32[24,256]{1,0:T(8,128)S(1)}, f32[432,128]{1,0:T(8,128)S(1)}, f32[432,128]{1,0:T(8,128)S(1)}, f32[432,128]{1,0:T(8,128)S(1)}, /*index=5*/f32[432,128]{1,0:T(8,128)S(1)}) custom-call(s32[6]{0:T(128)S(1)} %concatenate.9.where, f32[1,128]{1,0:T(1,128)S(1)} %pad_bitcast_fusion.ids, f32[176,1152]{1,0:T(8,128)} %bitcast.41, ...), custom_call_target="tpu_custom_call" | custom-call | tf_op jit(solution)/shard_map/first/pallas_call | solution.py:332
  12.3 15.3 %all_to_all.40 = f32[16,1,128]{2,1,0:T(1,128)S(1)} all-to-all(f32[16,1,128]{2,1,0:T(1,128)S(1)} %broadcast_in_dim.19), channel_id=1, replica_groups=mesh['y'=4,'c'=2,'x'=4,'z'=4] {'x','z'}, dimensions={0} | all-to-all | bytes 16384 | tf_op jit(solution)/shard_map/all_to_all | solution.py:40
  28.8 2.6 %shard_map.85 = (f32[192,384]{1,0:T(8,128)S(1)}, f32[192,384]{1,0:T(8,128)S(1)}) custom-call(s32[6]{0:T(128)S(1)} %concatenate.9.where, f32[16,128]{1,0:T(8,128)S(1)} %bitcast.48, f32[16,128]{1,0:T(8,128)S(1)} %collective-permute-done.4.ids_other, f32[192,384]{1,0:T(8,128)S(1)} %bitcast.46, f32[192,384]{1,0:T(8,128)S(1)} %collective-permute-done.5.refs_1_, ...), custom_call_target="tpu_custom_call" | custom-call | tf_op jit(solution)/shard_map/pallas_call | solution.py:54
  34.2 5.2 %collective-permute-done.in_a = f32[432,128]{1,0:T(8,128)S(1)} collective-permute-done((f32[432,128]{1,0:T(8,128)S(1)}, f32[432,128]{1,0:T(8,128)S(1)}, u32[]{:S(2)}, u32[]{:S(2)}) %collective-permute-start) | collective-permute-done | bytes 221216 | tf_op jit(solution)/shard_map/ppermute | solution.py:36
  39.3 3.6 %collective-permute-done.1.in_b = f32[432,128]{1,0:T(8,128)S(1)} collective-permute-done((f32[432,128]{1,0:T(8,128)S(1)}, f32[432,128]{1,0:T(8,128)S(1)}, u32[]{:S(2)}, u32[]{:S(2)}) %collective-permute-start.1) | collective-permute-done | bytes 221216 | tf_op jit(solution)/shard_map/ppermute | solution.py:36
  44.1 12.3 %all_to_all.41.after.own.values = f32[16,24,256]{2,1,0:T(8,128)S(1)} all-to-all(f32[16,24,256]{2,1,0:T(8,128)S(1)} %get-tuple-element.84), channel_id=1, replica_groups=mesh['y'=4,'c'=2,'x'=4,'z'=4] {'y','x'}, dimensions={0} | all-to-all | bytes 786432 | tf_op jit(solution)/shard_map/all_to_all | solution.py:40
  56.4 2.4 %collective-permute-start.11 = (f32[192,384]{1,0:T(8,128)S(1)}, f32[192,384]{1,0:T(8,128)S(1)}, u32[]{:S(2)}, u32[]{:S(2)}) collective-permute-start(f32[192,384]{1,0:T(8,128)S(1)} %add.5.refs_0_), channel_id=1, source_target_pairs={{0,2},{1,3},{2,0},{3,1},{4,6},{5,7},{6,4},{7,5},{8,10},{9,11},{10,... | collective-permute-start | bytes 884744 | tf_op jit(solution)/shard_map/ppermute | solution.py:31
  59.7 2.9 %shard_map.87 = (f32[128,176]{1,0:T(8,128)S(1)}, f32[1024,176]{1,0:T(8,128)S(1)}, f32[128,176]{1,0:T(8,128)S(1)}, f32[1024,176]{1,0:T(8,128)S(1)}, f32[1,176]{1,...) custom-call(f32[16,24,256]{2,1,0:T(8,128)S(1)} %all_to_all.41.after.own.values, ...), custom_call_target="tpu_custom_call" | custom-call | tf_op jit(solution)/shard_map/pallas_call | solution.py:54
  62.6 10.8 %collective-permute-done.10.refs_1_ = f32[192,384]{1,0:T(8,128)S(1)} collective-permute-done((f32[192,384]{1,0:T(8,128)S(1)}, f32[192,384]{1,0:T(8,128)S(1)}, u32[]{:S(2)}, u32[]{:S(2)}) %collective-permute-start.10) | collective-permute-done | bytes 294944 | tf_op jit(solution)/shard_map/ppermute | solution.py:31
  74.0 2.6 %shard_map.88 = (bf16[384,384]{1,0:T(8,128)(2,1)S(1)}, bf16[384,384]{1,0:T(8,128)(2,1)S(1)}, bf16[384,384]{1,0:T(8,128)(2,1)S(1)}, bf16[384,384]{1,0:T(8,128)(2,1)S(1)}) custom-call(s32[6]{0:T(128)S(1)} %concatenate.9.where, f32[16,24,256]{2,1,0:T(8,128)S(1)} %all_to_all.41.after.own.values, f32[16,24,256]{2,1,0:T(8,128)S(1)} %collective-permute-done.9.other.values, ...), custom_call_target="tpu_custom_call" | custom-call | tf_op jit(solution)/shard_map/pallas_call | solution.py:54
  77.5 13.5 %all_to_all.42.terms = f32[16,24,256]{2,1,0:T(8,128)S(1)} all-to-all(f32[16,24,256]{2,1,0:T(8,128)S(1)} %shard_map.90), channel_id=1, replica_groups=mesh['y'=4,'c'=2,'x'=4,'z'=4] {'x','z'}, dimensions={0} | all-to-all | bytes 786432 | tf_op jit(solution)/shard_map/all_to_all | solution.py:40
  98.6 3.6 %collective-permute-done.14.in_b = f32[432,128]{1,0:T(8,128)S(1)} collective-permute-done((f32[432,128]{1,0:T(8,128)S(1)}, f32[432,128]{1,0:T(8,128)S(1)}, u32[]{:S(2)}, u32[]{:S(2)}) %collective-permute-start.14) | collective-permute-done | bytes 221216 | tf_op jit(solution)/shard_map/ppermute | solution.py:36
  103.3 13.4 %all_to_all.43.after.values = f32[16,24,256]{2,1,0:T(8,128)S(1)} all-to-all(f32[16,24,256]{2,1,0:T(8,128)S(1)} %get-tuple-element.102), channel_id=1, replica_groups=mesh['y'=4,'c'=2,'x'=4,'z'=4] {'y','x'}, dimensions={0} | all-to-all | bytes 786432 | tf_op jit(solution)/shard_map/all_to_all | solution.py:40
  117.1 2.9 %shard_map.93 = (f32[128,176]{1,0:T(8,128)S(1)}, f32[1024,176]{1,0:T(8,128)S(1)}, f32[128,176]{1,0:T(8,128)S(1)}, f32[1024,176]{1,0:T(8,128)S(1)}, f32[1,176]{1,...) custom-call(f32[16,24,256]{2,1,0:T(8,128)S(1)} %all_to_all.43.after.values, ...), custom_call_target="tpu_custom_call" | custom-call | tf_op jit(solution)/shard_map/pallas_call | solution.py:54
  120.6 14.3 %all_to_all.44.terms = f32[16,24,256]{2,1,0:T(8,128)S(1)} all-to-all(f32[16,24,256]{2,1,0:T(8,128)S(1)} %shard_map.95), channel_id=1, replica_groups=mesh['y'=4,'c'=2,'x'=4,'z'=4] {'x','z'}, dimensions={0} | all-to-all | bytes 786432 | tf_op jit(solution)/shard_map/all_to_all | solution.py:40
  139.8 2.3 %collective-permute-done.18.in_a = f32[432,128]{1,0:T(8,128)S(1)} collective-permute-done((f32[432,128]{1,0:T(8,128)S(1)}, f32[432,128]{1,0:T(8,128)S(1)}, u32[]{:S(2)}, u32[]{:S(2)}) %collective-permute-start.18) | collective-permute-done | bytes 221216 | tf_op jit(solution)/shard_map/ppermute | solution.py:36
  142.1 3.8 %collective-permute-done.19.in_b = f32[432,128]{1,0:T(8,128)S(1)} collective-permute-done((f32[432,128]{1,0:T(8,128)S(1)}, f32[432,128]{1,0:T(8,128)S(1)}, u32[]{:S(2)}, u32[]{:S(2)}) %collective-permute-start.19) | collective-permute-done | bytes 221216 | tf_op jit(solution)/shard_map/ppermute | solution.py:36
  147.0 13.0 %all_to_all.45.after.values = f32[16,24,256]{2,1,0:T(8,128)S(1)} all-to-all(f32[16,24,256]{2,1,0:T(8,128)S(1)} %get-tuple-element.120), channel_id=1, replica_groups=mesh['y'=4,'c'=2,'x'=4,'z'=4] {'y','x'}, dimensions={0} | all-to-all | bytes 786432 | tf_op jit(solution)/shard_map/all_to_all | solution.py:40
  162.9 4.2 %all-to-all-start.6 = ((f32[16,24,256]{2,1,0:T(8,128)}), f32[16,24,256]{2,1,0:T(8,128)S(1)}, u32[]{:S(2)}, u32[]{:S(2)}) async-start(f32[16,24,256]{2,1,0:T(8,128)} %shard_map.100), calls=%async_computation.6 | async-start | bytes 786432 | tf_op jit(solution)/shard_map/all_to_all | solution.py:40
  168.4 2.5 %copy.11 = f32[1,1,176,1152]{3,2,1,0:T(8,128)} copy(f32[1,1,176,1152]{2,3,1,0:T(8,128)} %maximum_bitcast_fusion) | data formatting | bytes 1622016
  170.9 6.5 %all-to-all-done.6.terms = f32[16,24,256]{2,1,0:T(8,128)S(1)} async-done(((f32[16,24,256]{2,1,0:T(8,128)}), f32[16,24,256]{2,1,0:T(8,128)S(1)}, u32[]{:S(2)}, u32[]{:S(2)}) %all-to-all-start.6) | async-done | bytes 393248 | tf_op jit(solution)/shard_map/all_to_all | solution.py:40
  178.1 5.2 %all-to-all-start.7 = ((f32[128,1,256]{2,1,0:T(1,128)}), f32[128,1,256]{2,1,0:T(1,128)S(1)}, u32[]{:S(2)}, u32[]{:S(2)}) async-start(f32[128,1,256]{2,1,0:T(1,128)} %get-tuple-element.138), calls=%async_computation.7 | async-start | bytes 262144 | tf_op jit(solution)/shard_map/all_to_all | solution.py:40
  184.8 8.1 %all-to-all-done.7 = f32[128,1,256]{2,1,0:T(1,128)S(1)} async-done(((f32[128,1,256]{2,1,0:T(1,128)}), f32[128,1,256]{2,1,0:T(1,128)S(1)}, u32[]{:S(2)}, u32[]{:S(2)}) %all-to-all-start.7) | async-done | bytes 131104 | tf_op jit(solution)/shard_map/all_to_all | solution.py:40
  (73 shorter events, 34.7 us)
Async XLA Ops:
  0.6 28.1 %collective-permute-start.5 = (f32[192,384]{1,0:T(8,128)}, f32[192,384]{1,0:T(8,128)S(1)}, u32[]{:S(2)}, u32[]{:S(2)}) collective-permute-start(f32[192,384]{1,0:T(8,128)} %bitcast.43), channel_id=1, source_target_pairs={{0,32},{32,64},{64,96},{96,0},{1,33},{33,65},{65,97},{97,1},{2,34}... | collective-permute-start | bytes 884744 | tf_op jit(solution)/shard_map/ppermute | solution.py:31
  2.4 26.4 %collective-permute-start.6 = (f32[192,384]{1,0:T(8,128)}, f32[192,384]{1,0:T(8,128)S(1)}, u32[]{:S(2)}, u32[]{:S(2)}) collective-permute-start(f32[192,384]{1,0:T(8,128)} %bitcast.44), channel_id=1, source_target_pairs={{0,64},{32,96},{64,0},{96,32},{1,65},{33,97},{65,1},{97,33},{2,66}... | collective-permute-start | bytes 884744 | tf_op jit(solution)/shard_map/ppermute | solution.py:31
  5.3 23.5 %collective-permute-start.7 = (f32[192,384]{1,0:T(8,128)}, f32[192,384]{1,0:T(8,128)S(1)}, u32[]{:S(2)}, u32[]{:S(2)}) collective-permute-start(f32[192,384]{1,0:T(8,128)} %bitcast.45), channel_id=1, source_target_pairs={{0,96},{32,0},{64,32},{96,64},{1,97},{33,1},{65,33},{97,65},{2,98}... | collective-permute-start | bytes 884744 | tf_op jit(solution)/shard_map/ppermute | solution.py:31
  31.4 2.7 %collective-permute-start.8 = (f32[192,384]{1,0:T(8,128)S(1)}, f32[192,384]{1,0:T(8,128)S(1)}, u32[]{:S(2)}, u32[]{:S(2)}) collective-permute-start(f32[192,384]{1,0:T(8,128)S(1)} %get-tuple-element.83), channel_id=1, source_target_pairs={{0,16},{16,0},{1,17},{17,1},{2,18},{18,2},{3,19},{19,3},{4,20},{20... | collective-permute-start | bytes 884744 | tf_op jit(solution)/shard_map/ppermute | solution.py:31
  31.6 7.7 %collective-permute-start = (f32[432,128]{1,0:T(8,128)S(1)}, f32[432,128]{1,0:T(8,128)S(1)}, u32[]{:S(2)}, u32[]{:S(2)}) collective-permute-start(f32[432,128]{1,0:T(8,128)S(1)} %get-tuple-element.76), channel_id=1, source_target_pairs={{0,1},{1,0},{2,3},{3,2},{4,5},{5,4},{6,7},{7,6},{8,9},{9,8},{10,11... | collective-permute-start | bytes 663560 | tf_op jit(solution)/shard_map/ppermute | solution.py:36
  32.2 10.7 %collective-permute-start.1 = (f32[432,128]{1,0:T(8,128)S(1)}, f32[432,128]{1,0:T(8,128)S(1)}, u32[]{:S(2)}, u32[]{:S(2)}) collective-permute-start(f32[432,128]{1,0:T(8,128)S(1)} %get-tuple-element.77), channel_id=1, source_target_pairs={{0,15},{1,2},{2,1},{3,4},{4,3},{5,6},{6,5},{7,8},{8,7},{9,10},{10,... | collective-permute-start | bytes 663560 | tf_op jit(solution)/shard_map/ppermute | solution.py:36
  34.0 8.9 %collective-permute-start.2 = (f32[432,128]{1,0:T(8,128)S(1)}, f32[432,128]{1,0:T(8,128)S(1)}, u32[]{:S(2)}, u32[]{:S(2)}) collective-permute-start(f32[432,128]{1,0:T(8,128)S(1)} %get-tuple-element.78), channel_id=1, source_target_pairs={{0,16},{16,0},{32,48},{48,32},{64,80},{80,64},{96,112},{112,96},{1... | collective-permute-start | bytes 663560 | tf_op jit(solution)/shard_map/ppermute | solution.py:36
  34.0 8.9 %collective-permute-start.3 = (f32[432,128]{1,0:T(8,128)S(1)}, f32[432,128]{1,0:T(8,128)S(1)}, u32[]{:S(2)}, u32[]{:S(2)}) collective-permute-start(f32[432,128]{1,0:T(8,128)S(1)} %get-tuple-element.79), channel_id=1, source_target_pairs={{0,112},{16,32},{32,16},{48,64},{64,48},{80,96},{96,80},{112,0},{1... | collective-permute-start | bytes 663560 | tf_op jit(solution)/shard_map/ppermute | solution.py:36
  56.4 17.6 %collective-permute-start.9 = (f32[16,24,256]{2,1,0:T(8,128)S(1)}, f32[16,24,256]{2,1,0:T(8,128)S(1)}, u32[]{:S(2)}, u32[]{:S(2)}) collective-permute-start(f32[16,24,256]{2,1,0:T(8,128)S(1)} %all_to_all.41.after.own.values), channel_id=1, source_target_pairs={{0,16},{16,0},{1,17},{17,1},{2,18},{18,2},{3,19},{19,3},{4,20},{20... | collective-permute-start | bytes 1179656 | tf_op jit(solution)/shard_map/ppermute | solution.py:31
  56.4 17.0 %collective-permute-start.10 = (f32[192,384]{1,0:T(8,128)S(1)}, f32[192,384]{1,0:T(8,128)S(1)}, u32[]{:S(2)}, u32[]{:S(2)}) collective-permute-start(f32[192,384]{1,0:T(8,128)S(1)} %add.5.refs_0_), channel_id=1, source_target_pairs={{0,1},{1,2},{2,3},{3,0},{4,5},{5,6},{6,7},{7,4},{8,9},{9,10},{10,1... | collective-permute-start | bytes 884744 | tf_op jit(solution)/shard_map/ppermute | solution.py:31
  56.4 17.0 %collective-permute-start.11 = (f32[192,384]{1,0:T(8,128)S(1)}, f32[192,384]{1,0:T(8,128)S(1)}, u32[]{:S(2)}, u32[]{:S(2)}) collective-permute-start(f32[192,384]{1,0:T(8,128)S(1)} %add.5.refs_0_), channel_id=1, source_target_pairs={{0,2},{1,3},{2,0},{3,1},{4,6},{5,7},{6,4},{7,5},{8,10},{9,11},{10,... | collective-permute-start | bytes 884744 | tf_op jit(solution)/shard_map/ppermute | solution.py:31
  58.9 15.1 %collective-permute-start.12 = (f32[192,384]{1,0:T(8,128)S(1)}, f32[192,384]{1,0:T(8,128)S(1)}, u32[]{:S(2)}, u32[]{:S(2)}) collective-permute-start(f32[192,384]{1,0:T(8,128)S(1)} %add.5.refs_0_), channel_id=1, source_target_pairs={{0,3},{1,0},{2,1},{3,2},{4,7},{5,4},{6,5},{7,6},{8,11},{9,8},{10,9... | collective-permute-start | bytes 884744 | tf_op jit(solution)/shard_map/ppermute | solution.py:31
  92.6 5.9 %collective-permute-start.13 = (f32[432,128]{1,0:T(8,128)S(1)}, f32[432,128]{1,0:T(8,128)S(1)}, u32[]{:S(2)}, u32[]{:S(2)}) collective-permute-start(f32[432,128]{1,0:T(8,128)S(1)} %get-tuple-element.97), channel_id=1, source_target_pairs={{0,1},{1,0},{2,3},{3,2},{4,5},{5,4},{6,7},{7,6},{8,9},{9,8},{10,11... | collective-permute-start | bytes 663560 | tf_op jit(solution)/shard_map/ppermute | solution.py:36
  92.9 9.3 %collective-permute-start.14 = (f32[432,128]{1,0:T(8,128)S(1)}, f32[432,128]{1,0:T(8,128)S(1)}, u32[]{:S(2)}, u32[]{:S(2)}) collective-permute-start(f32[432,128]{1,0:T(8,128)S(1)} %get-tuple-element.98), channel_id=1, source_target_pairs={{0,15},{1,2},{2,1},{3,4},{4,3},{5,6},{6,5},{7,8},{8,7},{9,10},{10,... | collective-permute-start | bytes 663560 | tf_op jit(solution)/shard_map/ppermute | solution.py:36
  95.2 7.0 %collective-permute-start.15 = (f32[432,128]{1,0:T(8,128)S(1)}, f32[432,128]{1,0:T(8,128)S(1)}, u32[]{:S(2)}, u32[]{:S(2)}) collective-permute-start(f32[432,128]{1,0:T(8,128)S(1)} %get-tuple-element.99), channel_id=1, source_target_pairs={{0,16},{16,0},{32,48},{48,32},{64,80},{80,64},{96,112},{112,96},{1... | collective-permute-start | bytes 663560 | tf_op jit(solution)/shard_map/ppermute | solution.py:36
  95.2 7.0 %collective-permute-start.16 = (f32[432,128]{1,0:T(8,128)S(1)}, f32[432,128]{1,0:T(8,128)S(1)}, u32[]{:S(2)}, u32[]{:S(2)}) collective-permute-start(f32[432,128]{1,0:T(8,128)S(1)} %get-tuple-element.100), channel_id=1, source_target_pairs={{0,112},{16,32},{32,16},{48,64},{64,48},{80,96},{96,80},{112,0},{1... | collective-permute-start | bytes 663560 | tf_op jit(solution)/shard_map/ppermute | solution.py:36
  116.7 3.4 %collective-permute-start.17 = (f32[16,24,256]{2,1,0:T(8,128)S(1)}, f32[16,24,256]{2,1,0:T(8,128)S(1)}, u32[]{:S(2)}, u32[]{:S(2)}) collective-permute-start(f32[16,24,256]{2,1,0:T(8,128)S(1)} %all_to_all.43.after.values), channel_id=1, source_target_pairs={{0,16},{16,0},{1,17},{17,1},{2,18},{18,2},{3,19},{19,3},{4,20},{20... | collective-permute-start | bytes 1179656 | tf_op jit(solution)/shard_map/ppermute | solution.py:31
  136.0 6.1 %collective-permute-start.18 = (f32[432,128]{1,0:T(8,128)S(1)}, f32[432,128]{1,0:T(8,128)S(1)}, u32[]{:S(2)}, u32[]{:S(2)}) collective-permute-start(f32[432,128]{1,0:T(8,128)S(1)} %get-tuple-element.115), channel_id=1, source_target_pairs={{0,1},{1,0},{2,3},{3,2},{4,5},{5,4},{6,7},{7,6},{8,9},{9,8},{10,11... | collective-permute-start | bytes 663560 | tf_op jit(solution)/shard_map/ppermute | solution.py:36
  136.5 9.4 %collective-permute-start.19 = (f32[432,128]{1,0:T(8,128)S(1)}, f32[432,128]{1,0:T(8,128)S(1)}, u32[]{:S(2)}, u32[]{:S(2)}) collective-permute-start(f32[432,128]{1,0:T(8,128)S(1)} %get-tuple-element.116), channel_id=1, source_target_pairs={{0,15},{1,2},{2,1},{3,4},{4,3},{5,6},{6,5},{7,8},{8,7},{9,10},{10,... | collective-permute-start | bytes 663560 | tf_op jit(solution)/shard_map/ppermute | solution.py:36
  138.6 7.3 %collective-permute-start.20 = (f32[432,128]{1,0:T(8,128)S(1)}, f32[432,128]{1,0:T(8,128)S(1)}, u32[]{:S(2)}, u32[]{:S(2)}) collective-permute-start(f32[432,128]{1,0:T(8,128)S(1)} %get-tuple-element.117), channel_id=1, source_target_pairs={{0,16},{16,0},{32,48},{48,32},{64,80},{80,64},{96,112},{112,96},{1... | collective-permute-start | bytes 663560 | tf_op jit(solution)/shard_map/ppermute | solution.py:36
  138.6 7.3 %collective-permute-start.21 = (f32[432,128]{1,0:T(8,128)S(1)}, f32[432,128]{1,0:T(8,128)S(1)}, u32[]{:S(2)}, u32[]{:S(2)}) collective-permute-start(f32[432,128]{1,0:T(8,128)S(1)} %get-tuple-element.118), channel_id=1, source_target_pairs={{0,112},{16,32},{32,16},{48,64},{64,48},{80,96},{96,80},{112,0},{1... | collective-permute-start | bytes 663560 | tf_op jit(solution)/shard_map/ppermute | solution.py:36
  160.0 1.7 collective-permute-start.22
  162.9 14.5 %all-to-all-start.6 = ((f32[16,24,256]{2,1,0:T(8,128)}), f32[16,24,256]{2,1,0:T(8,128)S(1)}, u32[]{:S(2)}, u32[]{:S(2)}) async-start(f32[16,24,256]{2,1,0:T(8,128)} %shard_map.100), calls=%async_computation.6 | async-start | bytes 786432 | tf_op jit(solution)/shard_map/all_to_all | solution.py:40
  178.1 14.8 %all-to-all-start.7 = ((f32[128,1,256]{2,1,0:T(1,128)}), f32[128,1,256]{2,1,0:T(1,128)S(1)}, u32[]{:S(2)}, u32[]{:S(2)}) async-start(f32[128,1,256]{2,1,0:T(1,128)} %get-tuple-element.138), calls=%async_computation.7 | async-start | bytes 262144 | tf_op jit(solution)/shard_map/all_to_all | solution.py:40
  (5 other events, 90.2 us)
where the time goes:
time: 195 us; the launch traced here: 194 us
  blocking collectives  81.8 us (42%)
  waiting for transfers between devices  48.1 us (25%)
  starting transfers between devices  28.9 us (15%)
  Pallas kernels  26.6 us (14%)
  local copies, waits for them, and re-layouts  4.82 us (2%)
  other arithmetic  2.64 us (1%)
    all_to_all x6, blocking collectives, to_all(): return lax.all_to_all(copies, axes, split_axis=0, concat_axis=0, tiled=True)  81.8 us
    pallas_call x17, Pallas kernels, run(): pl.pallas_call(body, out_shape=outs, in_specs=[sm()] * scalars + [vm()] *...  22.4 us
    ppermute x12, waiting for transfers between devices, swapped(): return lax.ppermute(array, axes, pairs)  20.6 us
    all_to_all x2, waiting for transfers between devices, to_all(): return lax.all_to_all(copies, axes, split_axis=0, concat_axis=0, tiled=True)  14.6 us
    ppermute x11, waiting for transfers between devices, turned(): lax.ppermute(array, axes, [(i, (i + by) % count) for i in range(count)])  12.8 us
    ppermute x12, starting transfers between devices, swapped(): return lax.ppermute(array, axes, pairs)  10.1 us
    ppermute x11, starting transfers between devices, turned(): lax.ppermute(array, axes, [(i, (i + by) % count) for i in range(count)])  9.5 us
    all_to_all x2, starting transfers between devices, to_all(): return lax.all_to_all(copies, axes, split_axis=0, concat_axis=0, tiled=True)  9.34 us
  transfers between devices with their start and end apart: 25, of which 12 were waited for; matrix products, arithmetic and copies ran while one was open for 3% of the time, Pallas kernels for 6%

commit v1 on v0

--- a/solution.py
+++ b/solution.py
@@ -103,21 +103,34 @@
 
 
 def cols_kernel(where, own, other, *refs):
-    blocks, outs, pick = refs[:-5], refs[-5:-1], refs[-1]
+    blocks, outs, sends, pick, total = refs[:NZ], refs[NZ : NZ + 4], refs[NZ + 4 : -2], refs[-2], refs[-1]
     my_x, my_z = where[2], where[3]
     held = blocks[0].shape[0]
     half = outs[0].shape[1]
     last = own.shape[2] - 1
+    corners = own.shape[1]
     columns = [v[n, :, last:] for v in (own, other) for n in range(v.shape[0])]
-    total = 0.0
+    summed = 0.0
     for k, block in enumerate(blocks):
         base = ((my_x * NZ + (my_z + NZ - k) % NZ) * held).astype(F32)
         mark(pick, [ids - base for ids in columns], held)
         for part in split(block[...]):
-            total = total + dot(pick[...], part)
-    total = total.T
+            summed = summed + dot(pick[...], part)
+    total[...] = summed
     for n in range(2):
-        outs[2 * n][...], outs[2 * n + 1][...] = split(total[:, n * half : (n + 1) * half])
+        outs[2 * n][...], outs[2 * n + 1][...] = split(summed[n * half : (n + 1) * half].T)
+    for k, send in enumerate(sends):
+        for n in range(NC * NY):
+            start = pl.multiple_of((n * NX + (my_x + k) % NX) * corners, TILE)
+            send[n * corners : (n + 1) * corners, :] = total[pl.ds(start, corners), :]
+
+
+def block_kernel(*refs):
+    parts, outs = refs[:NX], refs[NX:]
+    block = ((parts[0][...] + parts[1][...]) + (parts[2][...] + parts[3][...])).T
+    half = block.shape[1] // 2
+    for n in range(2):
+        outs[2 * n][...], outs[2 * n + 1][...] = split(block[:, n * half : (n + 1) * half])
 
 
 def pack(out, main, rest, count):
@@ -223,7 +236,7 @@
     step_on(steps, flex, direction[TOP:], low, *outs[5:])
 
 
-def bulk_kernel(steps, after, balanced, stiff, flex, res_top, res_low, dir_top, dir_low, sol_top, sol_low, *outs):
+def bulk_kernel(steps, balanced, stiff, flex, res_top, res_low, dir_top, dir_low, sol_top, sol_low, *outs):
     new_res_top, new_res_low, new_sol_top, new_sol_low, squares = outs[:5]
     stiffed = dot(stiff[...], balanced[...])
     low = res_low[...] - stiffed[TOP:]
@@ -237,7 +250,7 @@
 
 
 def split_dot(high, low, values):
-    values_high, values_low = split(values[...].reshape(-1, values.shape[2]))
+    values_high, values_low = split(values)
     return dot(high[...], values_high) + (dot(high[...], values_low) + dot(low[...], values_high))
 
 
@@ -247,18 +260,34 @@
     return parts[0]
 
 
-def riders(values):
-    return tree_sum([values[k, 0:TILE, :] for k in range(values.shape[0])])
-
-
-def half_product_kernel(high, low, values, total, ride):
-    total[...] = split_dot(high, low, values)
-    ride[...] = riders(values)
-
-
-def product_kernel(loads, after, high, low, values, half, ride, total):
-    result = (half[...] + split_dot(high, low, values)).reshape(total.shape)
-    both = ride[...] + riders(values)
+def first_half_kernel(high, low, values, total):
+    total[...] = split_dot(high, low, values[...].reshape(-1, values.shape[2]))
+
+
+def first_product_kernel(after, high, low, values, half, total):
+    more = split_dot(high, low, values[...].reshape(-1, values.shape[2]))
+    total[...] = (half[...] + more).reshape(total.shape)
+
+
+def gathered(where, blocks, stack):
+    corners = blocks[0].shape[1]
+    for k, block in enumerate(blocks):
+        at = pl.multiple_of(((where[0] + NY - k) % NY) * corners, TILE)
+        stack[pl.ds(at, corners), :] = block[0]
+    b = [block[0, 0:TILE, :] for block in blocks]
+    return (b[0] + b[2]) + (b[1] + b[3])
+
+
+def half_product_kernel(where, high, low, *refs):
+    blocks, total, ride, stack = refs[:NY], refs[NY], refs[NY + 1], refs[NY + 2]
+    ride[...] = gathered(where, blocks, stack)
+    total[...] = split_dot(high, low, stack[...])
+
+
+def product_kernel(loads, where, after, high, low, half, ride, *refs):
+    blocks, total, stack = refs[:NY], refs[NY], refs[NY + 1]
+    both = ride[...] + gathered(where, blocks, stack)
+    result = (half[...] + split_dot(high, low, stack[...])).reshape(total.shape)
     lane = lax.broadcasted_iota(jnp.int32, both.shape, 1)
     for k in range(total.shape[0]):
         total[k] = result[k]
@@ -268,7 +297,7 @@
 def correction_of(terms, squares, res_top, new_res_top, earlier):
     corners = terms.shape[1]
     total = tree_sum([terms[k] for k in range(terms.shape[0])])
-    earlier[...] = total[0:TILE, :] * (1.0 / NX)
+    earlier[...] = total[0:TILE, :]
     new_res_top[...] = res_top[...]
     new_res_top[:corners, :] = res_top[:corners, :] - total[:, : res_top.shape[1]]
     top = new_res_top[...]
@@ -349,10 +378,7 @@
     own_ids = to_all(own_ids, GY).reshape(N_GY, LANES)
     other_ids = turned(own_ids, "c", NC, 1)
     own_rows, other_rows = call(
-        rows_kernel,
-        [shape(cols_held, half)] * 2,
-        scalars=1,
-        scratch=[pltpu.VMEM((2 * half, rows_held), BF16)],
+        rows_kernel, [shape(cols_held, half)] * 2, scalars=1, scratch=[pltpu.VMEM((2 * half, rows_held), BF16)]
     )(where, own_ids, other_ids, *inv_blocks)
     own_rows = own_rows + turned(other_rows, "c", NC, 1)
 
@@ -361,8 +387,8 @@
         row_parts.append(turned(own_rows, "z", NZ, k))
 
     tops, lows = shape(TOP, loads), shape(order - TOP, loads)
-    told_shape = shape(NY * NX, corners, width)
     ride_shape = shape(TILE, width)
+    corner_scratch = [pltpu.VMEM((NY * corners, width), F32)]
     ordering = (own_rows,)
     rho_prev = 1.0 / cheb_sigma
     norms = []
@@ -374,41 +400,60 @@
             ins.append(swapped(sends[k], axes, count, k % 2))
         balanced, told = call(
             balance_kernel,
-            [shape(order, loads, dtype=BF16), told_shape],
+            [shape(order, loads, dtype=BF16), shape(NY * NX if iteration == 0 else 1, corners, width)],
             scalars=1,
             scratch=[pltpu.VMEM((corners, width), F32)],
         )(where, flexed, *ins, stiff_block, extra, *ordering)
         ordering = ()
-        values = to_all(told, ("y", "x"))
         steps = None
         if not last:
             rho_next = 1.0 / (2.0 * cheb_sigma - rho_prev)
             steps = (rho_next * rho_prev, 2.0 * rho_next / cheb_half)
             rho_prev = rho_next
         if iteration == 0:
+            values = to_all(told, ("y", "x"))
             kernel, state = first_bulk_kernel, (right,)
+            order_after = (values,)
         else:
+            values = [told]
+            for k in range(1, NY):
+                values.append(turned(told, "y", NY, k))
             kernel, state = bulk_kernel, (res_top, res_low, dir_top, dir_low, sol_top, sol_low)
+            order_after = ()
         outs = call(
             functools.partial(kernel, steps),
             [tops, lows, tops, lows, shape(1, loads)] + ([] if last else [lows, shape(order, loads)]),
-        )(values, balanced, stiff_block, flex_block, *state)
+        )(*order_after, balanced, stiff_block, flex_block, *state)
         res_top, res_low, sol_top, sol_low, squares = outs[:5]
-        values_other = turned(values, "c", NC, 1)
         if iteration == 0:
             dir_top = sol_top
-            own_high, own_low, other_high, other_low = call(
+            values_other = turned(values, "c", NC, 1)
+            own_high, own_low, other_high, other_low, *shares = call(
                 cols_kernel,
-                [shape(half, half, dtype=BF16)] * 4,
+                [shape(half, half, dtype=BF16)] * 4 + [shape(half // NX * 2, half)] * NX,
                 scalars=1,
-                scratch=[pltpu.VMEM((2 * half, cols_held), BF16)],
+                scratch=[pltpu.VMEM((2 * half, cols_held), BF16), pltpu.VMEM((2 * half, half), F32)],
             )(where, values, values_other, *row_parts)
-        partial, ride = call(half_product_kernel, [shape(half, width), ride_shape])(
-            own_high, own_low, values
-        )
-        (partial,) = call(
-            functools.partial(product_kernel, loads), [shape(N_GY, corners, width)]
-        )(squares, other_high, other_low, values_other, partial, ride)
+            (partial,) = call(first_half_kernel, [shape(half, width)])(own_high, own_low, values)
+            (partial,) = call(first_product_kernel, [shape(N_GY, corners, width)])(
+                squares, other_high, other_low, values_other, partial
+            )
+            for k in range(1, NX):
+                shares[k] = turned(shares[k], "x", NX, k)
+            block = call(block_kernel, [shape(half, NY * corners, dtype=BF16)] * 4)(*shares)
+        else:
+            others = []
+            for k in range(NY):
+                others.append(turned(values[k], "c", NC, 1))
+            partial, ride = call(
+                half_product_kernel, [shape(half, width), ride_shape], scalars=1, scratch=corner_scratch
+            )(where, *block[:2], *values)
+            (partial,) = call(
+                functools.partial(product_kernel, loads),
+                [shape(N_GY, corners, width)],
+                scalars=1,
+                scratch=corner_scratch,
+            )(where, squares, *block[2:], partial, ride, *others)
         terms = to_all(partial, GY)
         if last:
             res_top, earlier, told = call(

time: 195 us -> 199 us (1.021)
  blocking collectives: 81.8 us -> 58.8 us
  waiting for transfers between devices: 48.1 us -> 63.8 us
  starting transfers between devices: 28.9 us -> 38.3 us
    all_to_all x6 -> x4, blocking collectives: 81.8 us -> 58.8 us  [to_all(): return lax.all_to_all(copies, axes, split_axis=0, concat_axis=0, tiled=True)]
    ppermute x11 -> x26, waiting for transfers between devices: 12.8 us -> 23.6 us  [turned(): lax.ppermute(array, axes, [(i, (i + by) % count) for i in range(count)])]
    ppermute x11 -> x26, starting transfers between devices: 9.5 us -> 17.5 us  [turned(): lax.ppermute(array, axes, [(i, (i + by) % count) for i in range(count)])]
    ppermute x12, waiting for transfers between devices: 20.6 us -> 25.2 us  [swapped(): return lax.ppermute(array, axes, pairs)]
    ppermute x12, starting transfers between devices: 10.1 us -> 12.1 us  [swapped(): return lax.ppermute(array, axes, pairs)]
    pallas_call x17 -> x18, Pallas kernels: 22.4 us -> 24.1 us  [run(): pl.pallas_call(body, out_shape=outs, in_specs=[sm()] * scalars + [vm()] *...]
  transfers between devices with their start and end apart: 25 -> 40, of which waited for: 12 -> 17; matrix products, arithmetic and copies ran while one was open for 3% -> 3% of each run, Pallas kernels for 6% -> 7%
where the time goes in v1:
time: 199 us; the launch traced here: 198 us
  waiting for transfers between devices  63.8 us (32%)
  blocking collectives  58.8 us (30%)
  starting transfers between devices  38.3 us (19%)
  Pallas kernels  28.3 us (14%)
  local copies, waits for them, and re-layouts  4.82 us (2%)
  other arithmetic  2.69 us (1%)
    all_to_all x4, blocking collectives, to_all(): return lax.all_to_all(copies, axes, split_axis=0, concat_axis=0, tiled=True)  58.8 us
    ppermute x12, waiting for transfers between devices, swapped(): return lax.ppermute(array, axes, pairs)  25.2 us
    pallas_call x18, Pallas kernels, run(): pl.pallas_call(body, out_shape=outs, in_specs=[sm()] * scalars + [vm()] *...  24.1 us
    ppermute x26, waiting for transfers between devices, turned(): lax.ppermute(array, axes, [(i, (i + by) % count) for i in range(count)])  23.6 us
    ppermute x26, starting transfers between devices, turned(): lax.ppermute(array, axes, [(i, (i + by) % count) for i in range(count)])  17.5 us
    all_to_all x2, waiting for transfers between devices, to_all(): return lax.all_to_all(copies, axes, split_axis=0, concat_axis=0, tiled=True)  15.1 us
    ppermute x12, starting transfers between devices, swapped(): return lax.ppermute(array, axes, pairs)  12.1 us
    all_to_all x2, starting transfers between devices, to_all(): return lax.all_to_all(copies, axes, split_axis=0, concat_axis=0, tiled=True)  8.63 us
  transfers between devices with their start and end apart: 40, of which 17 were waited for; matrix products, arithmetic and copies ran while one was open for 3% of the time, Pallas kernels for 7%

profile of v1, /device:TPU:0, one launch (start us, length us, event | category | flops | bytes accessed | tf_op | source)
XLA Modules:
  0.0 197.7 jit_solution(7511472053309992364)
XLA Ops:
  0.6 3.2 %collective-permute-start.7 = (f32[192,384]{1,0:T(8,128)}, f32[192,384]{1,0:T(8,128)S(1)}, u32[]{:S(2)}, u32[]{:S(2)}) collective-permute-start(f32[192,384]{1,0:T(8,128)} %bitcast.43), channel_id=1, source_target_pairs={{0,96},{32,0},{64,32},{96,64},{1,97},{33,1},{65,33},{97,65},{2,98}... | collective-permute-start | bytes 884744 | tf_op jit(solution)/shard_map/ppermute | solution.py:31
  6.8 4.2 %first.1 = (f32[1152,176]{1,0:T(8,128)S(1)}, f32[24,256]{1,0:T(8,128)S(1)}, f32[432,128]{1,0:T(8,128)S(1)}, f32[432,128]{1,0:T(8,128)S(1)}, f32[432,128]{1,0:T(8,128)S(1)}, /*index=5*/f32[432,128]{1,0:T(8,128)S(1)}) custom-call(s32[6]{0:T(128)S(1)} %concatenate.9.where, f32[1,128]{1,0:T(1,128)S(1)} %pad_bitcast_fusion.ids, f32[176,1152]{1,0:T(8,128)} %bitcast.41, ...), custom_call_target="tpu_custom_call" | custom-call | tf_op jit(solution)/shard_map/first/pallas_call | solution.py:361
  11.1 15.3 %all_to_all.30 = f32[16,1,128]{2,1,0:T(1,128)S(1)} all-to-all(f32[16,1,128]{2,1,0:T(1,128)S(1)} %broadcast_in_dim.19), channel_id=1, replica_groups=mesh['y'=4,'c'=2,'x'=4,'z'=4] {'x','z'}, dimensions={0} | all-to-all | bytes 16384 | tf_op jit(solution)/shard_map/all_to_all | solution.py:40
  27.5 2.6 %shard_map.85 = (f32[192,384]{1,0:T(8,128)S(1)}, f32[192,384]{1,0:T(8,128)S(1)}) custom-call(s32[6]{0:T(128)S(1)} %concatenate.9.where, f32[16,128]{1,0:T(8,128)S(1)} %bitcast.48, f32[16,128]{1,0:T(8,128)S(1)} %collective-permute-done.4.ids_other, f32[192,384]{1,0:T(8,128)S(1)} %bitcast.46, f32[192,384]{1,0:T(8,128)S(1)} %collective-permute-done.5.refs_1_, ...), custom_call_target="tpu_custom_call" | custom-call | tf_op jit(solution)/shard_map/pallas_call | solution.py:54
  35.2 2.9 %collective-permute-done.in_a = f32[432,128]{1,0:T(8,128)S(1)} collective-permute-done((f32[432,128]{1,0:T(8,128)S(1)}, f32[432,128]{1,0:T(8,128)S(1)}, u32[]{:S(2)}, u32[]{:S(2)}) %collective-permute-start) | collective-permute-done | bytes 221216 | tf_op jit(solution)/shard_map/ppermute | solution.py:36
  38.1 3.6 %collective-permute-done.1.in_b = f32[432,128]{1,0:T(8,128)S(1)} collective-permute-done((f32[432,128]{1,0:T(8,128)S(1)}, f32[432,128]{1,0:T(8,128)S(1)}, u32[]{:S(2)}, u32[]{:S(2)}) %collective-permute-start.1) | collective-permute-done | bytes 221216 | tf_op jit(solution)/shard_map/ppermute | solution.py:36
  42.8 13.0 %all_to_all.31.after.own.values = f32[16,24,256]{2,1,0:T(8,128)S(1)} all-to-all(f32[16,24,256]{2,1,0:T(8,128)S(1)} %get-tuple-element.90), channel_id=1, replica_groups=mesh['y'=4,'c'=2,'x'=4,'z'=4] {'y','x'}, dimensions={0} | all-to-all | bytes 786432 | tf_op jit(solution)/shard_map/all_to_all | solution.py:40
  55.9 2.6 %collective-permute-start.12 = (f32[192,384]{1,0:T(8,128)S(1)}, f32[192,384]{1,0:T(8,128)S(1)}, u32[]{:S(2)}, u32[]{:S(2)}) collective-permute-start(f32[192,384]{1,0:T(8,128)S(1)} %add.5.refs_0_), channel_id=1, source_target_pairs={{0,3},{1,0},{2,1},{3,2},{4,7},{5,4},{6,5},{7,6},{8,11},{9,8},{10,9... | collective-permute-start | bytes 884744 | tf_op jit(solution)/shard_map/ppermute | solution.py:31
  59.3 2.9 %shard_map.87 = (f32[128,176]{1,0:T(8,128)S(1)}, f32[1024,176]{1,0:T(8,128)S(1)}, f32[128,176]{1,0:T(8,128)S(1)}, f32[1024,176]{1,0:T(8,128)S(1)}, f32[1,176]{1,...) custom-call(f32[16,24,256]{2,1,0:T(8,128)S(1)} %all_to_all.31.after.own.values, ...), custom_call_target="tpu_custom_call" | custom-call | tf_op jit(solution)/shard_map/pallas_call | solution.py:54
  62.2 9.5 %collective-permute-done.12.refs_3_ = f32[192,384]{1,0:T(8,128)S(1)} collective-permute-done((f32[192,384]{1,0:T(8,128)S(1)}, f32[192,384]{1,0:T(8,128)S(1)}, u32[]{:S(2)}, u32[]{:S(2)}) %collective-permute-start.12) | collective-permute-done | bytes 294944 | tf_op jit(solution)/shard_map/ppermute | solution.py:31
  71.7 3.4 %collective-permute-done.10.refs_1_ = f32[192,384]{1,0:T(8,128)S(1)} collective-permute-done((f32[192,384]{1,0:T(8,128)S(1)}, f32[192,384]{1,0:T(8,128)S(1)}, u32[]{:S(2)}, u32[]{:S(2)}) %collective-permute-start.10) | collective-permute-done | bytes 294944 | tf_op jit(solution)/shard_map/ppermute | solution.py:31
  75.1 2.6 %shard_map.88 = (bf16[384,384]{1,0:T(8,128)(2,1)S(1)}, bf16[384,384]{1,0:T(8,128)(2,1)S(1)}, bf16[384,384]{1,0:T(8,128)(2,1)S(1)}, bf16[384,384]{1,0:T(8,128)(2,...) custom-call(s32[6]{0:T(128)S(1)} %concatenate.9.where, ...), custom_call_target="tpu_custom_call" | custom-call | tf_op jit(solution)/shard_map/pallas_call | solution.py:54
  78.7 12.6 %all_to_all.32.terms = f32[16,24,256]{2,1,0:T(8,128)S(1)} all-to-all(f32[16,24,256]{2,1,0:T(8,128)S(1)} %shard_map.90), channel_id=1, replica_groups=mesh['y'=4,'c'=2,'x'=4,'z'=4] {'x','z'}, dimensions={0} | all-to-all | bytes 786432 | tf_op jit(solution)/shard_map/all_to_all | solution.py:40
  99.3 6.9 %collective-permute-done.14.in_b = f32[432,128]{1,0:T(8,128)S(1)} collective-permute-done((f32[432,128]{1,0:T(8,128)S(1)}, f32[432,128]{1,0:T(8,128)S(1)}, u32[]{:S(2)}, u32[]{:S(2)}) %collective-permute-start.14) | collective-permute-done | bytes 221216 | tf_op jit(solution)/shard_map/ppermute | solution.py:36
  106.3 6.6 %collective-permute-done.16.in_y = f32[432,128]{1,0:T(8,128)S(1)} collective-permute-done((f32[432,128]{1,0:T(8,128)S(1)}, f32[432,128]{1,0:T(8,128)S(1)}, u32[]{:S(2)}, u32[]{:S(2)}) %collective-permute-start.16) | collective-permute-done | bytes 221216 | tf_op jit(solution)/shard_map/ppermute | solution.py:36
  120.8 2.9 %shard_map.93 = (f32[128,176]{1,0:T(8,128)S(1)}, f32[1024,176]{1,0:T(8,128)S(1)}, f32[128,176]{1,0:T(8,128)S(1)}, f32[1024,176]{1,0:T(8,128)S(1)}, f32[1,176]{1,...) custom-call(bf16[1152,176]{1,0:T(8,128)(2,1)S(1)} %get-tuple-element.106.balanced, ...), custom_call_target="tpu_custom_call" | custom-call | tf_op jit(solution)/shard_map/pallas_call | solution.py:54
  125.5 18.0 %all_to_all.33.terms = f32[16,24,256]{2,1,0:T(8,128)S(1)} all-to-all(f32[16,24,256]{2,1,0:T(8,128)S(1)} %shard_map.96), channel_id=1, replica_groups=mesh['y'=4,'c'=2,'x'=4,'z'=4] {'x','z'}, dimensions={0} | all-to-all | bytes 786432 | tf_op jit(solution)/shard_map/all_to_all | solution.py:40
  150.7 3.8 %collective-permute-done.28.in_b = f32[432,128]{1,0:T(8,128)S(1)} collective-permute-done((f32[432,128]{1,0:T(8,128)S(1)}, f32[432,128]{1,0:T(8,128)S(1)}, u32[]{:S(2)}, u32[]{:S(2)}) %collective-permute-start.28) | collective-permute-done | bytes 221216 | tf_op jit(solution)/shard_map/ppermute | solution.py:36
  159.6 3.3 %collective-permute-done.32.refs_2_ = f32[1,24,256]{2,1,0:T(8,128)S(1)} collective-permute-done((f32[1,24,256]{2,1,0:T(8,128)S(1)}, f32[1,24,256]{2,1,0:T(8,128)S(1)}, u32[]{:S(2)}, u32[]{:S(2)}) %collective-permute-start.32) | collective-permute-done | bytes 24608 | tf_op jit(solution)/shard_map/ppermute | solution.py:31
  167.1 3.6 %all-to-all-start.4 = ((f32[16,24,256]{2,1,0:T(8,128)}), f32[16,24,256]{2,1,0:T(8,128)S(1)}, u32[]{:S(2)}, u32[]{:S(2)}) async-start(f32[16,24,256]{2,1,0:T(8,128)} %shard_map.101), calls=%async_computation.4 | async-start | bytes 786432 | tf_op jit(solution)/shard_map/all_to_all | solution.py:40
  172.0 2.5 %copy.11 = f32[1,1,176,1152]{3,2,1,0:T(8,128)} copy(f32[1,1,176,1152]{2,3,1,0:T(8,128)} %maximum_bitcast_fusion) | data formatting | bytes 1622016
  174.5 7.0 %all-to-all-done.4.terms = f32[16,24,256]{2,1,0:T(8,128)S(1)} async-done(((f32[16,24,256]{2,1,0:T(8,128)}), f32[16,24,256]{2,1,0:T(8,128)S(1)}, u32[]{:S(2)}, u32[]{:S(2)}) %all-to-all-start.4) | async-done | bytes 393248 | tf_op jit(solution)/shard_map/all_to_all | solution.py:40
  182.2 5.1 %all-to-all-start.5 = ((f32[128,1,256]{2,1,0:T(1,128)}), f32[128,1,256]{2,1,0:T(1,128)S(1)}, u32[]{:S(2)}, u32[]{:S(2)}) async-start(f32[128,1,256]{2,1,0:T(1,128)} %get-tuple-element.150), calls=%async_computation.5 | async-start | bytes 262144 | tf_op jit(solution)/shard_map/all_to_all | solution.py:40
  188.8 8.1 %all-to-all-done.5 = f32[128,1,256]{2,1,0:T(1,128)S(1)} async-done(((f32[128,1,256]{2,1,0:T(1,128)}), f32[128,1,256]{2,1,0:T(1,128)S(1)}, u32[]{:S(2)}, u32[]{:S(2)}) %all-to-all-start.5) | async-done | bytes 131104 | tf_op jit(solution)/shard_map/all_to_all | solution.py:40
  (102 shorter events, 50.6 us)
Async XLA Ops:
  0.6 26.9 %collective-permute-start.7 = (f32[192,384]{1,0:T(8,128)}, f32[192,384]{1,0:T(8,128)S(1)}, u32[]{:S(2)}, u32[]{:S(2)}) collective-permute-start(f32[192,384]{1,0:T(8,128)} %bitcast.43), channel_id=1, source_target_pairs={{0,96},{32,0},{64,32},{96,64},{1,97},{33,1},{65,33},{97,65},{2,98}... | collective-permute-start | bytes 884744 | tf_op jit(solution)/shard_map/ppermute | solution.py:31
  3.8 23.7 %collective-permute-start.6 = (f32[192,384]{1,0:T(8,128)}, f32[192,384]{1,0:T(8,128)S(1)}, u32[]{:S(2)}, u32[]{:S(2)}) collective-permute-start(f32[192,384]{1,0:T(8,128)} %bitcast.44), channel_id=1, source_target_pairs={{0,64},{32,96},{64,0},{96,32},{1,65},{33,97},{65,1},{97,33},{2,66}... | collective-permute-start | bytes 884744 | tf_op jit(solution)/shard_map/ppermute | solution.py:31
  4.5 23.1 %collective-permute-start.5 = (f32[192,384]{1,0:T(8,128)}, f32[192,384]{1,0:T(8,128)S(1)}, u32[]{:S(2)}, u32[]{:S(2)}) collective-permute-start(f32[192,384]{1,0:T(8,128)} %bitcast.45), channel_id=1, source_target_pairs={{0,32},{32,64},{64,96},{96,0},{1,33},{33,65},{65,97},{97,1},{2,34}... | collective-permute-start | bytes 884744 | tf_op jit(solution)/shard_map/ppermute | solution.py:31
  30.4 7.7 %collective-permute-start = (f32[432,128]{1,0:T(8,128)S(1)}, f32[432,128]{1,0:T(8,128)S(1)}, u32[]{:S(2)}, u32[]{:S(2)}) collective-permute-start(f32[432,128]{1,0:T(8,128)S(1)} %get-tuple-element.82), channel_id=1, source_target_pairs={{0,1},{1,0},{2,3},{3,2},{4,5},{5,4},{6,7},{7,6},{8,9},{9,8},{10,11... | collective-permute-start | bytes 663560 | tf_op jit(solution)/shard_map/ppermute | solution.py:36
  31.0 10.7 %collective-permute-start.1 = (f32[432,128]{1,0:T(8,128)S(1)}, f32[432,128]{1,0:T(8,128)S(1)}, u32[]{:S(2)}, u32[]{:S(2)}) collective-permute-start(f32[432,128]{1,0:T(8,128)S(1)} %get-tuple-element.83), channel_id=1, source_target_pairs={{0,15},{1,2},{2,1},{3,4},{4,3},{5,6},{6,5},{7,8},{8,7},{9,10},{10,... | collective-permute-start | bytes 663560 | tf_op jit(solution)/shard_map/ppermute | solution.py:36
  32.8 8.9 %collective-permute-start.2 = (f32[432,128]{1,0:T(8,128)S(1)}, f32[432,128]{1,0:T(8,128)S(1)}, u32[]{:S(2)}, u32[]{:S(2)}) collective-permute-start(f32[432,128]{1,0:T(8,128)S(1)} %get-tuple-element.84), channel_id=1, source_target_pairs={{0,16},{16,0},{32,48},{48,32},{64,80},{80,64},{96,112},{112,96},{1... | collective-permute-start | bytes 663560 | tf_op jit(solution)/shard_map/ppermute | solution.py:36
  32.8 8.9 %collective-permute-start.3 = (f32[432,128]{1,0:T(8,128)S(1)}, f32[432,128]{1,0:T(8,128)S(1)}, u32[]{:S(2)}, u32[]{:S(2)}) collective-permute-start(f32[432,128]{1,0:T(8,128)S(1)} %get-tuple-element.85), channel_id=1, source_target_pairs={{0,112},{16,32},{32,16},{48,64},{64,48},{80,96},{96,80},{112,0},{1... | collective-permute-start | bytes 663560 | tf_op jit(solution)/shard_map/ppermute | solution.py:36
  55.9 19.2 %collective-permute-start.9 = (f32[16,24,256]{2,1,0:T(8,128)S(1)}, f32[16,24,256]{2,1,0:T(8,128)S(1)}, u32[]{:S(2)}, u32[]{:S(2)}) collective-permute-start(f32[16,24,256]{2,1,0:T(8,128)S(1)} %all_to_all.31.after.own.values), channel_id=1, source_target_pairs={{0,16},{16,0},{1,17},{17,1},{2,18},{18,2},{3,19},{19,3},{4,20},{20... | collective-permute-start | bytes 1179656 | tf_op jit(solution)/shard_map/ppermute | solution.py:31
  55.9 15.9 %collective-permute-start.12 = (f32[192,384]{1,0:T(8,128)S(1)}, f32[192,384]{1,0:T(8,128)S(1)}, u32[]{:S(2)}, u32[]{:S(2)}) collective-permute-start(f32[192,384]{1,0:T(8,128)S(1)} %add.5.refs_0_), channel_id=1, source_target_pairs={{0,3},{1,0},{2,1},{3,2},{4,7},{5,4},{6,5},{7,6},{8,11},{9,8},{10,9... | collective-permute-start | bytes 884744 | tf_op jit(solution)/shard_map/ppermute | solution.py:31
  58.4 13.3 %collective-permute-start.11 = (f32[192,384]{1,0:T(8,128)S(1)}, f32[192,384]{1,0:T(8,128)S(1)}, u32[]{:S(2)}, u32[]{:S(2)}) collective-permute-start(f32[192,384]{1,0:T(8,128)S(1)} %add.5.refs_0_), channel_id=1, source_target_pairs={{0,2},{1,3},{2,0},{3,1},{4,6},{5,7},{6,4},{7,5},{8,10},{9,11},{10,... | collective-permute-start | bytes 884744 | tf_op jit(solution)/shard_map/ppermute | solution.py:31
  58.4 16.7 %collective-permute-start.10 = (f32[192,384]{1,0:T(8,128)S(1)}, f32[192,384]{1,0:T(8,128)S(1)}, u32[]{:S(2)}, u32[]{:S(2)}) collective-permute-start(f32[192,384]{1,0:T(8,128)S(1)} %add.5.refs_0_), channel_id=1, source_target_pairs={{0,1},{1,2},{2,3},{3,0},{4,5},{5,6},{6,7},{7,4},{8,9},{9,10},{10,1... | collective-permute-start | bytes 884744 | tf_op jit(solution)/shard_map/ppermute | solution.py:31
  93.1 13.1 %collective-permute-start.14 = (f32[432,128]{1,0:T(8,128)S(1)}, f32[432,128]{1,0:T(8,128)S(1)}, u32[]{:S(2)}, u32[]{:S(2)}) collective-permute-start(f32[432,128]{1,0:T(8,128)S(1)} %get-tuple-element.102), channel_id=1, source_target_pairs={{0,15},{1,2},{2,1},{3,4},{4,3},{5,6},{6,5},{7,8},{8,7},{9,10},{10,... | collective-permute-start | bytes 663560 | tf_op jit(solution)/shard_map/ppermute | solution.py:36
  95.4 19.4 %collective-permute-start.17 = (f32[192,384]{1,0:T(8,128)S(1)}, f32[192,384]{1,0:T(8,128)S(1)}, u32[]{:S(2)}, u32[]{:S(2)}) collective-permute-start(f32[192,384]{1,0:T(8,128)S(1)} %get-tuple-element.114), channel_id=1, source_target_pairs={{0,4},{4,8},{8,12},{12,0},{1,5},{5,9},{9,13},{13,1},{2,6},{6,10},{... | collective-permute-start | bytes 884744 | tf_op jit(solution)/shard_map/ppermute | solution.py:31
  96.3 19.7 %collective-permute-start.18 = (f32[192,384]{1,0:T(8,128)S(1)}, f32[192,384]{1,0:T(8,128)S(1)}, u32[]{:S(2)}, u32[]{:S(2)}) collective-permute-start(f32[192,384]{1,0:T(8,128)S(1)} %get-tuple-element.115), channel_id=1, source_target_pairs={{0,8},{4,12},{8,0},{12,4},{1,9},{5,13},{9,1},{13,5},{2,10},{6,14},... | collective-permute-start | bytes 884744 | tf_op jit(solution)/shard_map/ppermute | solution.py:31
  97.8 22.7 %collective-permute-start.19 = (f32[192,384]{1,0:T(8,128)S(1)}, f32[192,384]{1,0:T(8,128)S(1)}, u32[]{:S(2)}, u32[]{:S(2)}) collective-permute-start(f32[192,384]{1,0:T(8,128)S(1)} %get-tuple-element.116), channel_id=1, source_target_pairs={{0,12},{4,0},{8,4},{12,8},{1,13},{5,1},{9,5},{13,9},{2,14},{6,2},{... | collective-permute-start | bytes 884744 | tf_op jit(solution)/shard_map/ppermute | solution.py:31
  99.3 6.9 %collective-permute-start.15 = (f32[432,128]{1,0:T(8,128)S(1)}, f32[432,128]{1,0:T(8,128)S(1)}, u32[]{:S(2)}, u32[]{:S(2)}) collective-permute-start(f32[432,128]{1,0:T(8,128)S(1)} %get-tuple-element.103), channel_id=1, source_target_pairs={{0,16},{16,0},{32,48},{48,32},{64,80},{80,64},{96,112},{112,96},{1... | collective-permute-start | bytes 663560 | tf_op jit(solution)/shard_map/ppermute | solution.py:36
  116.0 8.6 %collective-permute-start.23 = (f32[1,24,256]{2,1,0:T(8,128)S(1)}, f32[1,24,256]{2,1,0:T(8,128)S(1)}, u32[]{:S(2)}, u32[]{:S(2)}) collective-permute-start(f32[1,24,256]{2,1,0:T(8,128)S(1)} %get-tuple-element.121.refs_0_), channel_id=1, source_target_pairs={{0,16},{16,0},{1,17},{17,1},{2,18},{18,2},{3,19},{19,3},{4,20},{20... | collective-permute-start | bytes 73736 | tf_op jit(solution)/shard_map/ppermute | solution.py:31
  117.8 6.8 %collective-permute-start.26 = (f32[1,24,256]{2,1,0:T(8,128)S(1)}, f32[1,24,256]{2,1,0:T(8,128)S(1)}, u32[]{:S(2)}, u32[]{:S(2)}) collective-permute-start(f32[1,24,256]{2,1,0:T(8,128)S(1)} %collective-permute-done.22.refs_3_), channel_id=1, source_target_pairs={{0,16},{16,0},{1,17},{17,1},{2,18},{18,2},{3,19},{19,3},{4,20},{20... | collective-permute-start | bytes 73736 | tf_op jit(solution)/shard_map/ppermute | solution.py:31
  145.0 9.4 %collective-permute-start.28 = (f32[432,128]{1,0:T(8,128)S(1)}, f32[432,128]{1,0:T(8,128)S(1)}, u32[]{:S(2)}, u32[]{:S(2)}) collective-permute-start(f32[432,128]{1,0:T(8,128)S(1)} %get-tuple-element.128), channel_id=1, source_target_pairs={{0,15},{1,2},{2,1},{3,4},{4,3},{5,6},{6,5},{7,8},{8,7},{9,10},{10,... | collective-permute-start | bytes 663560 | tf_op jit(solution)/shard_map/ppermute | solution.py:36
  147.2 7.3 %collective-permute-start.29 = (f32[432,128]{1,0:T(8,128)S(1)}, f32[432,128]{1,0:T(8,128)S(1)}, u32[]{:S(2)}, u32[]{:S(2)}) collective-permute-start(f32[432,128]{1,0:T(8,128)S(1)} %get-tuple-element.129), channel_id=1, source_target_pairs={{0,16},{16,0},{32,48},{48,32},{64,80},{80,64},{96,112},{112,96},{1... | collective-permute-start | bytes 663560 | tf_op jit(solution)/shard_map/ppermute | solution.py:36
  147.2 7.3 %collective-permute-start.30 = (f32[432,128]{1,0:T(8,128)S(1)}, f32[432,128]{1,0:T(8,128)S(1)}, u32[]{:S(2)}, u32[]{:S(2)}) collective-permute-start(f32[432,128]{1,0:T(8,128)S(1)} %get-tuple-element.130), channel_id=1, source_target_pairs={{0,112},{16,32},{32,16},{48,64},{64,48},{80,96},{96,80},{112,0},{1... | collective-permute-start | bytes 663560 | tf_op jit(solution)/shard_map/ppermute | solution.py:36
  158.6 6.9 %collective-permute-start.34 = (f32[1,24,256]{2,1,0:T(8,128)S(1)}, f32[1,24,256]{2,1,0:T(8,128)S(1)}, u32[]{:S(2)}, u32[]{:S(2)}) collective-permute-start(f32[1,24,256]{2,1,0:T(8,128)S(1)} %get-tuple-element.142.refs_0_), channel_id=1, source_target_pairs={{0,16},{16,0},{1,17},{17,1},{2,18},{18,2},{3,19},{19,3},{4,20},{20... | collective-permute-start | bytes 73736 | tf_op jit(solution)/shard_map/ppermute | solution.py:31
  167.1 14.3 %all-to-all-start.4 = ((f32[16,24,256]{2,1,0:T(8,128)}), f32[16,24,256]{2,1,0:T(8,128)S(1)}, u32[]{:S(2)}, u32[]{:S(2)}) async-start(f32[16,24,256]{2,1,0:T(8,128)} %shard_map.101), calls=%async_computation.4 | async-start | bytes 786432 | tf_op jit(solution)/shard_map/all_to_all | solution.py:40
  182.2 14.7 %all-to-all-start.5 = ((f32[128,1,256]{2,1,0:T(1,128)}), f32[128,1,256]{2,1,0:T(1,128)S(1)}, u32[]{:S(2)}, u32[]{:S(2)}) async-start(f32[128,1,256]{2,1,0:T(1,128)} %get-tuple-element.150), calls=%async_computation.5 | async-start | bytes 262144 | tf_op jit(solution)/shard_map/all_to_all | solution.py:40
  (20 other events, 165.3 us)

commit v2 on v1

--- a/solution.py
+++ b/solution.py
@@ -48,17 +48,16 @@
     return pl.BlockSpec(memory_space=pltpu.SMEM)
 
 
-def call(body, outs, scalars=0, scratch=()):
+def call(body, outs, scratch=()):
     def run(*operands):
-        held = [pltpu.with_memory_space_constraint(o, pltpu.VMEM) for o in operands[scalars:]]
         return pl.pallas_call(
             body,
             out_shape=outs,
-            in_specs=[sm()] * scalars + [vm()] * len(held),
+            in_specs=[vm() for _ in operands],
             out_specs=[vm() for _ in outs],
             scratch_shapes=scratch,
             compiler_params=pltpu.CompilerParams(vmem_limit_bytes=VMEM_BYTES),
-        )(*operands[:scalars], *held)
+        )(*[pltpu.with_memory_space_constraint(o, pltpu.VMEM) for o in operands])
 
     return run
 
@@ -84,13 +83,16 @@
         pick[n * corners : (n + 2) * corners, :] = jnp.where(at == ids, 1.0, 0.0).astype(BF16)
 
 
-def rows_kernel(where, ids_own, ids_other, *refs):
+def rows_kernel(facts, *refs):
     blocks, own, other, pick = refs[:-3], refs[-3], refs[-2], refs[-1]
-    my_y, my_c = where[0], where[1]
+    my_y, my_c = lax.axis_index("y"), lax.axis_index("c")
     held = blocks[0].shape[1]
     half = own.shape[1]
     corners = half // N_GY
-    lists = [ids[...].T[:corners] for ids in (ids_own, ids_other)]
+    lists = []
+    for core in (my_c, 1 - my_c):
+        start = pl.multiple_of((my_y * NC + core) * N_GY, TILE)
+        lists.append(facts[pl.ds(start, N_GY), :].T[:corners])
     total = 0.0
     for k, block in enumerate(blocks):
         base = ((((my_y + NY - k) % NY) * NC + my_c) * held).astype(F32)
@@ -102,14 +104,18 @@
     other[...] = total[:, half:]
 
 
-def cols_kernel(where, own, other, *refs):
-    blocks, outs, sends, pick, total = refs[:NZ], refs[NZ : NZ + 4], refs[NZ + 4 : -2], refs[-2], refs[-1]
-    my_x, my_z = where[2], where[3]
+def cols_kernel(facts, *refs):
+    blocks, sends, pick, total, lines = refs[:NZ], refs[NZ:-3], refs[-3], refs[-2], refs[-1]
+    my_c, my_x, my_z = (lax.axis_index(a) for a in ("c", "x", "z"))
     held = blocks[0].shape[0]
-    half = outs[0].shape[1]
-    last = own.shape[2] - 1
-    corners = own.shape[1]
-    columns = [v[n, :, last:] for v in (own, other) for n in range(v.shape[0])]
+    corners = sends[0].shape[0] // (NC * NY)
+    columns = []
+    for core in (my_c, 1 - my_c):
+        for n in range(NY * NX):
+            at = (((n // NX) * NC + core) * NX + n % NX) * NZ + my_z
+            lines[n : n + 1, :] = facts[pl.ds(at, 1), :]
+        turned_lines = lines[...].T[:corners]
+        columns += [turned_lines[:, n : n + 1] for n in range(NY * NX)]
     summed = 0.0
     for k, block in enumerate(blocks):
         base = ((my_x * NZ + (my_z + NZ - k) % NZ) * held).astype(F32)
@@ -117,8 +123,6 @@
         for part in split(block[...]):
             summed = summed + dot(pick[...], part)
     total[...] = summed
-    for n in range(2):
-        outs[2 * n][...], outs[2 * n + 1][...] = split(summed[n * half : (n + 1) * half].T)
     for k, send in enumerate(sends):
         for n in range(NC * NY):
             start = pl.multiple_of((n * NX + (my_x + k) % NX) * corners, TILE)
@@ -139,52 +143,57 @@
     out[0:side, :] = main
     out[side : side + half, 0:wide] = rest[:half]
     out[side : side + half, wide : 2 * wide] = rest[half:]
-    out[side : side + half, 2 * wide :] = jnp.full((half, LANES - 2 * wide), count.astype(F32))
-
-
-def first_kernel(where, ids, right, flex, flexed, extra, *sends):
+    out[side : side + half, 2 * wide :] = jnp.broadcast_to(count[:, 2 * wide :], (half, LANES - 2 * wide))
+
+
+def sent_sides():
+    odd_b, odd_a = lax.axis_index("z") % 2, lax.axis_index("c")
+    return (1 - odd_b, odd_b, 3 - odd_a, 2 + odd_a)
+
+
+def first_kernel(side_rows, after, right, flex, flexed, extra, counts, *refs):
+    sends, direction = refs[:-1], refs[-1]
     step = pl.program_id(0)
+    side = flex.shape[0]
 
     @pl.when(step == 0)
     def _():
-        column = jnp.broadcast_to(ids[...], (LANES, LANES)).T
+        direction[...] = (right[...] / cheb_center).astype(BF16).T
         extra[...] = jnp.zeros_like(extra)
-        extra[:, extra.shape[1] - LANES :] = column[: extra.shape[0]]
-
-    side = flex.shape[0]
-    odd_b, odd_a = where[3] % 2, where[1]
-    direction = (right[...] / cheb_center).astype(BF16)
-    part = dot(flex[...], direction, ((1,), (1,)))
+        line = lax.broadcasted_iota(jnp.int32, counts.shape, 0)
+        east, south = side_rows[0].astype(F32), side_rows[1].astype(F32)
+        counts[...] = jnp.where(line == 0, east, south)
+
+    part = dot(flex[...], direction[...])
     flexed[pl.ds(pl.multiple_of(step * side, side), side), :] = part
-    for k, wanted in enumerate((1 - odd_b, odd_b, 3 - odd_a, 2 + odd_a)):
+    for k, wanted in enumerate(sent_sides()):
 
         @pl.when(step == wanted)
         def _():
-            pack(sends[k], part[:, :LANES], part[:, LANES:], where[4 + k // 2])
-
-
-def send_sides(where, flexed, *sends):
+            pack(sends[k], part[:, :LANES], part[:, LANES:], counts[k // 2 : k // 2 + 1, :])
+
+
+def send_sides(counts, flexed, *sends):
     side = flexed.shape[0] // SIDES
-    odd_b, odd_a = where[3] % 2, where[1]
-    for k, wanted in enumerate((1 - odd_b, odd_b, 3 - odd_a, 2 + odd_a)):
+    for k, wanted in enumerate(sent_sides()):
         rows = pl.ds(pl.multiple_of(wanted * side, 32), side)
-        pack(sends[k], flexed[rows, 0:LANES], flexed[rows, LANES:], where[4 + k // 2])
-
-
-def balance_kernel(where, flexed, in_a, in_b, in_c, in_y, stiff, extra, *refs):
-    balanced, told, message = refs[-3:]
+        pack(sends[k], flexed[rows, 0:LANES], flexed[rows, LANES:], counts[k // 2 : k // 2 + 1, :])
+
+
+def balance_kernel(counts, flexed, in_a, in_b, in_c, in_y, stiff, extra, balanced, told):
     side = flexed.shape[0] // SIDES
     loads = flexed.shape[1]
     wide = loads - LANES
     half = side // 2
-    row = where[0] * NC + where[1]
-    col = where[2] * NZ + where[3]
-    odd_b, odd_a = where[3] % 2 == 1, where[1] == 1
+    my_y, my_c, my_x, my_z = (lax.axis_index(a) for a in ALL)
+    row = my_y * NC + my_c
+    col = my_x * NZ + my_z
+    odd_b, odd_a = my_z % 2 == 1, my_c == 1
     spot = (slice(side, side + 1), slice(2 * wide, 2 * wide + 1))
     count_west = jnp.where(odd_b, in_a[spot], in_b[spot])
     count_north = jnp.where(odd_a, in_c[spot], in_y[spot])
-    count_east = jnp.full((1, 1), where[4].astype(F32))
-    count_south = jnp.full((1, 1), where[5].astype(F32))
+    count_east = counts[0:1, 0:1]
+    count_south = counts[1:2, 0:1]
 
     for rows, lanes, there in (
         ((0, side), (0, LANES), ((0, side), (0, LANES))),
@@ -210,10 +219,8 @@
         for k, result in enumerate(results):
             balanced[k * side + rows[0] : k * side + rows[1], lanes[0] : lanes[1]] = result.astype(BF16)
     corners = told.shape[1]
-    message[...] = extra[...]
-    message[:, 0:loads] = dot(stiff[0:32, :], balanced[...])[:corners]
-    for k in range(told.shape[0]):
-        told[k] = message[...]
+    told[0] = extra[...]
+    told[0, :, 0:loads] = dot(stiff[0:32, :], balanced[...])[:corners]
 
 
 def step_on(steps, flex, dir_low, low, new_dir_low, flex_base):
@@ -222,7 +229,7 @@
     flex_base[...] = dot(flex[:, TOP:], new_dir.astype(BF16))
 
 
-def first_bulk_kernel(steps, after, balanced, stiff, flex, right, *outs):
+def first_bulk_kernel(steps, balanced, stiff, flex, right, *outs):
     right = right[...].T
     res_top, res_low, sol_top, sol_low, squares = outs[:5]
     stiffed = dot(stiff[...], balanced[...])
@@ -260,33 +267,25 @@
     return parts[0]
 
 
-def first_half_kernel(high, low, values, total):
-    total[...] = split_dot(high, low, values[...].reshape(-1, values.shape[2]))
-
-
-def first_product_kernel(after, high, low, values, half, total):
-    more = split_dot(high, low, values[...].reshape(-1, values.shape[2]))
-    total[...] = (half[...] + more).reshape(total.shape)
-
-
-def gathered(where, blocks, stack):
+def gathered(blocks, stack):
+    my_y = lax.axis_index("y")
     corners = blocks[0].shape[1]
     for k, block in enumerate(blocks):
-        at = pl.multiple_of(((where[0] + NY - k) % NY) * corners, TILE)
+        at = pl.multiple_of(((my_y + NY - k) % NY) * corners, TILE)
         stack[pl.ds(at, corners), :] = block[0]
     b = [block[0, 0:TILE, :] for block in blocks]
     return (b[0] + b[2]) + (b[1] + b[3])
 
 
-def half_product_kernel(where, high, low, *refs):
+def half_product_kernel(high, low, *refs):
     blocks, total, ride, stack = refs[:NY], refs[NY], refs[NY + 1], refs[NY + 2]
-    ride[...] = gathered(where, blocks, stack)
+    ride[...] = gathered(blocks, stack)
     total[...] = split_dot(high, low, stack[...])
 
 
-def product_kernel(loads, where, after, high, low, half, ride, *refs):
+def product_kernel(loads, after, high, low, half, ride, *refs):
     blocks, total, stack = refs[:NY], refs[NY], refs[NY + 1]
-    both = ride[...] + gathered(where, blocks, stack)
+    both = ride[...] + gathered(blocks, stack)
     result = (half[...] + split_dot(high, low, stack[...])).reshape(total.shape)
     lane = lax.broadcasted_iota(jnp.int32, both.shape, 1)
     for k in range(total.shape[0]):
@@ -310,13 +309,13 @@
     told[...] = jnp.broadcast_to(padded[None], told.shape)
 
 
-def correct_kernel(steps, where, terms, squares, res_top, dir_top, flex, flex_base, *outs):
+def correct_kernel(steps, counts, terms, squares, res_top, dir_top, flex, flex_base, *outs):
     new_res_top, earlier, extra, new_dir_top, flexed = outs[:5]
     top, norm = correction_of(terms, squares, res_top, new_res_top, earlier)
     new_dir = steps[0] * dir_top[...] + steps[1] * top
     new_dir_top[...] = new_dir
     flexed[...] = flex_base[...] + dot(flex[:, :TOP], new_dir.astype(BF16))
-    send_sides(where, flexed, *outs[5:])
+    send_sides(counts, flexed, *outs[5:])
     loads, width = norm.shape[1], extra.shape[1]
     spare = width - loads
     padded = jnp.concatenate([norm, jnp.zeros((1, spare), F32)], axis=1)
@@ -346,50 +345,58 @@
     corners = corner_map.shape[2]
     rows_held, cols_held = coarse_inv.shape
     half = N_GY * corners
-    ids = corner_map[0, 0]
-    where = jnp.concatenate([jnp.stack([lax.axis_index(a) for a in ALL]), side_rows[0, 0]])
-    where = where.astype(jnp.int32)
-
     inv_t = coarse_inv.T
     inv_blocks = [inv_t]
     for k in range(1, NY):
         inv_blocks.append(turned(inv_t, "y", NY, k))
 
+    facts = jnp.pad(corner_map[0, 0].astype(F32), (0, LANES - corners))
+    facts = jnp.broadcast_to(facts[None, None], (N_GX * N_GY, 1, LANES))
+    facts = to_all(facts, ALL).reshape(N_GX * N_GY, LANES)
+
+    own_rows, other_rows = call(
+        rows_kernel, [shape(cols_held, half)] * 2, scratch=[pltpu.VMEM((2 * half, rows_held), BF16)]
+    )(facts, *inv_blocks)
+    own_rows = own_rows + turned(other_rows, "c", NC, 1)
+
+    row_parts = [own_rows]
+    for k in range(1, NZ):
+        row_parts.append(turned(own_rows, "z", NZ, k))
+
     sides = [shape(side + side // 2, LANES)] * SIDES
-    ids_line = jnp.pad(ids.astype(F32), (0, LANES - corners))[None]
     from_hbm = [pltpu.with_memory_space_constraint(a, pltpu.HBM) for a in (right, flex_block)]
-    flexed, extra, *sends = pl.pallas_call(
+    flexed, extra, counts, *sends = pl.pallas_call(
         first_kernel,
         grid=(SIDES,),
-        out_shape=[shape(order, loads), shape(corners, width)] + sides,
+        out_shape=[shape(order, loads), shape(corners, width), shape(TILE, LANES)] + sides,
         in_specs=[
             sm(),
             vm(),
             pl.BlockSpec((loads, order), lambda i: (0, 0)),
             pl.BlockSpec((side, order), lambda i: (i, 0)),
         ],
-        out_specs=[vm() for _ in range(2 + SIDES)],
+        out_specs=[vm() for _ in range(3 + SIDES)],
+        scratch_shapes=[pltpu.VMEM((order, loads), BF16)],
         compiler_params=pltpu.CompilerParams(vmem_limit_bytes=VMEM_BYTES),
         name="first",
-    )(where, ids_line, *from_hbm)
-
-    own_ids, *sends = lax.optimization_barrier((ids_line, *sends))
-    own_ids = jnp.broadcast_to(own_ids[None], (N_GY, 1, LANES))
-    own_ids = to_all(own_ids, GY).reshape(N_GY, LANES)
-    other_ids = turned(own_ids, "c", NC, 1)
-    own_rows, other_rows = call(
-        rows_kernel, [shape(cols_held, half)] * 2, scalars=1, scratch=[pltpu.VMEM((2 * half, rows_held), BF16)]
-    )(where, own_ids, other_ids, *inv_blocks)
-    own_rows = own_rows + turned(other_rows, "c", NC, 1)
-
-    row_parts = [own_rows]
-    for k in range(1, NZ):
-        row_parts.append(turned(own_rows, "z", NZ, k))
+    )(side_rows[0, 0], pltpu.with_memory_space_constraint(facts, pltpu.VMEM), *from_hbm)
+
+    shares = list(call(
+        cols_kernel,
+        [shape(half // NX * 2, half)] * NX,
+        scratch=[
+            pltpu.VMEM((2 * half, cols_held), BF16),
+            pltpu.VMEM((2 * half, half), F32),
+            pltpu.VMEM((NY * NX, LANES), F32),
+        ],
+    )(facts, *row_parts))
+    for k in range(1, NX):
+        shares[k] = turned(shares[k], "x", NX, k)
+    block = call(block_kernel, [shape(half, NY * corners, dtype=BF16)] * 4)(*shares)
 
     tops, lows = shape(TOP, loads), shape(order - TOP, loads)
     ride_shape = shape(TILE, width)
     corner_scratch = [pltpu.VMEM((NY * corners, width), F32)]
-    ordering = (own_rows,)
     rho_prev = 1.0 / cheb_sigma
     norms = []
     for iteration in range(ITERS):
@@ -399,61 +406,38 @@
             axes, count = (GY, N_GY) if k < 2 else (GX, N_GX)
             ins.append(swapped(sends[k], axes, count, k % 2))
         balanced, told = call(
-            balance_kernel,
-            [shape(order, loads, dtype=BF16), shape(NY * NX if iteration == 0 else 1, corners, width)],
-            scalars=1,
-            scratch=[pltpu.VMEM((corners, width), F32)],
-        )(where, flexed, *ins, stiff_block, extra, *ordering)
-        ordering = ()
+            balance_kernel, [shape(order, loads, dtype=BF16), shape(1, corners, width)]
+        )(counts, flexed, *ins, stiff_block, extra)
+        values = [told]
+        for k in range(1, NY):
+            values.append(turned(told, "y", NY, k))
         steps = None
         if not last:
             rho_next = 1.0 / (2.0 * cheb_sigma - rho_prev)
             steps = (rho_next * rho_prev, 2.0 * rho_next / cheb_half)
             rho_prev = rho_next
         if iteration == 0:
-            values = to_all(told, ("y", "x"))
             kernel, state = first_bulk_kernel, (right,)
-            order_after = (values,)
         else:
-            values = [told]
-            for k in range(1, NY):
-                values.append(turned(told, "y", NY, k))
             kernel, state = bulk_kernel, (res_top, res_low, dir_top, dir_low, sol_top, sol_low)
-            order_after = ()
         outs = call(
             functools.partial(kernel, steps),
             [tops, lows, tops, lows, shape(1, loads)] + ([] if last else [lows, shape(order, loads)]),
-        )(*order_after, balanced, stiff_block, flex_block, *state)
+        )(balanced, stiff_block, flex_block, *state)
         res_top, res_low, sol_top, sol_low, squares = outs[:5]
         if iteration == 0:
             dir_top = sol_top
-            values_other = turned(values, "c", NC, 1)
-            own_high, own_low, other_high, other_low, *shares = call(
-                cols_kernel,
-                [shape(half, half, dtype=BF16)] * 4 + [shape(half // NX * 2, half)] * NX,
-                scalars=1,
-                scratch=[pltpu.VMEM((2 * half, cols_held), BF16), pltpu.VMEM((2 * half, half), F32)],
-            )(where, values, values_other, *row_parts)
-            (partial,) = call(first_half_kernel, [shape(half, width)])(own_high, own_low, values)
-            (partial,) = call(first_product_kernel, [shape(N_GY, corners, width)])(
-                squares, other_high, other_low, values_other, partial
-            )
-            for k in range(1, NX):
-                shares[k] = turned(shares[k], "x", NX, k)
-            block = call(block_kernel, [shape(half, NY * corners, dtype=BF16)] * 4)(*shares)
-        else:
-            others = []
-            for k in range(NY):
-                others.append(turned(values[k], "c", NC, 1))
-            partial, ride = call(
-                half_product_kernel, [shape(half, width), ride_shape], scalars=1, scratch=corner_scratch
-            )(where, *block[:2], *values)
-            (partial,) = call(
-                functools.partial(product_kernel, loads),
-                [shape(N_GY, corners, width)],
-                scalars=1,
-                scratch=corner_scratch,
-            )(where, squares, *block[2:], partial, ride, *others)
+        others = []
+        for k in range(NY):
+            others.append(turned(values[k], "c", NC, 1))
+        partial, ride = call(
+            half_product_kernel, [shape(half, width), ride_shape], scratch=corner_scratch
+        )(*block[:2], *values)
+        (partial,) = call(
+            functools.partial(product_kernel, loads),
+            [shape(N_GY, corners, width)],
+            scratch=corner_scratch,
+        )(squares, *block[2:], partial, ride, *others)
         terms = to_all(partial, GY)
         if last:
             res_top, earlier, told = call(
@@ -464,8 +448,7 @@
             res_top, earlier, extra, dir_top, flexed, *sends = call(
                 functools.partial(correct_kernel, steps),
                 [tops, ride_shape, shape(corners, width), tops, shape(order, loads)] + sides,
-                scalars=1,
-            )(where, terms, squares, res_top, dir_top, flex_block, flex_base)
+            )(counts, terms, squares, res_top, dir_top, flex_block, flex_base)
         if iteration > 0:
             norms.append(rider_values(earlier, loads))
     norms.append(to_all(told, ALL).sum(axis=0)[0, :loads])

time: 199 us -> 181 us (0.910)
  blocking collectives: 58.8 us -> 47.5 us
  waiting for transfers between devices: 63.8 us -> 54.1 us
  starting transfers between devices: 38.3 us -> 47.6 us
  Pallas kernels: 28.3 us -> 22.7 us
    all_to_all x4 -> x3, blocking collectives: 58.8 us -> 47.5 us  [to_all(): return lax.all_to_all(copies, axes, split_axis=0, concat_axis=0, tiled=True)]
    ppermute x12, waiting for transfers between devices: 25.2 us -> 14.1 us  [swapped(): return lax.ppermute(array, axes, pairs)]
    ppermute x26 -> x31, starting transfers between devices: 17.5 us -> 24.3 us  [turned(): lax.ppermute(array, axes, [(i, (i + by) % count) for i in range(count)])]
    pallas_call x18, Pallas kernels: 24.1 us -> 18.4 us  [run(): pl.pallas_call(body, out_shape=outs, in_specs=[vm() for _ in operands], o...]
    ppermute x12, starting transfers between devices: 12.1 us -> 14.2 us  [swapped(): return lax.ppermute(array, axes, pairs)]
    ppermute x26 -> x31, waiting for transfers between devices: 23.6 us -> 24.9 us  [turned(): lax.ppermute(array, axes, [(i, (i + by) % count) for i in range(count)])]
    unnamed x10 -> x12, local copies, waits for them, and re-layouts: 3.76 us -> 4.71 us
  transfers between devices with their start and end apart: 40 -> 45, of which waited for: 17 -> 18; matrix products, arithmetic and copies ran while one was open for 3% -> 3% of each run, Pallas kernels for 7% -> 9%
where the time goes in v2:
time: 181 us; the launch traced here: 180 us
  waiting for transfers between devices  54.1 us (30%)
  starting transfers between devices  47.6 us (26%)
  blocking collectives  47.5 us (26%)
  Pallas kernels  22.7 us (13%)
  local copies, waits for them, and re-layouts  5.07 us (3%)
  other arithmetic  2.67 us (1%)
    all_to_all x3, blocking collectives, to_all(): return lax.all_to_all(copies, axes, split_axis=0, concat_axis=0, tiled=True)  47.5 us
    ppermute x31, waiting for transfers between devices, turned(): lax.ppermute(array, axes, [(i, (i + by) % count) for i in range(count)])  24.9 us
    ppermute x31, starting transfers between devices, turned(): lax.ppermute(array, axes, [(i, (i + by) % count) for i in range(count)])  24.3 us
    pallas_call x18, Pallas kernels, run(): pl.pallas_call(body, out_shape=outs, in_specs=[vm() for _ in operands], o...  18.4 us
    all_to_all x2, waiting for transfers between devices, to_all(): return lax.all_to_all(copies, axes, split_axis=0, concat_axis=0, tiled=True)  15.1 us
    ppermute x12, starting transfers between devices, swapped(): return lax.ppermute(array, axes, pairs)  14.2 us
    ppermute x12, waiting for transfers between devices, swapped(): return lax.ppermute(array, axes, pairs)  14.1 us
    all_to_all x2, starting transfers between devices, to_all(): return lax.all_to_all(copies, axes, split_axis=0, concat_axis=0, tiled=True)  9.06 us
  transfers between devices with their start and end apart: 45, of which 18 were waited for; matrix products, arithmetic and copies ran while one was open for 3% of the time, Pallas kernels for 9%

profile of v2, /device:TPU:0, one launch (start us, length us, event | category | flops | bytes accessed | tf_op | source)
XLA Modules:
  0.0 180.5 jit_solution(4886033905558056908)
XLA Ops:
  2.4 2.9 %collective-permute-start.5 = (f32[192,384]{1,0:T(8,128)}, f32[192,384]{1,0:T(8,128)S(1)}, u32[]{:S(2)}, u32[]{:S(2)}) collective-permute-start(f32[192,384]{1,0:T(8,128)} %bitcast.40), channel_id=1, source_target_pairs={{0,64},{32,96},{64,0},{96,32},{1,65},{33,97},{65,1},{97,33},{2,66}... | collective-permute-start | bytes 884744 | tf_op jit(solution)/shard_map/ppermute | solution.py:31
  7.4 17.9 %all_to_all.25 = f32[128,1,128]{2,1,0:T(1,128)S(1)} all-to-all(f32[128,1,128]{2,1,0:T(1,128)S(1)} %broadcast_in_dim.12), channel_id=1, replica_groups=mesh['y'=4,'c'=2,'x'=4,'z'=4] {'y','c','x','z'}, dimensions={0} | all-to-all | bytes 131072 | tf_op jit(solution)/shard_map/all_to_all | solution.py:40
  33.6 4.3 %first.1 = (f32[1152,176]{1,0:T(8,128)S(1)}, f32[24,256]{1,0:T(8,128)S(1)}, f32[8,128]{1,0:T(8,128)S(1)}, f32[432,128]{1,0:T(8,128)S(1)}, f32[432,128]{1,0:T(8,1...) custom-call(s32[2]{0:T(128)S(1)} %bitcast.43, f32[128,128]{1,0:T(8,128)S(1)} %bitcast.37, f32[176,1152]{1,0:T(8,128)} %bitcast.34, ...), custom_call_target="tpu_custom_call" | custom-call | tf_op jit(solution)/shard_map/first/pallas_call | solution.py:368
  38.6 2.7 %collective-permute-start.1 = (f32[432,128]{1,0:T(8,128)S(1)}, f32[432,128]{1,0:T(8,128)S(1)}, u32[]{:S(2)}, u32[]{:S(2)}) collective-permute-start(f32[432,128]{1,0:T(8,128)S(1)} %get-tuple-element.74), channel_id=1, source_target_pairs={{0,15},{1,2},{2,1},{3,4},{4,3},{5,6},{6,5},{7,8},{8,7},{9,10},{10,... | collective-permute-start | bytes 663560 | tf_op jit(solution)/shard_map/ppermute | solution.py:36
  41.3 10.1 %collective-permute-done.8.refs_1_ = f32[192,384]{1,0:T(8,128)S(1)} collective-permute-done((f32[192,384]{1,0:T(8,128)S(1)}, f32[192,384]{1,0:T(8,128)S(1)}, u32[]{:S(2)}, u32[]{:S(2)}) %collective-permute-start.8) | collective-permute-done | bytes 294944 | tf_op jit(solution)/shard_map/ppermute | solution.py:31
  51.3 2.2 %shard_map.88 = (f32[192,384]{1,0:T(8,128)S(1)}, f32[192,384]{1,0:T(8,128)S(1)}, f32[192,384]{1,0:T(8,128)S(1)}, f32[192,384]{1,0:T(8,128)S(1)}) custom-call(f32[128,128]{1,0:T(8,128)S(1)} %bitcast.38, f32[192,384]{1,0:T(8,128)S(1)} %add.5.refs_0_, f32[192,384]{1,0:T(8,128)S(1)} %collective-permute-done.8.refs_1_, ...), custom_call_target="tpu_custom_call" | custom-call | tf_op jit(solution)/shard_map/pallas_call | solution.py:53
  59.1 3.2 %collective-permute-done.3.in_y = f32[432,128]{1,0:T(8,128)S(1)} collective-permute-done((f32[432,128]{1,0:T(8,128)S(1)}, f32[432,128]{1,0:T(8,128)S(1)}, u32[]{:S(2)}, u32[]{:S(2)}) %collective-permute-start.3) | collective-permute-done | bytes 221216 | tf_op jit(solution)/shard_map/ppermute | solution.py:36
  65.0 3.0 %collective-permute-done.14.refs_1_ = f32[1,24,256]{2,1,0:T(8,128)S(1)} collective-permute-done((f32[1,24,256]{2,1,0:T(8,128)S(1)}, f32[1,24,256]{2,1,0:T(8,128)S(1)}, u32[]{:S(2)}, u32[]{:S(2)}) %collective-permute-start.14) | collective-permute-done | bytes 24608 | tf_op jit(solution)/shard_map/ppermute | solution.py:31
  68.6 3.2 %collective-permute-done.16.refs_3_ = f32[1,24,256]{2,1,0:T(8,128)S(1)} collective-permute-done((f32[1,24,256]{2,1,0:T(8,128)S(1)}, f32[1,24,256]{2,1,0:T(8,128)S(1)}, u32[]{:S(2)}, u32[]{:S(2)}) %collective-permute-start.16) | collective-permute-done | bytes 24608 | tf_op jit(solution)/shard_map/ppermute | solution.py:31
  72.6 2.9 %shard_map.86 = (f32[128,176]{1,0:T(8,128)S(1)}, f32[1024,176]{1,0:T(8,128)S(1)}, f32[128,176]{1,0:T(8,128)S(1)}, f32[1024,176]{1,0:T(8,128)S(1)}, f32[1,176]{1,...) custom-call(bf16[1152,176]{1,0:T(8,128)(2,1)S(1)} %get-tuple-element.78.balanced, ...), custom_call_target="tpu_custom_call" | custom-call | tf_op jit(solution)/shard_map/pallas_call | solution.py:53
  76.6 16.1 %all_to_all.26.terms = f32[16,24,256]{2,1,0:T(8,128)S(1)} all-to-all(f32[16,24,256]{2,1,0:T(8,128)S(1)} %shard_map.91), channel_id=1, replica_groups=mesh['y'=4,'c'=2,'x'=4,'z'=4] {'x','z'}, dimensions={0} | all-to-all | bytes 786432 | tf_op jit(solution)/shard_map/all_to_all | solution.py:40
  94.1 2.2 %collective-permute-start.22 = (f32[432,128]{1,0:T(8,128)S(1)}, f32[432,128]{1,0:T(8,128)S(1)}, u32[]{:S(2)}, u32[]{:S(2)}) collective-permute-start(f32[432,128]{1,0:T(8,128)S(1)} %get-tuple-element.98), channel_id=1, source_target_pairs={{0,15},{1,2},{2,1},{3,4},{4,3},{5,6},{6,5},{7,8},{8,7},{9,10},{10,... | collective-permute-start | bytes 663560 | tf_op jit(solution)/shard_map/ppermute | solution.py:36
  97.6 2.5 %collective-permute-done.21.in_a = f32[432,128]{1,0:T(8,128)S(1)} collective-permute-done((f32[432,128]{1,0:T(8,128)S(1)}, f32[432,128]{1,0:T(8,128)S(1)}, u32[]{:S(2)}, u32[]{:S(2)}) %collective-permute-start.21) | collective-permute-done | bytes 221216 | tf_op jit(solution)/shard_map/ppermute | solution.py:36
  100.1 3.6 %collective-permute-done.22.in_b = f32[432,128]{1,0:T(8,128)S(1)} collective-permute-done((f32[432,128]{1,0:T(8,128)S(1)}, f32[432,128]{1,0:T(8,128)S(1)}, u32[]{:S(2)}, u32[]{:S(2)}) %collective-permute-start.22) | collective-permute-done | bytes 221216 | tf_op jit(solution)/shard_map/ppermute | solution.py:36
  104.4 2.7 %collective-permute-start.26 = (f32[1,24,256]{2,1,0:T(8,128)S(1)}, f32[1,24,256]{2,1,0:T(8,128)S(1)}, u32[]{:S(2)}, u32[]{:S(2)}) collective-permute-start(f32[1,24,256]{2,1,0:T(8,128)S(1)} %get-tuple-element.109.refs_0_), channel_id=1, source_target_pairs={{0,64},{32,96},{64,0},{96,32},{1,65},{33,97},{65,1},{97,33},{2,66}... | collective-permute-start | bytes 73736 | tf_op jit(solution)/shard_map/ppermute | solution.py:31
  110.9 3.0 %shard_map.94 = (f32[128,176]{1,0:T(8,128)S(1)}, f32[1024,176]{1,0:T(8,128)S(1)}, f32[128,176]{1,0:T(8,128)S(1)}, f32[1024,176]{1,0:T(8,128)S(1)}, f32[1,176]{1,...) custom-call(bf16[1152,176]{1,0:T(8,128)(2,1)S(1)} %get-tuple-element.102.balanced, ...), custom_call_target="tpu_custom_call" | custom-call | tf_op jit(solution)/shard_map/pallas_call | solution.py:53
  114.6 13.6 %all_to_all.27.terms = f32[16,24,256]{2,1,0:T(8,128)S(1)} all-to-all(f32[16,24,256]{2,1,0:T(8,128)S(1)} %shard_map.96), channel_id=1, replica_groups=mesh['y'=4,'c'=2,'x'=4,'z'=4] {'x','z'}, dimensions={0} | all-to-all | bytes 786432 | tf_op jit(solution)/shard_map/all_to_all | solution.py:40
  131.4 2.5 %collective-permute-start.35 = (f32[432,128]{1,0:T(8,128)S(1)}, f32[432,128]{1,0:T(8,128)S(1)}, u32[]{:S(2)}, u32[]{:S(2)}) collective-permute-start(f32[432,128]{1,0:T(8,128)S(1)} %get-tuple-element.118), channel_id=1, source_target_pairs={{0,112},{16,32},{32,16},{48,64},{64,48},{80,96},{96,80},{112,0},{1... | collective-permute-start | bytes 663560 | tf_op jit(solution)/shard_map/ppermute | solution.py:36
  134.9 3.8 %collective-permute-done.33.in_b = f32[432,128]{1,0:T(8,128)S(1)} collective-permute-done((f32[432,128]{1,0:T(8,128)S(1)}, f32[432,128]{1,0:T(8,128)S(1)}, u32[]{:S(2)}, u32[]{:S(2)}) %collective-permute-start.33) | collective-permute-done | bytes 221216 | tf_op jit(solution)/shard_map/ppermute | solution.py:36
  149.5 3.6 %all-to-all-start.3 = ((f32[16,24,256]{2,1,0:T(8,128)}), f32[16,24,256]{2,1,0:T(8,128)S(1)}, u32[]{:S(2)}, u32[]{:S(2)}) async-start(f32[16,24,256]{2,1,0:T(8,128)} %shard_map.101), calls=%async_computation.3 | async-start | bytes 786432 | tf_op jit(solution)/shard_map/all_to_all | solution.py:40
  154.4 2.5 %copy.11 = f32[1,1,176,1152]{3,2,1,0:T(8,128)} copy(f32[1,1,176,1152]{2,3,1,0:T(8,128)} %maximum_bitcast_fusion) | data formatting | bytes 1622016
  156.9 7.0 %all-to-all-done.3.terms = f32[16,24,256]{2,1,0:T(8,128)S(1)} async-done(((f32[16,24,256]{2,1,0:T(8,128)}), f32[16,24,256]{2,1,0:T(8,128)S(1)}, u32[]{:S(2)}, u32[]{:S(2)}) %all-to-all-start.3) | async-done | bytes 393248 | tf_op jit(solution)/shard_map/all_to_all | solution.py:40
  164.6 5.5 %all-to-all-start.4 = ((f32[128,1,256]{2,1,0:T(1,128)}), f32[128,1,256]{2,1,0:T(1,128)S(1)}, u32[]{:S(2)}, u32[]{:S(2)}) async-start(f32[128,1,256]{2,1,0:T(1,128)} %get-tuple-element.138), calls=%async_computation.4 | async-start | bytes 262144 | tf_op jit(solution)/shard_map/all_to_all | solution.py:40
  171.6 8.1 %all-to-all-done.4 = f32[128,1,256]{2,1,0:T(1,128)S(1)} async-done(((f32[128,1,256]{2,1,0:T(1,128)}), f32[128,1,256]{2,1,0:T(1,128)S(1)}, u32[]{:S(2)}, u32[]{:S(2)}) %all-to-all-start.4) | async-done | bytes 131104 | tf_op jit(solution)/shard_map/all_to_all | solution.py:40
  (112 shorter events, 50.5 us)
Async XLA Ops:
  0.6 24.6 %collective-permute-start.4 = (f32[192,384]{1,0:T(8,128)}, f32[192,384]{1,0:T(8,128)S(1)}, u32[]{:S(2)}, u32[]{:S(2)}) collective-permute-start(f32[192,384]{1,0:T(8,128)} %bitcast.39), channel_id=1, source_target_pairs={{0,32},{32,64},{64,96},{96,0},{1,33},{33,65},{65,97},{97,1},{2,34}... | collective-permute-start | bytes 884744 | tf_op jit(solution)/shard_map/ppermute | solution.py:31
  2.4 22.8 %collective-permute-start.5 = (f32[192,384]{1,0:T(8,128)}, f32[192,384]{1,0:T(8,128)S(1)}, u32[]{:S(2)}, u32[]{:S(2)}) collective-permute-start(f32[192,384]{1,0:T(8,128)} %bitcast.40), channel_id=1, source_target_pairs={{0,64},{32,96},{64,0},{96,32},{1,65},{33,97},{65,1},{97,33},{2,66}... | collective-permute-start | bytes 884744 | tf_op jit(solution)/shard_map/ppermute | solution.py:31
  5.3 19.9 %collective-permute-start.6 = (f32[192,384]{1,0:T(8,128)}, f32[192,384]{1,0:T(8,128)S(1)}, u32[]{:S(2)}, u32[]{:S(2)}) collective-permute-start(f32[192,384]{1,0:T(8,128)} %bitcast.41), channel_id=1, source_target_pairs={{0,96},{32,0},{64,32},{96,64},{1,97},{33,1},{65,33},{97,65},{2,98}... | collective-permute-start | bytes 884744 | tf_op jit(solution)/shard_map/ppermute | solution.py:31
  29.9 21.4 %collective-permute-start.8 = (f32[192,384]{1,0:T(8,128)S(1)}, f32[192,384]{1,0:T(8,128)S(1)}, u32[]{:S(2)}, u32[]{:S(2)}) collective-permute-start(f32[192,384]{1,0:T(8,128)S(1)} %add.5.refs_0_), channel_id=1, source_target_pairs={{0,1},{1,2},{2,3},{3,0},{4,5},{5,6},{6,7},{7,4},{8,9},{9,10},{10,1... | collective-permute-start | bytes 884744 | tf_op jit(solution)/shard_map/ppermute | solution.py:31
  30.9 20.5 %collective-permute-start.9 = (f32[192,384]{1,0:T(8,128)S(1)}, f32[192,384]{1,0:T(8,128)S(1)}, u32[]{:S(2)}, u32[]{:S(2)}) collective-permute-start(f32[192,384]{1,0:T(8,128)S(1)} %add.5.refs_0_), channel_id=1, source_target_pairs={{0,2},{1,3},{2,0},{3,1},{4,6},{5,7},{6,4},{7,5},{8,10},{9,11},{10,... | collective-permute-start | bytes 884744 | tf_op jit(solution)/shard_map/ppermute | solution.py:31
  32.1 19.2 %collective-permute-start.10 = (f32[192,384]{1,0:T(8,128)S(1)}, f32[192,384]{1,0:T(8,128)S(1)}, u32[]{:S(2)}, u32[]{:S(2)}) collective-permute-start(f32[192,384]{1,0:T(8,128)S(1)} %add.5.refs_0_), channel_id=1, source_target_pairs={{0,3},{1,0},{2,1},{3,2},{4,7},{5,4},{6,5},{7,6},{8,11},{9,8},{10,9... | collective-permute-start | bytes 884744 | tf_op jit(solution)/shard_map/ppermute | solution.py:31
  38.0 17.8 %collective-permute-start = (f32[432,128]{1,0:T(8,128)S(1)}, f32[432,128]{1,0:T(8,128)S(1)}, u32[]{:S(2)}, u32[]{:S(2)}) collective-permute-start(f32[432,128]{1,0:T(8,128)S(1)} %get-tuple-element.73), channel_id=1, source_target_pairs={{0,1},{1,0},{2,3},{3,2},{4,5},{5,4},{6,7},{7,6},{8,9},{9,8},{10,11... | collective-permute-start | bytes 663560 | tf_op jit(solution)/shard_map/ppermute | solution.py:36
  38.6 19.1 %collective-permute-start.1 = (f32[432,128]{1,0:T(8,128)S(1)}, f32[432,128]{1,0:T(8,128)S(1)}, u32[]{:S(2)}, u32[]{:S(2)}) collective-permute-start(f32[432,128]{1,0:T(8,128)S(1)} %get-tuple-element.74), channel_id=1, source_target_pairs={{0,15},{1,2},{2,1},{3,4},{4,3},{5,6},{6,5},{7,8},{8,7},{9,10},{10,... | collective-permute-start | bytes 663560 | tf_op jit(solution)/shard_map/ppermute | solution.py:36
  53.6 18.3 %collective-permute-start.11 = (f32[192,384]{1,0:T(8,128)S(1)}, f32[192,384]{1,0:T(8,128)S(1)}, u32[]{:S(2)}, u32[]{:S(2)}) collective-permute-start(f32[192,384]{1,0:T(8,128)S(1)} %get-tuple-element.83), channel_id=1, source_target_pairs={{0,4},{4,8},{8,12},{12,0},{1,5},{5,9},{9,13},{13,1},{2,6},{6,10},{... | collective-permute-start | bytes 884744 | tf_op jit(solution)/shard_map/ppermute | solution.py:31
  54.2 18.1 %collective-permute-start.12 = (f32[192,384]{1,0:T(8,128)S(1)}, f32[192,384]{1,0:T(8,128)S(1)}, u32[]{:S(2)}, u32[]{:S(2)}) collective-permute-start(f32[192,384]{1,0:T(8,128)S(1)} %get-tuple-element.84), channel_id=1, source_target_pairs={{0,8},{4,12},{8,0},{12,4},{1,9},{5,13},{9,1},{13,5},{2,10},{6,14},... | collective-permute-start | bytes 884744 | tf_op jit(solution)/shard_map/ppermute | solution.py:31
  55.8 6.6 %collective-permute-start.3 = (f32[432,128]{1,0:T(8,128)S(1)}, f32[432,128]{1,0:T(8,128)S(1)}, u32[]{:S(2)}, u32[]{:S(2)}) collective-permute-start(f32[432,128]{1,0:T(8,128)S(1)} %get-tuple-element.76), channel_id=1, source_target_pairs={{0,112},{16,32},{32,16},{48,64},{64,48},{80,96},{96,80},{112,0},{1... | collective-permute-start | bytes 663560 | tf_op jit(solution)/shard_map/ppermute | solution.py:36
  57.6 17.9 %collective-permute-start.13 = (f32[192,384]{1,0:T(8,128)S(1)}, f32[192,384]{1,0:T(8,128)S(1)}, u32[]{:S(2)}, u32[]{:S(2)}) collective-permute-start(f32[192,384]{1,0:T(8,128)S(1)} %get-tuple-element.85), channel_id=1, source_target_pairs={{0,12},{4,0},{8,4},{12,8},{1,13},{5,1},{9,5},{13,9},{2,14},{6,2},{... | collective-permute-start | bytes 884744 | tf_op jit(solution)/shard_map/ppermute | solution.py:31
  68.6 7.6 %collective-permute-start.17 = (f32[1,24,256]{2,1,0:T(8,128)S(1)}, f32[1,24,256]{2,1,0:T(8,128)S(1)}, u32[]{:S(2)}, u32[]{:S(2)}) collective-permute-start(f32[1,24,256]{2,1,0:T(8,128)S(1)} %get-tuple-element.90.refs_0_), channel_id=1, source_target_pairs={{0,16},{16,0},{1,17},{17,1},{2,18},{18,2},{3,19},{19,3},{4,20},{20... | collective-permute-start | bytes 73736 | tf_op jit(solution)/shard_map/ppermute | solution.py:31
  93.8 6.4 %collective-permute-start.21 = (f32[432,128]{1,0:T(8,128)S(1)}, f32[432,128]{1,0:T(8,128)S(1)}, u32[]{:S(2)}, u32[]{:S(2)}) collective-permute-start(f32[432,128]{1,0:T(8,128)S(1)} %get-tuple-element.97), channel_id=1, source_target_pairs={{0,1},{1,0},{2,3},{3,2},{4,5},{5,4},{6,7},{7,6},{8,9},{9,8},{10,11... | collective-permute-start | bytes 663560 | tf_op jit(solution)/shard_map/ppermute | solution.py:36
  94.1 9.7 %collective-permute-start.22 = (f32[432,128]{1,0:T(8,128)S(1)}, f32[432,128]{1,0:T(8,128)S(1)}, u32[]{:S(2)}, u32[]{:S(2)}) collective-permute-start(f32[432,128]{1,0:T(8,128)S(1)} %get-tuple-element.98), channel_id=1, source_target_pairs={{0,15},{1,2},{2,1},{3,4},{4,3},{5,6},{6,5},{7,8},{8,7},{9,10},{10,... | collective-permute-start | bytes 663560 | tf_op jit(solution)/shard_map/ppermute | solution.py:36
  96.3 7.4 %collective-permute-start.23 = (f32[432,128]{1,0:T(8,128)S(1)}, f32[432,128]{1,0:T(8,128)S(1)}, u32[]{:S(2)}, u32[]{:S(2)}) collective-permute-start(f32[432,128]{1,0:T(8,128)S(1)} %get-tuple-element.99), channel_id=1, source_target_pairs={{0,16},{16,0},{32,48},{48,32},{64,80},{80,64},{96,112},{112,96},{1... | collective-permute-start | bytes 663560 | tf_op jit(solution)/shard_map/ppermute | solution.py:36
  96.3 7.4 %collective-permute-start.24 = (f32[432,128]{1,0:T(8,128)S(1)}, f32[432,128]{1,0:T(8,128)S(1)}, u32[]{:S(2)}, u32[]{:S(2)}) collective-permute-start(f32[432,128]{1,0:T(8,128)S(1)} %get-tuple-element.100), channel_id=1, source_target_pairs={{0,112},{16,32},{32,16},{48,64},{64,48},{80,96},{96,80},{112,0},{1... | collective-permute-start | bytes 663560 | tf_op jit(solution)/shard_map/ppermute | solution.py:36
  107.6 6.6 %collective-permute-start.28 = (f32[1,24,256]{2,1,0:T(8,128)S(1)}, f32[1,24,256]{2,1,0:T(8,128)S(1)}, u32[]{:S(2)}, u32[]{:S(2)}) collective-permute-start(f32[1,24,256]{2,1,0:T(8,128)S(1)} %get-tuple-element.109.refs_0_), channel_id=1, source_target_pairs={{0,16},{16,0},{1,17},{17,1},{2,18},{18,2},{3,19},{19,3},{4,20},{20... | collective-permute-start | bytes 73736 | tf_op jit(solution)/shard_map/ppermute | solution.py:31
  128.7 6.2 %collective-permute-start.32 = (f32[432,128]{1,0:T(8,128)S(1)}, f32[432,128]{1,0:T(8,128)S(1)}, u32[]{:S(2)}, u32[]{:S(2)}) collective-permute-start(f32[432,128]{1,0:T(8,128)S(1)} %get-tuple-element.115), channel_id=1, source_target_pairs={{0,1},{1,0},{2,3},{3,2},{4,5},{5,4},{6,7},{7,6},{8,9},{9,8},{10,11... | collective-permute-start | bytes 663560 | tf_op jit(solution)/shard_map/ppermute | solution.py:36
  129.2 9.4 %collective-permute-start.33 = (f32[432,128]{1,0:T(8,128)S(1)}, f32[432,128]{1,0:T(8,128)S(1)}, u32[]{:S(2)}, u32[]{:S(2)}) collective-permute-start(f32[432,128]{1,0:T(8,128)S(1)} %get-tuple-element.116), channel_id=1, source_target_pairs={{0,15},{1,2},{2,1},{3,4},{4,3},{5,6},{6,5},{7,8},{8,7},{9,10},{10,... | collective-permute-start | bytes 663560 | tf_op jit(solution)/shard_map/ppermute | solution.py:36
  131.4 7.3 %collective-permute-start.34 = (f32[432,128]{1,0:T(8,128)S(1)}, f32[432,128]{1,0:T(8,128)S(1)}, u32[]{:S(2)}, u32[]{:S(2)}) collective-permute-start(f32[432,128]{1,0:T(8,128)S(1)} %get-tuple-element.117), channel_id=1, source_target_pairs={{0,16},{16,0},{32,48},{48,32},{64,80},{80,64},{96,112},{112,96},{1... | collective-permute-start | bytes 663560 | tf_op jit(solution)/shard_map/ppermute | solution.py:36
  131.4 7.3 %collective-permute-start.35 = (f32[432,128]{1,0:T(8,128)S(1)}, f32[432,128]{1,0:T(8,128)S(1)}, u32[]{:S(2)}, u32[]{:S(2)}) collective-permute-start(f32[432,128]{1,0:T(8,128)S(1)} %get-tuple-element.118), channel_id=1, source_target_pairs={{0,112},{16,32},{32,16},{48,64},{64,48},{80,96},{96,80},{112,0},{1... | collective-permute-start | bytes 663560 | tf_op jit(solution)/shard_map/ppermute | solution.py:36
  149.5 14.3 %all-to-all-start.3 = ((f32[16,24,256]{2,1,0:T(8,128)}), f32[16,24,256]{2,1,0:T(8,128)S(1)}, u32[]{:S(2)}, u32[]{:S(2)}) async-start(f32[16,24,256]{2,1,0:T(8,128)} %shard_map.101), calls=%async_computation.3 | async-start | bytes 786432 | tf_op jit(solution)/shard_map/all_to_all | solution.py:40
  164.6 15.1 %all-to-all-start.4 = ((f32[128,1,256]{2,1,0:T(1,128)}), f32[128,1,256]{2,1,0:T(1,128)S(1)}, u32[]{:S(2)}, u32[]{:S(2)}) async-start(f32[128,1,256]{2,1,0:T(1,128)} %get-tuple-element.138), calls=%async_computation.4 | async-start | bytes 262144 | tf_op jit(solution)/shard_map/all_to_all | solution.py:40
  (26 other events, 168.5 us)

commit v3 on v2

--- a/solution.py
+++ b/solution.py
@@ -44,10 +44,6 @@
     return pl.BlockSpec(memory_space=pltpu.VMEM)
 
 
-def sm():
-    return pl.BlockSpec(memory_space=pltpu.SMEM)
-
-
 def call(body, outs, scratch=()):
     def run(*operands):
         return pl.pallas_call(
@@ -83,16 +79,13 @@
         pick[n * corners : (n + 2) * corners, :] = jnp.where(at == ids, 1.0, 0.0).astype(BF16)
 
 
-def rows_kernel(facts, *refs):
+def rows_kernel(ids_own, ids_other, *refs):
     blocks, own, other, pick = refs[:-3], refs[-3], refs[-2], refs[-1]
     my_y, my_c = lax.axis_index("y"), lax.axis_index("c")
     held = blocks[0].shape[1]
     half = own.shape[1]
     corners = half // N_GY
-    lists = []
-    for core in (my_c, 1 - my_c):
-        start = pl.multiple_of((my_y * NC + core) * N_GY, TILE)
-        lists.append(facts[pl.ds(start, N_GY), :].T[:corners])
+    lists = [ids[...].T[:corners] for ids in (ids_own, ids_other)]
     total = 0.0
     for k, block in enumerate(blocks):
         base = ((((my_y + NY - k) % NY) * NC + my_c) * held).astype(F32)
@@ -104,18 +97,14 @@
     other[...] = total[:, half:]
 
 
-def cols_kernel(facts, *refs):
-    blocks, sends, pick, total, lines = refs[:NZ], refs[NZ:-3], refs[-3], refs[-2], refs[-1]
-    my_c, my_x, my_z = (lax.axis_index(a) for a in ("c", "x", "z"))
+def cols_kernel(own, other, *refs):
+    blocks, outs, sends, pick, total = refs[:NZ], refs[NZ : NZ + 4], refs[NZ + 4 : -2], refs[-2], refs[-1]
+    my_x, my_z = lax.axis_index("x"), lax.axis_index("z")
     held = blocks[0].shape[0]
-    corners = sends[0].shape[0] // (NC * NY)
-    columns = []
-    for core in (my_c, 1 - my_c):
-        for n in range(NY * NX):
-            at = (((n // NX) * NC + core) * NX + n % NX) * NZ + my_z
-            lines[n : n + 1, :] = facts[pl.ds(at, 1), :]
-        turned_lines = lines[...].T[:corners]
-        columns += [turned_lines[:, n : n + 1] for n in range(NY * NX)]
+    half = outs[0].shape[1]
+    last = own.shape[2] - 1
+    corners = own.shape[1]
+    columns = [v[n, :, last:] for v in (own, other) for n in range(v.shape[0])]
     summed = 0.0
     for k, block in enumerate(blocks):
         base = ((my_x * NZ + (my_z + NZ - k) % NZ) * held).astype(F32)
@@ -123,6 +112,8 @@
         for part in split(block[...]):
             summed = summed + dot(pick[...], part)
     total[...] = summed
+    for n in range(2):
+        outs[2 * n][...], outs[2 * n + 1][...] = split(summed[n * half : (n + 1) * half].T)
     for k, send in enumerate(sends):
         for n in range(NC * NY):
             start = pl.multiple_of((n * NX + (my_x + k) % NX) * corners, TILE)
@@ -151,26 +142,15 @@
     return (1 - odd_b, odd_b, 3 - odd_a, 2 + odd_a)
 
 
-def first_kernel(side_rows, after, right, flex, flexed, extra, counts, *refs):
-    sends, direction = refs[:-1], refs[-1]
-    step = pl.program_id(0)
-    side = flex.shape[0]
-
-    @pl.when(step == 0)
-    def _():
-        direction[...] = (right[...] / cheb_center).astype(BF16).T
-        extra[...] = jnp.zeros_like(extra)
-        line = lax.broadcasted_iota(jnp.int32, counts.shape, 0)
-        east, south = side_rows[0].astype(F32), side_rows[1].astype(F32)
-        counts[...] = jnp.where(line == 0, east, south)
-
-    part = dot(flex[...], direction[...])
-    flexed[pl.ds(pl.multiple_of(step * side, side), side), :] = part
-    for k, wanted in enumerate(sent_sides()):
-
-        @pl.when(step == wanted)
-        def _():
-            pack(sends[k], part[:, :LANES], part[:, LANES:], counts[k // 2 : k // 2 + 1, :])
+def first_kernel(after, ids, live, right, flex, flexed, extra, counts, *sends):
+    direction = (right[...] / cheb_center).astype(BF16)
+    flexed[...] = dot(flex[...], direction, ((1,), (1,)))
+    counts[0:1, :] = jnp.broadcast_to(live[0:1, 0:1], (1, LANES))
+    counts[1:2, :] = jnp.broadcast_to(live[0:1, 1:2], (1, LANES))
+    send_sides(counts, flexed, *sends)
+    column = jnp.broadcast_to(ids[...], (LANES, LANES)).T
+    extra[...] = jnp.zeros_like(extra)
+    extra[:, extra.shape[1] - LANES :] = column[: extra.shape[0]]
 
 
 def send_sides(counts, flexed, *sends):
@@ -221,6 +201,8 @@
     corners = told.shape[1]
     told[0] = extra[...]
     told[0, :, 0:loads] = dot(stiff[0:32, :], balanced[...])[:corners]
+    for k in range(1, told.shape[0]):
+        told[k] = told[0]
 
 
 def step_on(steps, flex, dir_low, low, new_dir_low, flex_base):
@@ -229,7 +211,7 @@
     flex_base[...] = dot(flex[:, TOP:], new_dir.astype(BF16))
 
 
-def first_bulk_kernel(steps, balanced, stiff, flex, right, *outs):
+def first_bulk_kernel(steps, after, balanced, stiff, flex, right, *outs):
     right = right[...].T
     res_top, res_low, sol_top, sol_low, squares = outs[:5]
     stiffed = dot(stiff[...], balanced[...])
@@ -265,6 +247,15 @@
     while len(parts) > 1:
         parts = [p + q for p, q in zip(parts[::2], parts[1::2])]
     return parts[0]
+
+
+def first_half_kernel(high, low, values, total):
+    total[...] = split_dot(high, low, values[...].reshape(-1, values.shape[2]))
+
+
+def first_product_kernel(after, high, low, values, half, total):
+    more = split_dot(high, low, values[...].reshape(-1, values.shape[2]))
+    total[...] = (half[...] + more).reshape(total.shape)
 
 
 def gathered(blocks, stack):
@@ -350,49 +341,24 @@
     for k in range(1, NY):
         inv_blocks.append(turned(inv_t, "y", NY, k))
 
-    facts = jnp.pad(corner_map[0, 0].astype(F32), (0, LANES - corners))
-    facts = jnp.broadcast_to(facts[None, None], (N_GX * N_GY, 1, LANES))
-    facts = to_all(facts, ALL).reshape(N_GX * N_GY, LANES)
-
+    ids_line = jnp.pad(corner_map[0, 0].astype(F32), (0, LANES - corners))[None]
+    own_ids = jnp.broadcast_to(ids_line[None], (N_GY, 1, LANES))
+    own_ids = to_all(own_ids, GY).reshape(N_GY, LANES)
+
+    sides = [shape(side + side // 2, LANES)] * SIDES
+    flexed, extra, counts, *sends = call(
+        first_kernel, [shape(order, loads), shape(corners, width), shape(TILE, LANES)] + sides
+    )(own_ids, ids_line, side_rows[0].astype(F32), right, flex_block)
+
+    other_ids = turned(own_ids, "c", NC, 1)
     own_rows, other_rows = call(
         rows_kernel, [shape(cols_held, half)] * 2, scratch=[pltpu.VMEM((2 * half, rows_held), BF16)]
-    )(facts, *inv_blocks)
+    )(own_ids, other_ids, *inv_blocks)
     own_rows = own_rows + turned(other_rows, "c", NC, 1)
 
     row_parts = [own_rows]
     for k in range(1, NZ):
         row_parts.append(turned(own_rows, "z", NZ, k))
-
-    sides = [shape(side + side // 2, LANES)] * SIDES
-    from_hbm = [pltpu.with_memory_space_constraint(a, pltpu.HBM) for a in (right, flex_block)]
-    flexed, extra, counts, *sends = pl.pallas_call(
-        first_kernel,
-        grid=(SIDES,),
-        out_shape=[shape(order, loads), shape(corners, width), shape(TILE, LANES)] + sides,
-        in_specs=[
-            sm(),
-            vm(),
-            pl.BlockSpec((loads, order), lambda i: (0, 0)),
-            pl.BlockSpec((side, order), lambda i: (i, 0)),
-        ],
-        out_specs=[vm() for _ in range(3 + SIDES)],
-        scratch_shapes=[pltpu.VMEM((order, loads), BF16)],
-        compiler_params=pltpu.CompilerParams(vmem_limit_bytes=VMEM_BYTES),
-        name="first",
-    )(side_rows[0, 0], pltpu.with_memory_space_constraint(facts, pltpu.VMEM), *from_hbm)
-
-    shares = list(call(
-        cols_kernel,
-        [shape(half // NX * 2, half)] * NX,
-        scratch=[
-            pltpu.VMEM((2 * half, cols_held), BF16),
-            pltpu.VMEM((2 * half, half), F32),
-            pltpu.VMEM((NY * NX, LANES), F32),
-        ],
-    )(facts, *row_parts))
-    for k in range(1, NX):
-        shares[k] = turned(shares[k], "x", NX, k)
-    block = call(block_kernel, [shape(half, NY * corners, dtype=BF16)] * 4)(*shares)
 
     tops, lows = shape(TOP, loads), shape(order - TOP, loads)
     ride_shape = shape(TILE, width)
@@ -406,38 +372,53 @@
             axes, count = (GY, N_GY) if k < 2 else (GX, N_GX)
             ins.append(swapped(sends[k], axes, count, k % 2))
         balanced, told = call(
-            balance_kernel, [shape(order, loads, dtype=BF16), shape(1, corners, width)]
+            balance_kernel, [shape(order, loads, dtype=BF16), shape(NY * NX if iteration == 0 else 1, corners, width)]
         )(counts, flexed, *ins, stiff_block, extra)
-        values = [told]
-        for k in range(1, NY):
-            values.append(turned(told, "y", NY, k))
         steps = None
         if not last:
             rho_next = 1.0 / (2.0 * cheb_sigma - rho_prev)
             steps = (rho_next * rho_prev, 2.0 * rho_next / cheb_half)
             rho_prev = rho_next
         if iteration == 0:
+            values = to_all(told, ("y", "x"))
             kernel, state = first_bulk_kernel, (right,)
+            order_after = (values,)
         else:
+            values = [told]
+            for k in range(1, NY):
+                values.append(turned(told, "y", NY, k))
             kernel, state = bulk_kernel, (res_top, res_low, dir_top, dir_low, sol_top, sol_low)
+            order_after = ()
         outs = call(
             functools.partial(kernel, steps),
             [tops, lows, tops, lows, shape(1, loads)] + ([] if last else [lows, shape(order, loads)]),
-        )(balanced, stiff_block, flex_block, *state)
+        )(*order_after, balanced, stiff_block, flex_block, *state)
         res_top, res_low, sol_top, sol_low, squares = outs[:5]
         if iteration == 0:
             dir_top = sol_top
-        others = []
-        for k in range(NY):
-            others.append(turned(values[k], "c", NC, 1))
-        partial, ride = call(
-            half_product_kernel, [shape(half, width), ride_shape], scratch=corner_scratch
-        )(*block[:2], *values)
-        (partial,) = call(
-            functools.partial(product_kernel, loads),
-            [shape(N_GY, corners, width)],
-            scratch=corner_scratch,
-        )(squares, *block[2:], partial, ride, *others)
+            values_other = turned(values, "c", NC, 1)
+            own_high, own_low, other_high, other_low, *shares = call(
+                cols_kernel,
+                [shape(half, half, dtype=BF16)] * 4 + [shape(half // NX * 2, half)] * NX,
+                scratch=[pltpu.VMEM((2 * half, cols_held), BF16), pltpu.VMEM((2 * half, half), F32)],
+            )(values, values_other, *row_parts)
+            (partial,) = call(first_half_kernel, [shape(half, width)])(own_high, own_low, values)
+            (partial,) = call(first_product_kernel, [shape(N_GY, corners, width)])(
+                squares, other_high, other_low, values_other, partial
+            )
+            for k in range(1, NX):
+                shares[k] = turned(shares[k], "x", NX, k)
+            block = call(block_kernel, [shape(half, NY * corners, dtype=BF16)] * 4)(*shares)
+        else:
+            others = []
+            for k in range(NY):
+                others.append(turned(values[k], "c", NC, 1))
+            partial, ride = call(
+                half_product_kernel, [shape(half, width), ride_shape], scratch=corner_scratch
+            )(*block[:2], *values)
+            (partial,) = call(
+                functools.partial(product_kernel, loads), [shape(N_GY, corners, width)], scratch=corner_scratch
+            )(squares, *block[2:], partial, ride, *others)
         terms = to_all(partial, GY)
         if last:
             res_top, earlier, told = call(

time: 181 us -> 193 us (1.066)
  blocking collectives: 47.5 us -> 31.3 us
  waiting for transfers between devices: 54.1 us -> 66.4 us
  local copies, waits for them, and re-layouts: 5.07 us -> 14 us
  starting transfers between devices: 47.6 us -> 53.1 us
    all_to_all x3 -> x2, blocking collectives: 47.5 us -> 31.3 us  [to_all(): return lax.all_to_all(copies, axes, split_axis=0, concat_axis=0, tiled=True)]
    all_to_all x2 -> x4, starting transfers between devices: 9.06 us -> 21.2 us  [to_all(): return lax.all_to_all(copies, axes, split_axis=0, concat_axis=0, tiled=True)]
    all_to_all x2 -> x4, waiting for transfers between devices: 15.1 us -> 25.9 us  [to_all(): return lax.all_to_all(copies, axes, split_axis=0, concat_axis=0, tiled=True)]
    unnamed x12 -> x32, local copies, waits for them, and re-layouts: 4.71 us -> 13.1 us
    ppermute x12, waiting for transfers between devices: 14.1 us -> 19.8 us  [swapped(): return lax.ppermute(array, axes, pairs)]
    ppermute x31 -> x26, starting transfers between devices: 24.3 us -> 19.4 us  [turned(): lax.ppermute(array, axes, [(i, (i + by) % count) for i in range(count)])]
    pallas_call x1 -> x0, Pallas kernels: 4.32 us -> none  [local(): pl.pallas_call(first_kernel, grid=(SIDES,), out_shape=[shape(order, loads...]
    ppermute x31 -> x26, waiting for transfers between devices: 24.9 us -> 20.6 us  [turned(): lax.ppermute(array, axes, [(i, (i + by) % count) for i in range(count)])]
  transfers between devices with their start and end apart: 45 -> 42, of which waited for: 18 -> 21; matrix products, arithmetic and copies ran while one was open for 3% -> 2% of each run, Pallas kernels for 9% -> 7%
where the time goes in v3:
time: 193 us; the launch traced here: 191 us
  waiting for transfers between devices  66.4 us (34%)
  starting transfers between devices  53.1 us (28%)
  blocking collectives  31.3 us (16%)
  Pallas kernels  22.5 us (12%)
  local copies, waits for them, and re-layouts  14 us (7%)
  other arithmetic  3.23 us (2%)
    all_to_all x2, blocking collectives, to_all(): return lax.all_to_all(copies, axes, split_axis=0, concat_axis=0, tiled=True)  31.3 us
    all_to_all x4, waiting for transfers between devices, to_all(): return lax.all_to_all(copies, axes, split_axis=0, concat_axis=0, tiled=True)  25.9 us
    pallas_call x19, Pallas kernels, run(): pl.pallas_call(body, out_shape=outs, in_specs=[vm() for _ in operands], o...  22.5 us
    all_to_all x4, starting transfers between devices, to_all(): return lax.all_to_all(copies, axes, split_axis=0, concat_axis=0, tiled=True)  21.2 us
    ppermute x26, waiting for transfers between devices, turned(): lax.ppermute(array, axes, [(i, (i + by) % count) for i in range(count)])  20.6 us
    ppermute x12, waiting for transfers between devices, swapped(): return lax.ppermute(array, axes, pairs)  19.8 us
    ppermute x26, starting transfers between devices, turned(): lax.ppermute(array, axes, [(i, (i + by) % count) for i in range(count)])  19.4 us
    unnamed x32, local copies, waits for them, and re-layouts  13.1 us
  transfers between devices with their start and end apart: 42, of which 21 were waited for; matrix products, arithmetic and copies ran while one was open for 2% of the time, Pallas kernels for 7%

profile of v3, /device:TPU:0, one launch (start us, length us, event | category | flops | bytes accessed | tf_op | source)
XLA Modules:
  0.0 191.5 jit_solution(4753964172701823122)
XLA Ops:
  1.9 8.0 %all-to-all-start = ((f32[16,1,128]{2,1,0:T(1,128)}), f32[16,1,128]{2,1,0:T(1,128)S(1)}, u32[]{:S(2)}, u32[]{:S(2)}) async-start(f32[16,1,128]{2,1,0:T(1,128)} %broadcast_in_dim.14), calls=%async_computation | async-start | bytes 16384 | tf_op jit(solution)/shard_map/all_to_all | solution.py:40
  10.6 6.9 %all-to-all-done = f32[16,1,128]{2,1,0:T(1,128)S(1)} async-done(((f32[16,1,128]{2,1,0:T(1,128)}), f32[16,1,128]{2,1,0:T(1,128)S(1)}, u32[]{:S(2)}, u32[]{:S(2)}) %all-to-all-start) | async-done | bytes 8224 | tf_op jit(solution)/shard_map/all_to_all | solution.py:40
  24.0 3.1 %collective-permute-start.3 = (f32[432,128]{1,0:T(8,128)S(1)}, f32[432,128]{1,0:T(8,128)S(1)}, u32[]{:S(2)}, u32[]{:S(2)}) collective-permute-start(f32[432,128]{1,0:T(8,128)S(1)} %get-tuple-element.78), channel_id=1, source_target_pairs={{0,112},{16,32},{32,16},{48,64},{64,48},{80,96},{96,80},{112,0},{1... | collective-permute-start | bytes 663560 | tf_op jit(solution)/shard_map/ppermute | solution.py:36
  27.9 2.9 %collective-permute-start.7 = (f32[192,384]{1,0:T(8,128)S(1)}, f32[192,384]{1,0:T(8,128)}, u32[]{:S(2)}, u32[]{:S(2)}) collective-permute-start(f32[192,384]{1,0:T(8,128)S(1)} %bitcast.40), channel_id=1, source_target_pairs={{0,64},{32,96},{64,0},{96,32},{1,65},{33,97},{65,1},{97,33},{2,66}... | collective-permute-start | bytes 884744 | tf_op jit(solution)/shard_map/ppermute | solution.py:31
  35.2 4.5 %all-to-all-start.1 = ((f32[16,24,256]{2,1,0:T(8,128)}), f32[16,24,256]{2,1,0:T(8,128)S(1)}, u32[]{:S(2)}, u32[]{:S(2)}) async-start(f32[16,24,256]{2,1,0:T(8,128)} %get-tuple-element.80), calls=%async_computation.1 | async-start | bytes 786432 | tf_op jit(solution)/shard_map/all_to_all | solution.py:40
  45.5 3.9 %shard_map.88 = (f32[192,384]{1,0:T(8,128)S(1)}, f32[192,384]{1,0:T(8,128)}) custom-call(f32[16,128]{1,0:T(8,128)S(1)} %bitcast.45, f32[16,128]{1,0:T(8,128)S(1)} %collective-permute-done.5.ids_other, f32[192,384]{1,0:T(8,128)S(1)} %bitcast.42, f32[192,384]{1,0:T(8,128)} %collective-permute-done.6.refs_1_, f32[192,384]{1,0:T(8,128)} %collective-permute-done.7.refs_2_, ...), custom_call_target="tpu_custom_call" | custom-call | tf_op jit(solution)/shard_map/pallas_call | solution.py:49
  59.5 2.9 %shard_map.87 = (f32[128,176]{1,0:T(8,128)S(1)}, f32[1024,176]{1,0:T(8,128)S(1)}, f32[128,176]{1,0:T(8,128)S(1)}, f32[1024,176]{1,0:T(8,128)S(1)}, f32[1,176]{1,...) custom-call(f32[16,24,256]{2,1,0:T(8,128)S(1)} %all-to-all-done.1.after.own.values, ...), custom_call_target="tpu_custom_call" | custom-call | tf_op jit(solution)/shard_map/pallas_call | solution.py:49
  62.5 2.9 %collective-permute-done.11.refs_2_ = f32[192,384]{1,0:T(8,128)S(1)} collective-permute-done((f32[192,384]{1,0:T(8,128)S(1)}, f32[192,384]{1,0:T(8,128)S(1)}, u32[]{:S(2)}, u32[]{:S(2)}) %collective-permute-start.11) | collective-permute-done | bytes 294944 | tf_op jit(solution)/shard_map/ppermute | solution.py:31
  65.4 5.1 %collective-permute-done.10.refs_1_ = f32[192,384]{1,0:T(8,128)S(1)} collective-permute-done((f32[192,384]{1,0:T(8,128)S(1)}, f32[192,384]{1,0:T(8,128)S(1)}, u32[]{:S(2)}, u32[]{:S(2)}) %collective-permute-start.10) | collective-permute-done | bytes 294944 | tf_op jit(solution)/shard_map/ppermute | solution.py:31
  70.5 2.1 %shard_map.89 = (bf16[384,384]{1,0:T(8,128)(2,1)S(1)}, bf16[384,384]{1,0:T(8,128)(2,1)S(1)}, bf16[384,384]{1,0:T(8,128)(2,1)S(1)}, bf16[384,384]{1,0:T(8,128)(2,...) custom-call(f32[16,24,256]{2,1,0:T(8,128)S(1)} %all-to-all-done.1.aft, ...), custom_call_target="tpu_custom_call" | custom-call | tf_op jit(solution)/shard_map/pallas_call | solution.py:49
  73.5 13.6 %all_to_all.30.terms = f32[16,24,256]{2,1,0:T(8,128)S(1)} all-to-all(f32[16,24,256]{2,1,0:T(8,128)S(1)} %shard_map.91), channel_id=1, replica_groups=mesh['y'=4,'c'=2,'x'=4,'z'=4] {'x','z'}, dimensions={0} | all-to-all | bytes 786432 | tf_op jit(solution)/shard_map/all_to_all | solution.py:40
  88.5 2.2 %collective-permute-start.14 = (f32[432,128]{1,0:T(8,128)S(1)}, f32[432,128]{1,0:T(8,128)S(1)}, u32[]{:S(2)}, u32[]{:S(2)}) collective-permute-start(f32[432,128]{1,0:T(8,128)S(1)} %get-tuple-element.94), channel_id=1, source_target_pairs={{0,15},{1,2},{2,1},{3,4},{4,3},{5,6},{6,5},{7,8},{8,7},{9,10},{10,... | collective-permute-start | bytes 663560 | tf_op jit(solution)/shard_map/ppermute | solution.py:36
  94.7 6.9 %collective-permute-done.14.in_b = f32[432,128]{1,0:T(8,128)S(1)} collective-permute-done((f32[432,128]{1,0:T(8,128)S(1)}, f32[432,128]{1,0:T(8,128)S(1)}, u32[]{:S(2)}, u32[]{:S(2)}) %collective-permute-start.14) | collective-permute-done | bytes 221216 | tf_op jit(solution)/shard_map/ppermute | solution.py:36
  101.6 6.6 %collective-permute-done.16.in_y = f32[432,128]{1,0:T(8,128)S(1)} collective-permute-done((f32[432,128]{1,0:T(8,128)S(1)}, f32[432,128]{1,0:T(8,128)S(1)}, u32[]{:S(2)}, u32[]{:S(2)}) %collective-permute-start.16) | collective-permute-done | bytes 221216 | tf_op jit(solution)/shard_map/ppermute | solution.py:36
  112.6 2.8 %collective-permute-done.21.refs_2_ = f32[1,24,256]{2,1,0:T(8,128)S(1)} collective-permute-done((f32[1,24,256]{2,1,0:T(8,128)S(1)}, f32[1,24,256]{2,1,0:T(8,128)S(1)}, u32[]{:S(2)}, u32[]{:S(2)}) %collective-permute-start.21) | collective-permute-done | bytes 24608 | tf_op jit(solution)/shard_map/ppermute | solution.py:31
  116.2 3.1 %shard_map.94 = (f32[128,176]{1,0:T(8,128)S(1)}, f32[1024,176]{1,0:T(8,128)S(1)}, f32[128,176]{1,0:T(8,128)S(1)}, f32[1024,176]{1,0:T(8,128)S(1)}, f32[1,176]{1,...) custom-call(bf16[1152,176]{1,0:T(8,128)(2,1)S(1)} %get-tuple-element.98.balanced, ...), custom_call_target="tpu_custom_call" | custom-call | tf_op jit(solution)/shard_map/pallas_call | solution.py:49
  120.0 17.7 %all_to_all.31.terms = f32[16,24,256]{2,1,0:T(8,128)S(1)} all-to-all(f32[16,24,256]{2,1,0:T(8,128)S(1)} %shard_map.97), channel_id=1, replica_groups=mesh['y'=4,'c'=2,'x'=4,'z'=4] {'x','z'}, dimensions={0} | all-to-all | bytes 786432 | tf_op jit(solution)/shard_map/all_to_all | solution.py:40
  138.7 2.2 %collective-permute-start.28 = (f32[432,128]{1,0:T(8,128)S(1)}, f32[432,128]{1,0:T(8,128)S(1)}, u32[]{:S(2)}, u32[]{:S(2)}) collective-permute-start(f32[432,128]{1,0:T(8,128)S(1)} %get-tuple-element.120), channel_id=1, source_target_pairs={{0,15},{1,2},{2,1},{3,4},{4,3},{5,6},{6,5},{7,8},{8,7},{9,10},{10,... | collective-permute-start | bytes 663560 | tf_op jit(solution)/shard_map/ppermute | solution.py:36
  144.8 3.6 %collective-permute-done.28.in_b = f32[432,128]{1,0:T(8,128)S(1)} collective-permute-done((f32[432,128]{1,0:T(8,128)S(1)}, f32[432,128]{1,0:T(8,128)S(1)}, u32[]{:S(2)}, u32[]{:S(2)}) %collective-permute-start.28) | collective-permute-done | bytes 221216 | tf_op jit(solution)/shard_map/ppermute | solution.py:36
  152.8 3.0 %collective-permute-done.32.refs_2_ = f32[1,24,256]{2,1,0:T(8,128)S(1)} collective-permute-done((f32[1,24,256]{2,1,0:T(8,128)S(1)}, f32[1,24,256]{2,1,0:T(8,128)S(1)}, u32[]{:S(2)}, u32[]{:S(2)}) %collective-permute-start.32) | collective-permute-done | bytes 24608 | tf_op jit(solution)/shard_map/ppermute | solution.py:31
  161.0 3.6 %all-to-all-start.4 = ((f32[16,24,256]{2,1,0:T(8,128)}), f32[16,24,256]{2,1,0:T(8,128)S(1)}, u32[]{:S(2)}, u32[]{:S(2)}) async-start(f32[16,24,256]{2,1,0:T(8,128)} %shard_map.102), calls=%async_computation.4 | async-start | bytes 786432 | tf_op jit(solution)/shard_map/all_to_all | solution.py:40
  166.0 9.3 %all-to-all-done.4.terms = f32[16,24,256]{2,1,0:T(8,128)S(1)} async-done(((f32[16,24,256]{2,1,0:T(8,128)}), f32[16,24,256]{2,1,0:T(8,128)S(1)}, u32[]{:S(2)}, u32[]{:S(2)}) %all-to-all-start.4) | async-done | bytes 393248 | tf_op jit(solution)/shard_map/all_to_all | solution.py:40
  176.1 5.1 %all-to-all-start.5 = ((f32[128,1,256]{2,1,0:T(1,128)}), f32[128,1,256]{2,1,0:T(1,128)S(1)}, u32[]{:S(2)}, u32[]{:S(2)}) async-start(f32[128,1,256]{2,1,0:T(1,128)} %get-tuple-element.142), calls=%async_computation.5 | async-start | bytes 262144 | tf_op jit(solution)/shard_map/all_to_all | solution.py:40
  182.6 8.1 %all-to-all-done.5 = f32[128,1,256]{2,1,0:T(1,128)S(1)} async-done(((f32[128,1,256]{2,1,0:T(1,128)}), f32[128,1,256]{2,1,0:T(1,128)S(1)}, u32[]{:S(2)}, u32[]{:S(2)}) %all-to-all-start.5) | async-done | bytes 131104 | tf_op jit(solution)/shard_map/all_to_all | solution.py:40
  (126 shorter events, 60.5 us)
Async XLA Ops:
  1.9 15.5 %all-to-all-start = ((f32[16,1,128]{2,1,0:T(1,128)}), f32[16,1,128]{2,1,0:T(1,128)S(1)}, u32[]{:S(2)}, u32[]{:S(2)}) async-start(f32[16,1,128]{2,1,0:T(1,128)} %broadcast_in_dim.14), calls=%async_computation | async-start | bytes 16384 | tf_op jit(solution)/shard_map/all_to_all | solution.py:40
  22.2 9.3 %collective-permute-start.1 = (f32[432,128]{1,0:T(8,128)S(1)}, f32[432,128]{1,0:T(8,128)S(1)}, u32[]{:S(2)}, u32[]{:S(2)}) collective-permute-start(f32[432,128]{1,0:T(8,128)S(1)} %get-tuple-element.76), channel_id=1, source_target_pairs={{0,15},{1,2},{2,1},{3,4},{4,3},{5,6},{6,5},{7,8},{8,7},{9,10},{10,... | collective-permute-start | bytes 663560 | tf_op jit(solution)/shard_map/ppermute | solution.py:36
  24.0 9.0 %collective-permute-start.2 = (f32[432,128]{1,0:T(8,128)S(1)}, f32[432,128]{1,0:T(8,128)S(1)}, u32[]{:S(2)}, u32[]{:S(2)}) collective-permute-start(f32[432,128]{1,0:T(8,128)S(1)} %get-tuple-element.77), channel_id=1, source_target_pairs={{0,16},{16,0},{32,48},{48,32},{64,80},{80,64},{96,112},{112,96},{1... | collective-permute-start | bytes 663560 | tf_op jit(solution)/shard_map/ppermute | solution.py:36
  24.0 9.0 %collective-permute-start.3 = (f32[432,128]{1,0:T(8,128)S(1)}, f32[432,128]{1,0:T(8,128)S(1)}, u32[]{:S(2)}, u32[]{:S(2)}) collective-permute-start(f32[432,128]{1,0:T(8,128)S(1)} %get-tuple-element.78), channel_id=1, source_target_pairs={{0,112},{16,32},{32,16},{48,64},{64,48},{80,96},{96,80},{112,0},{1... | collective-permute-start | bytes 663560 | tf_op jit(solution)/shard_map/ppermute | solution.py:36
  27.1 16.3 %collective-permute-start.8 = (f32[192,384]{1,0:T(8,128)S(1)}, f32[192,384]{1,0:T(8,128)}, u32[]{:S(2)}, u32[]{:S(2)}) collective-permute-start(f32[192,384]{1,0:T(8,128)S(1)} %bitcast.39), channel_id=1, source_target_pairs={{0,96},{32,0},{64,32},{96,64},{1,97},{33,1},{65,33},{97,65},{2,98}... | collective-permute-start | bytes 884744 | tf_op jit(solution)/shard_map/ppermute | solution.py:31
  27.9 15.6 %collective-permute-start.7 = (f32[192,384]{1,0:T(8,128)S(1)}, f32[192,384]{1,0:T(8,128)}, u32[]{:S(2)}, u32[]{:S(2)}) collective-permute-start(f32[192,384]{1,0:T(8,128)S(1)} %bitcast.40), channel_id=1, source_target_pairs={{0,64},{32,96},{64,0},{96,32},{1,65},{33,97},{65,1},{97,33},{2,66}... | collective-permute-start | bytes 884744 | tf_op jit(solution)/shard_map/ppermute | solution.py:31
  31.4 13.1 %collective-permute-start.6 = (f32[192,384]{1,0:T(8,128)S(1)}, f32[192,384]{1,0:T(8,128)}, u32[]{:S(2)}, u32[]{:S(2)}) collective-permute-start(f32[192,384]{1,0:T(8,128)S(1)} %bitcast.41), channel_id=1, source_target_pairs={{0,32},{32,64},{64,96},{96,0},{1,33},{33,65},{65,97},{97,1},{2,34}... | collective-permute-start | bytes 884744 | tf_op jit(solution)/shard_map/ppermute | solution.py:31
  35.2 15.9 %all-to-all-start.1 = ((f32[16,24,256]{2,1,0:T(8,128)}), f32[16,24,256]{2,1,0:T(8,128)S(1)}, u32[]{:S(2)}, u32[]{:S(2)}) async-start(f32[16,24,256]{2,1,0:T(8,128)} %get-tuple-element.80), calls=%async_computation.1 | async-start | bytes 786432 | tf_op jit(solution)/shard_map/all_to_all | solution.py:40
  51.2 19.3 %collective-permute-start.4 = (f32[16,24,256]{2,1,0:T(8,128)S(1)}, f32[16,24,256]{2,1,0:T(8,128)S(1)}, u32[]{:S(2)}, u32[]{:S(2)}) collective-permute-start(f32[16,24,256]{2,1,0:T(8,128)S(1)} %all-to-all-done.1.after.own.values), channel_id=1, source_target_pairs={{0,16},{16,0},{1,17},{17,1},{2,18},{18,2},{3,19},{19,3},{4,20},{20... | collective-permute-start | bytes 1179656 | tf_op jit(solution)/shard_map/ppermute | solution.py:31
  52.4 10.1 %collective-permute-start.12 = (f32[192,384]{1,0:T(8,128)S(1)}, f32[192,384]{1,0:T(8,128)S(1)}, u32[]{:S(2)}, u32[]{:S(2)}) collective-permute-start(f32[192,384]{1,0:T(8,128)S(1)} %add.5.refs_0_), channel_id=1, source_target_pairs={{0,3},{1,0},{2,1},{3,2},{4,7},{5,4},{6,5},{7,6},{8,11},{9,8},{10,9... | collective-permute-start | bytes 884744 | tf_op jit(solution)/shard_map/ppermute | solution.py:31
  54.0 11.4 %collective-permute-start.11 = (f32[192,384]{1,0:T(8,128)S(1)}, f32[192,384]{1,0:T(8,128)S(1)}, u32[]{:S(2)}, u32[]{:S(2)}) collective-permute-start(f32[192,384]{1,0:T(8,128)S(1)} %add.5.refs_0_), channel_id=1, source_target_pairs={{0,2},{1,3},{2,0},{3,1},{4,6},{5,7},{6,4},{7,5},{8,10},{9,11},{10,... | collective-permute-start | bytes 884744 | tf_op jit(solution)/shard_map/ppermute | solution.py:31
  54.7 15.7 %collective-permute-start.10 = (f32[192,384]{1,0:T(8,128)S(1)}, f32[192,384]{1,0:T(8,128)S(1)}, u32[]{:S(2)}, u32[]{:S(2)}) collective-permute-start(f32[192,384]{1,0:T(8,128)S(1)} %add.5.refs_0_), channel_id=1, source_target_pairs={{0,1},{1,2},{2,3},{3,0},{4,5},{5,6},{6,7},{7,4},{8,9},{9,10},{10,1... | collective-permute-start | bytes 884744 | tf_op jit(solution)/shard_map/ppermute | solution.py:31
  88.5 13.1 %collective-permute-start.14 = (f32[432,128]{1,0:T(8,128)S(1)}, f32[432,128]{1,0:T(8,128)S(1)}, u32[]{:S(2)}, u32[]{:S(2)}) collective-permute-start(f32[432,128]{1,0:T(8,128)S(1)} %get-tuple-element.94), channel_id=1, source_target_pairs={{0,15},{1,2},{2,1},{3,4},{4,3},{5,6},{6,5},{7,8},{8,7},{9,10},{10,... | collective-permute-start | bytes 663560 | tf_op jit(solution)/shard_map/ppermute | solution.py:36
  90.7 19.7 %collective-permute-start.17 = (f32[192,384]{1,0:T(8,128)S(1)}, f32[192,384]{1,0:T(8,128)S(1)}, u32[]{:S(2)}, u32[]{:S(2)}) collective-permute-start(f32[192,384]{1,0:T(8,128)S(1)} %get-tuple-element.106), channel_id=1, source_target_pairs={{0,4},{4,8},{8,12},{12,0},{1,5},{5,9},{9,13},{13,1},{2,6},{6,10},{... | collective-permute-start | bytes 884744 | tf_op jit(solution)/shard_map/ppermute | solution.py:31
  91.7 19.4 %collective-permute-start.18 = (f32[192,384]{1,0:T(8,128)S(1)}, f32[192,384]{1,0:T(8,128)S(1)}, u32[]{:S(2)}, u32[]{:S(2)}) collective-permute-start(f32[192,384]{1,0:T(8,128)S(1)} %get-tuple-element.107), channel_id=1, source_target_pairs={{0,8},{4,12},{8,0},{12,4},{1,9},{5,13},{9,1},{13,5},{2,10},{6,14},... | collective-permute-start | bytes 884744 | tf_op jit(solution)/shard_map/ppermute | solution.py:31
  93.1 22.8 %collective-permute-start.19 = (f32[192,384]{1,0:T(8,128)S(1)}, f32[192,384]{1,0:T(8,128)S(1)}, u32[]{:S(2)}, u32[]{:S(2)}) collective-permute-start(f32[192,384]{1,0:T(8,128)S(1)} %get-tuple-element.108), channel_id=1, source_target_pairs={{0,12},{4,0},{8,4},{12,8},{1,13},{5,1},{9,5},{13,9},{2,14},{6,2},{... | collective-permute-start | bytes 884744 | tf_op jit(solution)/shard_map/ppermute | solution.py:31
  111.1 8.5 %collective-permute-start.23 = (f32[1,24,256]{2,1,0:T(8,128)S(1)}, f32[1,24,256]{2,1,0:T(8,128)S(1)}, u32[]{:S(2)}, u32[]{:S(2)}) collective-permute-start(f32[1,24,256]{2,1,0:T(8,128)S(1)} %get-tuple-element.113.refs_0_), channel_id=1, source_target_pairs={{0,16},{16,0},{1,17},{17,1},{2,18},{18,2},{3,19},{19,3},{4,20},{20... | collective-permute-start | bytes 73736 | tf_op jit(solution)/shard_map/ppermute | solution.py:31
  138.7 9.7 %collective-permute-start.28 = (f32[432,128]{1,0:T(8,128)S(1)}, f32[432,128]{1,0:T(8,128)S(1)}, u32[]{:S(2)}, u32[]{:S(2)}) collective-permute-start(f32[432,128]{1,0:T(8,128)S(1)} %get-tuple-element.120), channel_id=1, source_target_pairs={{0,15},{1,2},{2,1},{3,4},{4,3},{5,6},{6,5},{7,8},{8,7},{9,10},{10,... | collective-permute-start | bytes 663560 | tf_op jit(solution)/shard_map/ppermute | solution.py:36
  140.9 7.4 %collective-permute-start.29 = (f32[432,128]{1,0:T(8,128)S(1)}, f32[432,128]{1,0:T(8,128)S(1)}, u32[]{:S(2)}, u32[]{:S(2)}) collective-permute-start(f32[432,128]{1,0:T(8,128)S(1)} %get-tuple-element.121), channel_id=1, source_target_pairs={{0,16},{16,0},{32,48},{48,32},{64,80},{80,64},{96,112},{112,96},{1... | collective-permute-start | bytes 663560 | tf_op jit(solution)/shard_map/ppermute | solution.py:36
  140.9 7.4 %collective-permute-start.30 = (f32[432,128]{1,0:T(8,128)S(1)}, f32[432,128]{1,0:T(8,128)S(1)}, u32[]{:S(2)}, u32[]{:S(2)}) collective-permute-start(f32[432,128]{1,0:T(8,128)S(1)} %get-tuple-element.122), channel_id=1, source_target_pairs={{0,112},{16,32},{32,16},{48,64},{64,48},{80,96},{96,80},{112,0},{1... | collective-permute-start | bytes 663560 | tf_op jit(solution)/shard_map/ppermute | solution.py:36
  152.0 7.8 %collective-permute-start.34 = (f32[1,24,256]{2,1,0:T(8,128)S(1)}, f32[1,24,256]{2,1,0:T(8,128)S(1)}, u32[]{:S(2)}, u32[]{:S(2)}) collective-permute-start(f32[1,24,256]{2,1,0:T(8,128)S(1)} %get-tuple-element.134.refs_0_), channel_id=1, source_target_pairs={{0,16},{16,0},{1,17},{17,1},{2,18},{18,2},{3,19},{19,3},{4,20},{20... | collective-permute-start | bytes 73736 | tf_op jit(solution)/shard_map/ppermute | solution.py:31
  152.8 7.1 %collective-permute-start.37 = (f32[1,24,256]{2,1,0:T(8,128)S(1)}, f32[1,24,256]{2,1,0:T(8,128)S(1)}, u32[]{:S(2)}, u32[]{:S(2)}) collective-permute-start(f32[1,24,256]{2,1,0:T(8,128)S(1)} %collective-permute-done.33.refs_3_), channel_id=1, source_target_pairs={{0,16},{16,0},{1,17},{17,1},{2,18},{18,2},{3,19},{19,3},{4,20},{20... | collective-permute-start | bytes 73736 | tf_op jit(solution)/shard_map/ppermute | solution.py:31
  161.0 14.3 %all-to-all-start.4 = ((f32[16,24,256]{2,1,0:T(8,128)}), f32[16,24,256]{2,1,0:T(8,128)S(1)}, u32[]{:S(2)}, u32[]{:S(2)}) async-start(f32[16,24,256]{2,1,0:T(8,128)} %shard_map.102), calls=%async_computation.4 | async-start | bytes 786432 | tf_op jit(solution)/shard_map/all_to_all | solution.py:40
  176.1 14.7 %all-to-all-start.5 = ((f32[128,1,256]{2,1,0:T(1,128)}), f32[128,1,256]{2,1,0:T(1,128)S(1)}, u32[]{:S(2)}, u32[]{:S(2)}) async-start(f32[128,1,256]{2,1,0:T(1,128)} %get-tuple-element.142), calls=%async_computation.5 | async-start | bytes 262144 | tf_op jit(solution)/shard_map/all_to_all | solution.py:40
  (33 other events, 180.9 us)

commit v4 on v3

--- a/solution.py
+++ b/solution.py
@@ -243,19 +243,32 @@
     return dot(high[...], values_high) + (dot(high[...], values_low) + dot(low[...], values_high))
 
 
-def tree_sum(parts):
-    while len(parts) > 1:
-        parts = [p + q for p, q in zip(parts[::2], parts[1::2])]
-    return parts[0]
-
-
 def first_half_kernel(high, low, values, total):
     total[...] = split_dot(high, low, values[...].reshape(-1, values.shape[2]))
 
 
-def first_product_kernel(after, high, low, values, half, total):
+def dealt(total, outs):
+    my_x, my_z = lax.axis_index("x"), lax.axis_index("z")
+    for k, out in enumerate(outs):
+        for j in range(NX):
+            out[j] = total[((my_x + j) % NX) * NZ + (my_z + k) % NZ]
+
+
+def first_product_kernel(high, low, values, half, *refs):
+    outs, total = refs[:-1], refs[-1]
     more = split_dot(high, low, values[...].reshape(-1, values.shape[2]))
     total[...] = (half[...] + more).reshape(total.shape)
+    dealt(total, outs)
+
+
+def ring_sum(parts):
+    return (parts[0] + parts[2]) + (parts[1] + parts[3])
+
+
+def sum_kernel(*refs):
+    parts, outs = refs[:NZ], refs[NZ:]
+    for j, out in enumerate(outs):
+        out[...] = ring_sum([p[j] for p in parts])
 
 
 def gathered(blocks, stack):
@@ -264,8 +277,7 @@
     for k, block in enumerate(blocks):
         at = pl.multiple_of(((my_y + NY - k) % NY) * corners, TILE)
         stack[pl.ds(at, corners), :] = block[0]
-    b = [block[0, 0:TILE, :] for block in blocks]
-    return (b[0] + b[2]) + (b[1] + b[3])
+    return ring_sum([block[0, 0:TILE, :] for block in blocks])
 
 
 def half_product_kernel(high, low, *refs):
@@ -274,19 +286,20 @@
     total[...] = split_dot(high, low, stack[...])
 
 
-def product_kernel(loads, after, high, low, half, ride, *refs):
-    blocks, total, stack = refs[:NY], refs[NY], refs[NY + 1]
+def product_kernel(loads, high, low, half, ride, *refs):
+    blocks, outs, stack, total = refs[:NY], refs[NY:-2], refs[-2], refs[-1]
     both = ride[...] + gathered(blocks, stack)
     result = (half[...] + split_dot(high, low, stack[...])).reshape(total.shape)
     lane = lax.broadcasted_iota(jnp.int32, both.shape, 1)
     for k in range(total.shape[0]):
         total[k] = result[k]
         total[k, 0:TILE, :] = jnp.where(lane < loads, result[k, 0:TILE, :], both)
-
-
-def correction_of(terms, squares, res_top, new_res_top, earlier):
-    corners = terms.shape[1]
-    total = tree_sum([terms[k] for k in range(terms.shape[0])])
+    dealt(total, outs)
+
+
+def correction_of(squares, res_top, terms, new_res_top, earlier):
+    corners = terms[0].shape[0]
+    total = ring_sum([t[...] for t in terms])
     earlier[...] = total[0:TILE, :]
     new_res_top[...] = res_top[...]
     new_res_top[:corners, :] = res_top[:corners, :] - total[:, : res_top.shape[1]]
@@ -294,15 +307,17 @@
     return top, squares[...] + jnp.sum(top * top, axis=0, keepdims=True)
 
 
-def last_kernel(terms, squares, res_top, new_res_top, earlier, told):
-    _, norm = correction_of(terms, squares, res_top, new_res_top, earlier)
+def last_kernel(squares, res_top, *refs):
+    terms, (new_res_top, earlier, told) = refs[:NX], refs[NX:]
+    _, norm = correction_of(squares, res_top, terms, new_res_top, earlier)
     padded = jnp.concatenate([norm, jnp.zeros((1, told.shape[2] - norm.shape[1]), F32)], axis=1)
     told[...] = jnp.broadcast_to(padded[None], told.shape)
 
 
-def correct_kernel(steps, counts, terms, squares, res_top, dir_top, flex, flex_base, *outs):
+def correct_kernel(steps, squares, res_top, counts, dir_top, flex, flex_base, *refs):
+    terms, outs = refs[:NX], refs[NX:]
     new_res_top, earlier, extra, new_dir_top, flexed = outs[:5]
-    top, norm = correction_of(terms, squares, res_top, new_res_top, earlier)
+    top, norm = correction_of(squares, res_top, terms, new_res_top, earlier)
     new_dir = steps[0] * dir_top[...] + steps[1] * top
     new_dir_top[...] = new_dir
     flexed[...] = flex_base[...] + dot(flex[:, :TOP], new_dir.astype(BF16))
@@ -363,6 +378,8 @@
     tops, lows = shape(TOP, loads), shape(order - TOP, loads)
     ride_shape = shape(TILE, width)
     corner_scratch = [pltpu.VMEM((NY * corners, width), F32)]
+    dealt_shapes = [shape(NX, corners, width)] * NZ
+    dealt_scratch = pltpu.VMEM((N_GY, corners, width), F32)
     rho_prev = 1.0 / cheb_sigma
     norms = []
     for iteration in range(ITERS):
@@ -403,8 +420,8 @@
                 scratch=[pltpu.VMEM((2 * half, cols_held), BF16), pltpu.VMEM((2 * half, half), F32)],
             )(values, values_other, *row_parts)
             (partial,) = call(first_half_kernel, [shape(half, width)])(own_high, own_low, values)
-            (partial,) = call(first_product_kernel, [shape(N_GY, corners, width)])(
-                squares, other_high, other_low, values_other, partial
+            shared = call(first_product_kernel, dealt_shapes, scratch=[dealt_scratch])(
+                other_high, other_low, values_other, partial
             )
             for k in range(1, NX):
                 shares[k] = turned(shares[k], "x", NX, k)
@@ -416,20 +433,25 @@
             partial, ride = call(
                 half_product_kernel, [shape(half, width), ride_shape], scratch=corner_scratch
             )(*block[:2], *values)
-            (partial,) = call(
-                functools.partial(product_kernel, loads), [shape(N_GY, corners, width)], scratch=corner_scratch
-            )(squares, *block[2:], partial, ride, *others)
-        terms = to_all(partial, GY)
+            shared = call(
+                functools.partial(product_kernel, loads), dealt_shapes, scratch=corner_scratch + [dealt_scratch]
+            )(*block[2:], partial, ride, *others)
+        shared = list(shared)
+        for k in range(1, NZ):
+            shared[k] = turned(shared[k], "z", NZ, k)
+        terms = list(call(sum_kernel, [shape(corners, width)] * NX)(*shared))
+        for k in range(1, NX):
+            terms[k] = turned(terms[k], "x", NX, k)
         if last:
             res_top, earlier, told = call(
                 last_kernel, [tops, ride_shape, shape(N_GX * N_GY, 1, width)]
-            )(terms, squares, res_top)
+            )(squares, res_top, *terms)
         else:
             dir_low, flex_base = outs[5:]
             res_top, earlier, extra, dir_top, flexed, *sends = call(
                 functools.partial(correct_kernel, steps),
                 [tops, ride_shape, shape(corners, width), tops, shape(order, loads)] + sides,
-            )(counts, terms, squares, res_top, dir_top, flex_block, flex_base)
+            )(squares, res_top, counts, dir_top, flex_block, flex_base, *terms)
         if iteration > 0:
             norms.append(rider_values(earlier, loads))
     norms.append(to_all(told, ALL).sum(axis=0)[0, :loads])

time: 193 us -> 206 us (1.067)
  blocking collectives: 31.3 us -> 0 us
  starting transfers between devices: 53.1 us -> 78.1 us
  waiting for transfers between devices: 66.4 us -> 79.9 us
  local copies, waits for them, and re-layouts: 14 us -> 20 us
    all_to_all x2 -> x0, blocking collectives: 31.3 us -> none  [to_all(): return lax.all_to_all(copies, axes, split_axis=0, concat_axis=0, tiled=True)]
    ppermute x26 -> x44, starting transfers between devices: 19.4 us -> 45.6 us  [turned(): lax.ppermute(array, axes, [(i, (i + by) % count) for i in range(count)])]
    ppermute x26 -> x44, waiting for transfers between devices: 20.6 us -> 44.6 us  [turned(): lax.ppermute(array, axes, [(i, (i + by) % count) for i in range(count)])]
    all_to_all x4 -> x3, waiting for transfers between devices: 25.9 us -> 16.4 us  [to_all(): return lax.all_to_all(copies, axes, split_axis=0, concat_axis=0, tiled=True)]
    unnamed x32 -> x46, local copies, waits for them, and re-layouts: 13.1 us -> 17.3 us
    pallas_call x19 -> x22, Pallas kernels: 22.5 us -> 21.2 us  [run(): pl.pallas_call(body, out_shape=outs, in_specs=[vm() for _ in operands], o...]
    all_to_all x4 -> x3, starting transfers between devices: 21.2 us -> 20.4 us  [to_all(): return lax.all_to_all(copies, axes, split_axis=0, concat_axis=0, tiled=True)]
  transfers between devices with their start and end apart: 42 -> 59, of which waited for: 21 -> 27; matrix products, arithmetic and copies ran while one was open for 2% -> 3% of each run, Pallas kernels for 7% -> 6%
where the time goes in v4:
time: 206 us; the launch traced here: 204 us
  waiting for transfers between devices  79.9 us (39%)
  starting transfers between devices  78.1 us (38%)
  Pallas kernels  21.2 us (10%)
  local copies, waits for them, and re-layouts  20 us (10%)
  other arithmetic  3.85 us (2%)
    ppermute x44, starting transfers between devices, turned(): lax.ppermute(array, axes, [(i, (i + by) % count) for i in range(count)])  45.6 us
    ppermute x44, waiting for transfers between devices, turned(): lax.ppermute(array, axes, [(i, (i + by) % count) for i in range(count)])  44.6 us
    pallas_call x22, Pallas kernels, run(): pl.pallas_call(body, out_shape=outs, in_specs=[vm() for _ in operands], o...  21.2 us
    all_to_all x3, starting transfers between devices, to_all(): return lax.all_to_all(copies, axes, split_axis=0, concat_axis=0, tiled=True)  20.4 us
    ppermute x12, waiting for transfers between devices, swapped(): return lax.ppermute(array, axes, pairs)  19 us
    unnamed x46, local copies, waits for them, and re-layouts  17.3 us
    all_to_all x3, waiting for transfers between devices, to_all(): return lax.all_to_all(copies, axes, split_axis=0, concat_axis=0, tiled=True)  16.4 us
    ppermute x12, starting transfers between devices, swapped(): return lax.ppermute(array, axes, pairs)  12.1 us
  transfers between devices with their start and end apart: 59, of which 27 were waited for; matrix products, arithmetic and copies ran while one was open for 3% of the time, Pallas kernels for 6%

profile of v4, /device:TPU:0, one launch (start us, length us, event | category | flops | bytes accessed | tf_op | source)
XLA Modules:
  0.0 204.2 jit_solution(10730668233309547420)
XLA Ops:
  1.9 8.0 %all-to-all-start = ((f32[16,1,128]{2,1,0:T(1,128)}), f32[16,1,128]{2,1,0:T(1,128)S(1)}, u32[]{:S(2)}, u32[]{:S(2)}) async-start(f32[16,1,128]{2,1,0:T(1,128)} %broadcast_in_dim.14), calls=%async_computation | async-start | bytes 16384 | tf_op jit(solution)/shard_map/all_to_all | solution.py:40
  10.6 6.9 %all-to-all-done = f32[16,1,128]{2,1,0:T(1,128)S(1)} async-done(((f32[16,1,128]{2,1,0:T(1,128)}), f32[16,1,128]{2,1,0:T(1,128)S(1)}, u32[]{:S(2)}, u32[]{:S(2)}) %all-to-all-start) | async-done | bytes 8224 | tf_op jit(solution)/shard_map/all_to_all | solution.py:40
  24.0 3.1 %collective-permute-start.3 = (f32[432,128]{1,0:T(8,128)S(1)}, f32[432,128]{1,0:T(8,128)S(1)}, u32[]{:S(2)}, u32[]{:S(2)}) collective-permute-start(f32[432,128]{1,0:T(8,128)S(1)} %get-tuple-element.102), channel_id=1, source_target_pairs={{0,112},{16,32},{32,16},{48,64},{64,48},{80,96},{96,80},{112,0},{1... | collective-permute-start | bytes 663560 | tf_op jit(solution)/shard_map/ppermute | solution.py:36
  27.9 2.9 %collective-permute-start.7 = (f32[192,384]{1,0:T(8,128)S(1)}, f32[192,384]{1,0:T(8,128)S(1)}, u32[]{:S(2)}, u32[]{:S(2)}) collective-permute-start(f32[192,384]{1,0:T(8,128)S(1)} %bitcast.40), channel_id=1, source_target_pairs={{0,64},{32,96},{64,0},{96,32},{1,65},{33,97},{65,1},{97,33},{2,66}... | collective-permute-start | bytes 884744 | tf_op jit(solution)/shard_map/ppermute | solution.py:31
  35.2 4.3 %all-to-all-start.1 = ((f32[16,24,256]{2,1,0:T(8,128)}), f32[16,24,256]{2,1,0:T(8,128)S(1)}, u32[]{:S(2)}, u32[]{:S(2)}) async-start(f32[16,24,256]{2,1,0:T(8,128)} %get-tuple-element.104), calls=%async_computation.1 | async-start | bytes 786432 | tf_op jit(solution)/shard_map/all_to_all | solution.py:40
  46.6 4.3 %all-to-all-done.1.after.own.values = f32[16,24,256]{2,1,0:T(8,128)S(1)} async-done(((f32[16,24,256]{2,1,0:T(8,128)}), f32[16,24,256]{2,1,0:T(8,128)S(1)}, u32[]{:S(2)}, u32[]{:S(2)}) %all-to-all-start.1) | async-done | bytes 393248 | tf_op jit(solution)/shard_map/all_to_all | solution.py:40
  53.7 7.3 %collective-permute-done.12.refs_3_ = f32[192,384]{1,0:T(8,128)S(1)} collective-permute-done((f32[192,384]{1,0:T(8,128)S(1)}, f32[192,384]{1,0:T(8,128)S(1)}, u32[]{:S(2)}, u32[]{:S(2)}) %collective-permute-start.12) | collective-permute-done | bytes 294944 | tf_op jit(solution)/shard_map/ppermute | solution.py:31
  61.0 3.1 %collective-permute-done.11.refs_2_ = f32[192,384]{1,0:T(8,128)S(1)} collective-permute-done((f32[192,384]{1,0:T(8,128)S(1)}, f32[192,384]{1,0:T(8,128)S(1)}, u32[]{:S(2)}, u32[]{:S(2)}) %collective-permute-start.11) | collective-permute-done | bytes 294944 | tf_op jit(solution)/shard_map/ppermute | solution.py:31
  64.1 5.0 %collective-permute-done.10.refs_1_ = f32[192,384]{1,0:T(8,128)S(1)} collective-permute-done((f32[192,384]{1,0:T(8,128)S(1)}, f32[192,384]{1,0:T(8,128)S(1)}, u32[]{:S(2)}, u32[]{:S(2)}) %collective-permute-start.10) | collective-permute-done | bytes 294944 | tf_op jit(solution)/shard_map/ppermute | solution.py:31
  75.5 4.7 %collective-permute-done.13.refs_1_ = f32[4,24,256]{2,1,0:T(8,128)S(1)} collective-permute-done((f32[4,24,256]{2,1,0:T(8,128)S(1)}, f32[4,24,256]{2,1,0:T(8,128)S(1)}, u32[]{:S(2)}, u32[]{:S(2)}) %collective-permute-start.13) | collective-permute-done | bytes 98336 | tf_op jit(solution)/shard_map/ppermute | solution.py:31
  85.5 2.9 %shard_map.87 = (f32[128,176]{1,0:T(8,128)S(1)}, f32[1024,176]{1,0:T(8,128)S(1)}, f32[128,176]{1,0:T(8,128)S(1)}, f32[1024,176]{1,0:T(8,128)S(1)}, f32[1,176]{1,...) custom-call(f32[16,24,256]{2,1,0:T(8,128)S(1)} %all-to-all-done.1.after.own.values, ...), custom_call_target="tpu_custom_call" | custom-call | tf_op jit(solution)/shard_map/pallas_call | solution.py:49
  93.4 2.8 %collective-permute-start.24 = (f32[192,384]{1,0:T(8,128)S(1)}, f32[192,384]{1,0:T(8,128)S(1)}, u32[]{:S(2)}, u32[]{:S(2)}) collective-permute-start(f32[192,384]{1,0:T(8,128)S(1)} %get-tuple-element.141), channel_id=1, source_target_pairs={{0,8},{4,12},{8,0},{12,4},{1,9},{5,13},{9,1},{13,5},{2,10},{6,14},... | collective-permute-start | bytes 884744 | tf_op jit(solution)/shard_map/ppermute | solution.py:31
  96.7 5.7 %collective-permute-done.20.in_b = f32[432,128]{1,0:T(8,128)S(1)} collective-permute-done((f32[432,128]{1,0:T(8,128)S(1)}, f32[432,128]{1,0:T(8,128)S(1)}, u32[]{:S(2)}, u32[]{:S(2)}) %collective-permute-start.20) | collective-permute-done | bytes 221216 | tf_op jit(solution)/shard_map/ppermute | solution.py:36
  102.4 6.6 %collective-permute-done.22.in_y = f32[432,128]{1,0:T(8,128)S(1)} collective-permute-done((f32[432,128]{1,0:T(8,128)S(1)}, f32[432,128]{1,0:T(8,128)S(1)}, u32[]{:S(2)}, u32[]{:S(2)}) %collective-permute-start.22) | collective-permute-done | bytes 221216 | tf_op jit(solution)/shard_map/ppermute | solution.py:36
  113.6 3.0 %collective-permute-done.27.refs_2_ = f32[1,24,256]{2,1,0:T(8,128)S(1)} collective-permute-done((f32[1,24,256]{2,1,0:T(8,128)S(1)}, f32[1,24,256]{2,1,0:T(8,128)S(1)}, u32[]{:S(2)}, u32[]{:S(2)}) %collective-permute-start.27) | collective-permute-done | bytes 24608 | tf_op jit(solution)/shard_map/ppermute | solution.py:31
  121.6 5.1 %collective-permute-done.33.refs_1_ = f32[4,24,256]{2,1,0:T(8,128)S(1)} collective-permute-done((f32[4,24,256]{2,1,0:T(8,128)S(1)}, f32[4,24,256]{2,1,0:T(8,128)S(1)}, u32[]{:S(2)}, u32[]{:S(2)}) %collective-permute-start.33) | collective-permute-done | bytes 98336 | tf_op jit(solution)/shard_map/ppermute | solution.py:31
  127.4 6.3 %collective-permute-start.36 = (f32[24,256]{1,0:T(8,128)S(1)}, f32[24,256]{1,0:T(8,128)S(1)}, u32[]{:S(2)}, u32[]{:S(2)}) collective-permute-start(f32[24,256]{1,0:T(8,128)S(1)} %get-tuple-element.155), channel_id=1, source_target_pairs={{0,4},{4,8},{8,12},{12,0},{1,5},{5,9},{9,13},{13,1},{2,6},{6,10},{... | collective-permute-start | bytes 73736 | tf_op jit(solution)/shard_map/ppermute | solution.py:31
  133.7 2.8 %collective-permute-start.38 = (f32[24,256]{1,0:T(8,128)S(1)}, f32[24,256]{1,0:T(8,128)S(1)}, u32[]{:S(2)}, u32[]{:S(2)}) collective-permute-start(f32[24,256]{1,0:T(8,128)S(1)} %get-tuple-element.157), channel_id=1, source_target_pairs={{0,12},{4,0},{8,4},{12,8},{1,13},{5,1},{9,5},{13,9},{2,14},{6,2},{... | collective-permute-start | bytes 73736 | tf_op jit(solution)/shard_map/ppermute | solution.py:31
  136.4 3.0 %shard_map.95 = (f32[128,176]{1,0:T(8,128)S(1)}, f32[1024,176]{1,0:T(8,128)S(1)}, f32[128,176]{1,0:T(8,128)S(1)}, f32[1024,176]{1,0:T(8,128)S(1)}, f32[1,176]{1,...) custom-call(bf16[1152,176]{1,0:T(8,128)(2,1)S(1)} %get-tuple-element.130.balanced, ...), custom_call_target="tpu_custom_call" | custom-call | tf_op jit(solution)/shard_map/pallas_call | solution.py:49
  141.1 2.9 %collective-permute-start.40 = (f32[432,128]{1,0:T(8,128)S(1)}, f32[432,128]{1,0:T(8,128)S(1)}, u32[]{:S(2)}, u32[]{:S(2)}) collective-permute-start(f32[432,128]{1,0:T(8,128)S(1)} %get-tuple-element.160), channel_id=1, source_target_pairs={{0,15},{1,2},{2,1},{3,4},{4,3},{5,6},{6,5},{7,8},{8,7},{9,10},{10,... | collective-permute-start | bytes 663560 | tf_op jit(solution)/shard_map/ppermute | solution.py:36
  147.3 3.3 %collective-permute-done.40.in_b = f32[432,128]{1,0:T(8,128)S(1)} collective-permute-done((f32[432,128]{1,0:T(8,128)S(1)}, f32[432,128]{1,0:T(8,128)S(1)}, u32[]{:S(2)}, u32[]{:S(2)}) %collective-permute-start.40) | collective-permute-done | bytes 221216 | tf_op jit(solution)/shard_map/ppermute | solution.py:36
  163.1 4.6 %collective-permute-done.50.refs_1_ = f32[4,24,256]{2,1,0:T(8,128)S(1)} collective-permute-done((f32[4,24,256]{2,1,0:T(8,128)S(1)}, f32[4,24,256]{2,1,0:T(8,128)S(1)}, u32[]{:S(2)}, u32[]{:S(2)}) %collective-permute-start.50) | collective-permute-done | bytes 98336 | tf_op jit(solution)/shard_map/ppermute | solution.py:31
  185.7 8.2 %all-to-all-start.2 = ((f32[128,1,256]{2,1,0:T(1,128)}), f32[128,1,256]{2,1,0:T(1,128)S(1)}, u32[]{:S(2)}, u32[]{:S(2)}) async-start(f32[128,1,256]{2,1,0:T(1,128)} %get-tuple-element.190), calls=%async_computation.2 | async-start | bytes 262144 | tf_op jit(solution)/shard_map/all_to_all | solution.py:40
  198.2 5.2 %all-to-all-done.2 = f32[128,1,256]{2,1,0:T(1,128)S(1)} async-done(((f32[128,1,256]{2,1,0:T(1,128)}), f32[128,1,256]{2,1,0:T(1,128)S(1)}, u32[]{:S(2)}, u32[]{:S(2)}) %all-to-all-start.2) | async-done | bytes 131104 | tf_op jit(solution)/shard_map/all_to_all | solution.py:40
  (174 shorter events, 91.3 us)
Async XLA Ops:
  1.9 15.5 %all-to-all-start = ((f32[16,1,128]{2,1,0:T(1,128)}), f32[16,1,128]{2,1,0:T(1,128)S(1)}, u32[]{:S(2)}, u32[]{:S(2)}) async-start(f32[16,1,128]{2,1,0:T(1,128)} %broadcast_in_dim.14), calls=%async_computation | async-start | bytes 16384 | tf_op jit(solution)/shard_map/all_to_all | solution.py:40
  22.2 9.3 %collective-permute-start.1 = (f32[432,128]{1,0:T(8,128)S(1)}, f32[432,128]{1,0:T(8,128)S(1)}, u32[]{:S(2)}, u32[]{:S(2)}) collective-permute-start(f32[432,128]{1,0:T(8,128)S(1)} %get-tuple-element.100), channel_id=1, source_target_pairs={{0,15},{1,2},{2,1},{3,4},{4,3},{5,6},{6,5},{7,8},{8,7},{9,10},{10,... | collective-permute-start | bytes 663560 | tf_op jit(solution)/shard_map/ppermute | solution.py:36
  24.0 9.0 %collective-permute-start.2 = (f32[432,128]{1,0:T(8,128)S(1)}, f32[432,128]{1,0:T(8,128)S(1)}, u32[]{:S(2)}, u32[]{:S(2)}) collective-permute-start(f32[432,128]{1,0:T(8,128)S(1)} %get-tuple-element.101), channel_id=1, source_target_pairs={{0,16},{16,0},{32,48},{48,32},{64,80},{80,64},{96,112},{112,96},{1... | collective-permute-start | bytes 663560 | tf_op jit(solution)/shard_map/ppermute | solution.py:36
  24.0 9.0 %collective-permute-start.3 = (f32[432,128]{1,0:T(8,128)S(1)}, f32[432,128]{1,0:T(8,128)S(1)}, u32[]{:S(2)}, u32[]{:S(2)}) collective-permute-start(f32[432,128]{1,0:T(8,128)S(1)} %get-tuple-element.102), channel_id=1, source_target_pairs={{0,112},{16,32},{32,16},{48,64},{64,48},{80,96},{96,80},{112,0},{1... | collective-permute-start | bytes 663560 | tf_op jit(solution)/shard_map/ppermute | solution.py:36
  27.1 16.3 %collective-permute-start.8 = (f32[192,384]{1,0:T(8,128)S(1)}, f32[192,384]{1,0:T(8,128)S(1)}, u32[]{:S(2)}, u32[]{:S(2)}) collective-permute-start(f32[192,384]{1,0:T(8,128)S(1)} %bitcast.39), channel_id=1, source_target_pairs={{0,96},{32,0},{64,32},{96,64},{1,97},{33,1},{65,33},{97,65},{2,98}... | collective-permute-start | bytes 884744 | tf_op jit(solution)/shard_map/ppermute | solution.py:31
  27.9 15.6 %collective-permute-start.7 = (f32[192,384]{1,0:T(8,128)S(1)}, f32[192,384]{1,0:T(8,128)S(1)}, u32[]{:S(2)}, u32[]{:S(2)}) collective-permute-start(f32[192,384]{1,0:T(8,128)S(1)} %bitcast.40), channel_id=1, source_target_pairs={{0,64},{32,96},{64,0},{96,32},{1,65},{33,97},{65,1},{97,33},{2,66}... | collective-permute-start | bytes 884744 | tf_op jit(solution)/shard_map/ppermute | solution.py:31
  31.4 13.0 %collective-permute-start.6 = (f32[192,384]{1,0:T(8,128)S(1)}, f32[192,384]{1,0:T(8,128)S(1)}, u32[]{:S(2)}, u32[]{:S(2)}) collective-permute-start(f32[192,384]{1,0:T(8,128)S(1)} %bitcast.41), channel_id=1, source_target_pairs={{0,32},{32,64},{64,96},{96,0},{1,33},{33,65},{65,97},{97,1},{2,34}... | collective-permute-start | bytes 884744 | tf_op jit(solution)/shard_map/ppermute | solution.py:31
  35.2 15.7 %all-to-all-start.1 = ((f32[16,24,256]{2,1,0:T(8,128)}), f32[16,24,256]{2,1,0:T(8,128)S(1)}, u32[]{:S(2)}, u32[]{:S(2)}) async-start(f32[16,24,256]{2,1,0:T(8,128)} %get-tuple-element.104), calls=%async_computation.1 | async-start | bytes 786432 | tf_op jit(solution)/shard_map/all_to_all | solution.py:40
  50.9 18.3 %collective-permute-start.4 = (f32[16,24,256]{2,1,0:T(8,128)S(1)}, f32[16,24,256]{2,1,0:T(8,128)S(1)}, u32[]{:S(2)}, u32[]{:S(2)}) collective-permute-start(f32[16,24,256]{2,1,0:T(8,128)S(1)} %all-to-all-done.1.after.own.values), channel_id=1, source_target_pairs={{0,16},{16,0},{1,17},{17,1},{2,18},{18,2},{3,19},{19,3},{4,20},{20... | collective-permute-start | bytes 1179656 | tf_op jit(solution)/shard_map/ppermute | solution.py:31
  51.0 9.9 %collective-permute-start.12 = (f32[192,384]{1,0:T(8,128)S(1)}, f32[192,384]{1,0:T(8,128)S(1)}, u32[]{:S(2)}, u32[]{:S(2)}) collective-permute-start(f32[192,384]{1,0:T(8,128)S(1)} %add.5.refs_0_), channel_id=1, source_target_pairs={{0,3},{1,0},{2,1},{3,2},{4,7},{5,4},{6,5},{7,6},{8,11},{9,8},{10,9... | collective-permute-start | bytes 884744 | tf_op jit(solution)/shard_map/ppermute | solution.py:31
  52.7 11.4 %collective-permute-start.11 = (f32[192,384]{1,0:T(8,128)S(1)}, f32[192,384]{1,0:T(8,128)S(1)}, u32[]{:S(2)}, u32[]{:S(2)}) collective-permute-start(f32[192,384]{1,0:T(8,128)S(1)} %add.5.refs_0_), channel_id=1, source_target_pairs={{0,2},{1,3},{2,0},{3,1},{4,6},{5,7},{6,4},{7,5},{8,10},{9,11},{10,... | collective-permute-start | bytes 884744 | tf_op jit(solution)/shard_map/ppermute | solution.py:31
  52.7 16.4 %collective-permute-start.10 = (f32[192,384]{1,0:T(8,128)S(1)}, f32[192,384]{1,0:T(8,128)S(1)}, u32[]{:S(2)}, u32[]{:S(2)}) collective-permute-start(f32[192,384]{1,0:T(8,128)S(1)} %add.5.refs_0_), channel_id=1, source_target_pairs={{0,1},{1,2},{2,3},{3,0},{4,5},{5,6},{6,7},{7,4},{8,9},{9,10},{10,1... | collective-permute-start | bytes 884744 | tf_op jit(solution)/shard_map/ppermute | solution.py:31
  90.0 12.4 %collective-permute-start.20 = (f32[432,128]{1,0:T(8,128)S(1)}, f32[432,128]{1,0:T(8,128)S(1)}, u32[]{:S(2)}, u32[]{:S(2)}) collective-permute-start(f32[432,128]{1,0:T(8,128)S(1)} %get-tuple-element.126), channel_id=1, source_target_pairs={{0,15},{1,2},{2,1},{3,4},{4,3},{5,6},{6,5},{7,8},{8,7},{9,10},{10,... | collective-permute-start | bytes 663560 | tf_op jit(solution)/shard_map/ppermute | solution.py:36
  92.6 18.6 %collective-permute-start.23 = (f32[192,384]{1,0:T(8,128)S(1)}, f32[192,384]{1,0:T(8,128)S(1)}, u32[]{:S(2)}, u32[]{:S(2)}) collective-permute-start(f32[192,384]{1,0:T(8,128)S(1)} %get-tuple-element.140), channel_id=1, source_target_pairs={{0,4},{4,8},{8,12},{12,0},{1,5},{5,9},{9,13},{13,1},{2,6},{6,10},{... | collective-permute-start | bytes 884744 | tf_op jit(solution)/shard_map/ppermute | solution.py:31
  93.4 18.8 %collective-permute-start.24 = (f32[192,384]{1,0:T(8,128)S(1)}, f32[192,384]{1,0:T(8,128)S(1)}, u32[]{:S(2)}, u32[]{:S(2)}) collective-permute-start(f32[192,384]{1,0:T(8,128)S(1)} %get-tuple-element.141), channel_id=1, source_target_pairs={{0,8},{4,12},{8,0},{12,4},{1,9},{5,13},{9,1},{13,5},{2,10},{6,14},... | collective-permute-start | bytes 884744 | tf_op jit(solution)/shard_map/ppermute | solution.py:31
  96.1 21.0 %collective-permute-start.25 = (f32[192,384]{1,0:T(8,128)S(1)}, f32[192,384]{1,0:T(8,128)S(1)}, u32[]{:S(2)}, u32[]{:S(2)}) collective-permute-start(f32[192,384]{1,0:T(8,128)S(1)} %get-tuple-element.142), channel_id=1, source_target_pairs={{0,12},{4,0},{8,4},{12,8},{1,13},{5,1},{9,5},{13,9},{2,14},{6,2},{... | collective-permute-start | bytes 884744 | tf_op jit(solution)/shard_map/ppermute | solution.py:31
  118.3 8.4 %collective-permute-start.33 = (f32[4,24,256]{2,1,0:T(8,128)S(1)}, f32[4,24,256]{2,1,0:T(8,128)S(1)}, u32[]{:S(2)}, u32[]{:S(2)}) collective-permute-start(f32[4,24,256]{2,1,0:T(8,128)S(1)} %get-tuple-element.151), channel_id=1, source_target_pairs={{0,1},{1,2},{2,3},{3,0},{4,5},{5,6},{6,7},{7,4},{8,9},{9,10},{10,1... | collective-permute-start | bytes 294920 | tf_op jit(solution)/shard_map/ppermute | solution.py:31
  118.4 8.4 %collective-permute-start.34 = (f32[4,24,256]{2,1,0:T(8,128)S(1)}, f32[4,24,256]{2,1,0:T(8,128)S(1)}, u32[]{:S(2)}, u32[]{:S(2)}) collective-permute-start(f32[4,24,256]{2,1,0:T(8,128)S(1)} %get-tuple-element.152), channel_id=1, source_target_pairs={{0,2},{1,3},{2,0},{3,1},{4,6},{5,7},{6,4},{7,5},{8,10},{9,11},{10,... | collective-permute-start | bytes 294920 | tf_op jit(solution)/shard_map/ppermute | solution.py:31
  127.4 12.1 %collective-permute-start.36 = (f32[24,256]{1,0:T(8,128)S(1)}, f32[24,256]{1,0:T(8,128)S(1)}, u32[]{:S(2)}, u32[]{:S(2)}) collective-permute-start(f32[24,256]{1,0:T(8,128)S(1)} %get-tuple-element.155), channel_id=1, source_target_pairs={{0,4},{4,8},{8,12},{12,0},{1,5},{5,9},{9,13},{13,1},{2,6},{6,10},{... | collective-permute-start | bytes 73736 | tf_op jit(solution)/shard_map/ppermute | solution.py:31
  141.1 9.6 %collective-permute-start.40 = (f32[432,128]{1,0:T(8,128)S(1)}, f32[432,128]{1,0:T(8,128)S(1)}, u32[]{:S(2)}, u32[]{:S(2)}) collective-permute-start(f32[432,128]{1,0:T(8,128)S(1)} %get-tuple-element.160), channel_id=1, source_target_pairs={{0,15},{1,2},{2,1},{3,4},{4,3},{5,6},{6,5},{7,8},{8,7},{9,10},{10,... | collective-permute-start | bytes 663560 | tf_op jit(solution)/shard_map/ppermute | solution.py:36
  169.0 15.2 %collective-permute-start.53 = (f32[24,256]{1,0:T(8,128)}, f32[24,256]{1,0:T(8,128)S(1)}, u32[]{:S(2)}, u32[]{:S(2)}) collective-permute-start(f32[24,256]{1,0:T(8,128)} %get-tuple-element.183), channel_id=1, source_target_pairs={{0,4},{4,8},{8,12},{12,0},{1,5},{5,9},{9,13},{13,1},{2,6},{6,10},{... | collective-permute-start | bytes 73736 | tf_op jit(solution)/shard_map/ppermute | solution.py:31
  169.5 14.7 %collective-permute-start.54 = (f32[24,256]{1,0:T(8,128)}, f32[24,256]{1,0:T(8,128)}, u32[]{:S(2)}, u32[]{:S(2)}) collective-permute-start(f32[24,256]{1,0:T(8,128)} %get-tuple-element.184), channel_id=1, source_target_pairs={{0,8},{4,12},{8,0},{12,4},{1,9},{5,13},{9,1},{13,5},{2,10},{6,14},... | collective-permute-start | bytes 73736 | tf_op jit(solution)/shard_map/ppermute | solution.py:31
  172.0 12.2 %collective-permute-start.55 = (f32[24,256]{1,0:T(8,128)}, f32[24,256]{1,0:T(8,128)}, u32[]{:S(2)}, u32[]{:S(2)}) collective-permute-start(f32[24,256]{1,0:T(8,128)} %get-tuple-element.185), channel_id=1, source_target_pairs={{0,12},{4,0},{8,4},{12,8},{1,13},{5,1},{9,5},{13,9},{2,14},{6,2},{... | collective-permute-start | bytes 73736 | tf_op jit(solution)/shard_map/ppermute | solution.py:31
  185.7 17.7 %all-to-all-start.2 = ((f32[128,1,256]{2,1,0:T(1,128)}), f32[128,1,256]{2,1,0:T(1,128)S(1)}, u32[]{:S(2)}, u32[]{:S(2)}) async-start(f32[128,1,256]{2,1,0:T(1,128)} %get-tuple-element.190), calls=%async_computation.2 | async-start | bytes 262144 | tf_op jit(solution)/shard_map/all_to_all | solution.py:40
  (57 other events, 301.4 us)

commit v5 on v3

--- a/solution.py
+++ b/solution.py
@@ -44,16 +44,19 @@
     return pl.BlockSpec(memory_space=pltpu.VMEM)
 
 
-def call(body, outs, scratch=()):
+def call(body, outs, scratch=(), unread=()):
     def run(*operands):
         return pl.pallas_call(
             body,
             out_shape=outs,
-            in_specs=[vm() for _ in operands],
+            in_specs=[vm() for _ in operands] + [pl.BlockSpec(memory_space=pltpu.HBM) for _ in unread],
             out_specs=[vm() for _ in outs],
             scratch_shapes=scratch,
             compiler_params=pltpu.CompilerParams(vmem_limit_bytes=VMEM_BYTES),
-        )(*[pltpu.with_memory_space_constraint(o, pltpu.VMEM) for o in operands])
+        )(
+            *[pltpu.with_memory_space_constraint(o, pltpu.VMEM) for o in operands],
+            *[pltpu.with_memory_space_constraint(o, pltpu.HBM) for o in unread],
+        )
 
     return run
 
@@ -142,11 +145,18 @@
     return (1 - odd_b, odd_b, 3 - odd_a, 2 + odd_a)
 
 
-def first_kernel(after, ids, live, right, flex, flexed, extra, counts, *sends):
+def ids_kernel(ids, side_rows, right, flex, told, line, counts):
+    line[...] = jnp.zeros_like(line)
+    line[:, 0 : ids.shape[1]] = ids[...].astype(F32)
+    told[...] = jnp.broadcast_to(line[...][None], told.shape)
+    live = side_rows[...].astype(F32)
+    which = lax.broadcasted_iota(jnp.int32, counts.shape, 0)
+    counts[...] = jnp.where(which == 0, live[:, 0:1], live[:, 1:2])
+
+
+def first_kernel(after, ids, counts, right, flex, flexed, extra, *sends):
     direction = (right[...] / cheb_center).astype(BF16)
     flexed[...] = dot(flex[...], direction, ((1,), (1,)))
-    counts[0:1, :] = jnp.broadcast_to(live[0:1, 0:1], (1, LANES))
-    counts[1:2, :] = jnp.broadcast_to(live[0:1, 1:2], (1, LANES))
     send_sides(counts, flexed, *sends)
     column = jnp.broadcast_to(ids[...], (LANES, LANES)).T
     extra[...] = jnp.zeros_like(extra)
@@ -205,10 +215,12 @@
         told[k] = told[0]
 
 
-def step_on(steps, flex, dir_low, low, new_dir_low, flex_base):
+def step_on(steps, flex, dir_low, low, new_dir_low, flex_base, rounded):
     new_dir = steps[0] * dir_low + steps[1] * low
     new_dir_low[...] = new_dir
-    flex_base[...] = dot(flex[:, TOP:], new_dir.astype(BF16))
+    rounded[0:TOP, :] = jnp.zeros((TOP, rounded.shape[1]), BF16)
+    rounded[TOP:, :] = new_dir.astype(BF16)
+    flex_base[...] = dot(flex[...], rounded[...])
 
 
 def first_bulk_kernel(steps, after, balanced, stiff, flex, right, *outs):
@@ -287,7 +299,8 @@
 def correction_of(terms, squares, res_top, new_res_top, earlier):
     corners = terms.shape[1]
     total = tree_sum([terms[k] for k in range(terms.shape[0])])
-    earlier[...] = total[0:TILE, :]
+    if earlier is not None:
+        earlier[...] = total[0:TILE, :]
     new_res_top[...] = res_top[...]
     new_res_top[:corners, :] = res_top[:corners, :] - total[:, : res_top.shape[1]]
     top = new_res_top[...]
@@ -300,13 +313,14 @@
     told[...] = jnp.broadcast_to(padded[None], told.shape)
 
 
-def correct_kernel(steps, counts, terms, squares, res_top, dir_top, flex, flex_base, *outs):
-    new_res_top, earlier, extra, new_dir_top, flexed = outs[:5]
+def correct_kernel(steps, first, counts, terms, squares, res_top, dir_top, flex, flex_base, *outs):
+    earlier, outs = (None, outs) if first else (outs[0], outs[1:])
+    new_res_top, extra, new_dir_top, flexed = outs[:4]
     top, norm = correction_of(terms, squares, res_top, new_res_top, earlier)
     new_dir = steps[0] * dir_top[...] + steps[1] * top
     new_dir_top[...] = new_dir
     flexed[...] = flex_base[...] + dot(flex[:, :TOP], new_dir.astype(BF16))
-    send_sides(counts, flexed, *outs[5:])
+    send_sides(counts, flexed, *outs[4:])
     loads, width = norm.shape[1], extra.shape[1]
     spare = width - loads
     padded = jnp.concatenate([norm, jnp.zeros((1, spare), F32)], axis=1)
@@ -341,14 +355,15 @@
     for k in range(1, NY):
         inv_blocks.append(turned(inv_t, "y", NY, k))
 
-    ids_line = jnp.pad(corner_map[0, 0].astype(F32), (0, LANES - corners))[None]
-    own_ids = jnp.broadcast_to(ids_line[None], (N_GY, 1, LANES))
+    own_ids, ids_line, counts = call(
+        ids_kernel, [shape(N_GY, 1, LANES), shape(1, LANES), shape(TILE, LANES)], unread=(right, flex_block)
+    )(corner_map[0], side_rows[0])
     own_ids = to_all(own_ids, GY).reshape(N_GY, LANES)
 
     sides = [shape(side + side // 2, LANES)] * SIDES
-    flexed, extra, counts, *sends = call(
-        first_kernel, [shape(order, loads), shape(corners, width), shape(TILE, LANES)] + sides
-    )(own_ids, ids_line, side_rows[0].astype(F32), right, flex_block)
+    flexed, extra, *sends = call(
+        first_kernel, [shape(order, loads), shape(corners, width)] + sides
+    )(own_ids, ids_line, counts, right, flex_block)
 
     other_ids = turned(own_ids, "c", NC, 1)
     own_rows, other_rows = call(
@@ -392,6 +407,7 @@
         outs = call(
             functools.partial(kernel, steps),
             [tops, lows, tops, lows, shape(1, loads)] + ([] if last else [lows, shape(order, loads)]),
+            scratch=[] if last else [pltpu.VMEM((order, loads), BF16)],
         )(*order_after, balanced, stiff_block, flex_block, *state)
         res_top, res_low, sol_top, sol_low, squares = outs[:5]
         if iteration == 0:
@@ -426,10 +442,15 @@
             )(terms, squares, res_top)
         else:
             dir_low, flex_base = outs[5:]
-            res_top, earlier, extra, dir_top, flexed, *sends = call(
-                functools.partial(correct_kernel, steps),
-                [tops, ride_shape, shape(corners, width), tops, shape(order, loads)] + sides,
+            outs = call(
+                functools.partial(correct_kernel, steps, iteration == 0),
+                ([ride_shape] if iteration > 0 else [])
+                + [tops, shape(corners, width), tops, shape(order, loads)]
+                + sides,
             )(counts, terms, squares, res_top, dir_top, flex_block, flex_base)
+            if iteration > 0:
+                earlier, *outs = outs
+            res_top, extra, dir_top, flexed, *sends = outs
         if iteration > 0:
             norms.append(rider_values(earlier, loads))
     norms.append(to_all(told, ALL).sum(axis=0)[0, :loads])

time: 193 us -> 195 us (1.010)
  blocking collectives: 31.3 us -> 49 us
  waiting for transfers between devices: 66.4 us -> 58.1 us
  starting transfers between devices: 53.1 us -> 46.1 us
  local copies, waits for them, and re-layouts: 14 us -> 11.4 us
  Pallas kernels: 22.5 us -> 24.7 us
    all_to_all x2 -> x3, blocking collectives: 31.3 us -> 49 us  [to_all(): return lax.all_to_all(copies, axes, split_axis=0, concat_axis=0, tiled=True)]
    all_to_all x4 -> x3, waiting for transfers between devices: 25.9 us -> 16.8 us  [to_all(): return lax.all_to_all(copies, axes, split_axis=0, concat_axis=0, tiled=True)]
    all_to_all x4 -> x3, starting transfers between devices: 21.2 us -> 12.9 us  [to_all(): return lax.all_to_all(copies, axes, split_axis=0, concat_axis=0, tiled=True)]
    pallas_call x19 -> x20, Pallas kernels: 22.5 us -> 24.7 us  [run(): pl.pallas_call(body, out_shape=outs, in_specs=[vm() for _ in operands] +...]
    unnamed x32, local copies, waits for them, and re-layouts: 13.1 us -> 11.1 us
    ppermute x26, starting transfers between devices: 19.4 us -> 21.4 us  [turned(): lax.ppermute(array, axes, [(i, (i + by) % count) for i in range(count)])]
  transfers between devices with their start and end apart: 42 -> 41, of which waited for: 21 -> 20; matrix products, arithmetic and copies ran while one was open for 2% -> 3% of each run, Pallas kernels for 7% -> 8%
where the time goes in v5:
time: 195 us; the launch traced here: 193 us
  waiting for transfers between devices  58.1 us (30%)
  blocking collectives  49 us (25%)
  starting transfers between devices  46.1 us (24%)
  Pallas kernels  24.7 us (13%)
  local copies, waits for them, and re-layouts  11.4 us (6%)
  other arithmetic  3.08 us (2%)
    all_to_all x3, blocking collectives, to_all(): return lax.all_to_all(copies, axes, split_axis=0, concat_axis=0, tiled=True)  49 us
    pallas_call x20, Pallas kernels, run(): pl.pallas_call(body, out_shape=outs, in_specs=[vm() for _ in operands] +...  24.7 us
    ppermute x26, starting transfers between devices, turned(): lax.ppermute(array, axes, [(i, (i + by) % count) for i in range(count)])  21.4 us
    ppermute x26, waiting for transfers between devices, turned(): lax.ppermute(array, axes, [(i, (i + by) % count) for i in range(count)])  20.7 us
    ppermute x12, waiting for transfers between devices, swapped(): return lax.ppermute(array, axes, pairs)  20.5 us
    all_to_all x3, waiting for transfers between devices, to_all(): return lax.all_to_all(copies, axes, split_axis=0, concat_axis=0, tiled=True)  16.8 us
    all_to_all x3, starting transfers between devices, to_all(): return lax.all_to_all(copies, axes, split_axis=0, concat_axis=0, tiled=True)  12.9 us
    ppermute x12, starting transfers between devices, swapped(): return lax.ppermute(array, axes, pairs)  11.8 us
  transfers between devices with their start and end apart: 41, of which 20 were waited for; matrix products, arithmetic and copies ran while one was open for 3% of the time, Pallas kernels for 8%

profile of v5, /device:TPU:0, one launch (start us, length us, event | category | flops | bytes accessed | tf_op | source)
XLA Modules:
  0.0 193.3 jit_solution(18037913160913673189)
XLA Ops:
  2.0 15.6 %all_to_all.30 = f32[16,1,128]{2,1,0:T(1,128)S(1)} all-to-all(f32[16,1,128]{2,1,0:T(1,128)S(1)} %get-tuple-element.76), channel_id=1, replica_groups=mesh['y'=4,'c'=2,'x'=4,'z'=4] {'x','z'}, dimensions={0} | all-to-all | bytes 16384 | tf_op jit(solution)/shard_map/all_to_all | solution.py:40
  21.3 3.1 %collective-permute-start.3 = (f32[432,128]{1,0:T(8,128)S(1)}, f32[432,128]{1,0:T(8,128)S(1)}, u32[]{:S(2)}, u32[]{:S(2)}) collective-permute-start(f32[432,128]{1,0:T(8,128)S(1)} %get-tuple-element.82), channel_id=1, source_target_pairs={{0,112},{16,32},{32,16},{48,64},{64,48},{80,96},{96,80},{112,0},{1... | collective-permute-start | bytes 663560 | tf_op jit(solution)/shard_map/ppermute | solution.py:36
  25.2 2.9 %collective-permute-start.7 = (f32[192,384]{1,0:T(8,128)}, f32[192,384]{1,0:T(8,128)}, u32[]{:S(2)}, u32[]{:S(2)}) collective-permute-start(f32[192,384]{1,0:T(8,128)} %bitcast.6.refs_0_), channel_id=1, source_target_pairs={{0,64},{32,96},{64,0},{96,32},{1,65},{33,97},{65,1},{97,33},{2,66}... | collective-permute-start | bytes 884744 | tf_op jit(solution)/shard_map/ppermute | solution.py:31
  32.6 4.3 %all-to-all-start.1 = ((f32[16,24,256]{2,1,0:T(8,128)}), f32[16,24,256]{2,1,0:T(8,128)}, u32[]{:S(2)}, u32[]{:S(2)}) async-start(f32[16,24,256]{2,1,0:T(8,128)} %copy-done.11), calls=%async_computation.1 | async-start | bytes 786432 | tf_op jit(solution)/shard_map/all_to_all | solution.py:40
  41.9 4.0 %shard_map.89 = (f32[192,384]{1,0:T(8,128)S(1)}, f32[192,384]{1,0:T(8,128)}) custom-call(f32[16,128]{1,0:T(8,128)S(1)} %bitcast.39, f32[16,128]{1,0:T(8,128)S(1)} %collective-permute-done.5.ids_other, f32[192,384]{1,0:T(8,128)} %bitcast.6.refs_0_, f32[192,384]{1,0:T(8,128)} %collective-permute-done.6.refs_1_, f32[192,384]{1,0:T(8,128)} %collective-permute-done.7.refs_2_, ...), custom_call_target="tpu_custom_call" | custom-call | tf_op jit(solution)/shard_map/pallas_call | solution.py:49
  54.7 4.2 %shard_map.88 = (f32[128,176]{1,0:T(8,128)S(1)}, f32[1024,176]{1,0:T(8,128)S(1)}, f32[128,176]{1,0:T(8,128)S(1)}, f32[1024,176]{1,0:T(8,128)S(1)}, f32[1,176]{1,...) custom-call(f32[16,24,256]{2,1,0:T(8,128)} %all-to-all-done.1.after.own.values, ...), custom_call_target="tpu_custom_call" | custom-call | tf_op jit(solution)/shard_map/pallas_call | solution.py:49
  59.6 3.1 %collective-permute-done.11.refs_2_ = f32[192,384]{1,0:T(8,128)S(1)} collective-permute-done((f32[192,384]{1,0:T(8,128)S(1)}, f32[192,384]{1,0:T(8,128)S(1)}, u32[]{:S(2)}, u32[]{:S(2)}) %collective-permute-start.11) | collective-permute-done | bytes 294944 | tf_op jit(solution)/shard_map/ppermute | solution.py:31
  62.7 5.1 %collective-permute-done.10.refs_1_ = f32[192,384]{1,0:T(8,128)S(1)} collective-permute-done((f32[192,384]{1,0:T(8,128)S(1)}, f32[192,384]{1,0:T(8,128)S(1)}, u32[]{:S(2)}, u32[]{:S(2)}) %collective-permute-start.10) | collective-permute-done | bytes 294944 | tf_op jit(solution)/shard_map/ppermute | solution.py:31
  67.8 3.1 %shard_map.90 = (bf16[384,384]{1,0:T(8,128)(2,1)S(1)}, bf16[384,384]{1,0:T(8,128)(2,1)S(1)}, bf16[384,384]{1,0:T(8,128)(2,1)S(1)}, bf16[384,384]{1,0:T(8,128)(2,...) custom-call(f32[16,24,256]{2,1,0:T(8,128)} %all-to-all-done.1.after.o, ...), custom_call_target="tpu_custom_call" | custom-call | tf_op jit(solution)/shard_map/pallas_call | solution.py:49
  72.8 15.9 %all_to_all.31.terms = f32[16,24,256]{2,1,0:T(8,128)S(1)} all-to-all(f32[16,24,256]{2,1,0:T(8,128)S(1)} %shard_map.92), channel_id=1, replica_groups=mesh['y'=4,'c'=2,'x'=4,'z'=4] {'x','z'}, dimensions={0} | all-to-all | bytes 786432 | tf_op jit(solution)/shard_map/all_to_all | solution.py:40
  95.9 6.9 %collective-permute-done.14.in_b = f32[432,128]{1,0:T(8,128)S(1)} collective-permute-done((f32[432,128]{1,0:T(8,128)S(1)}, f32[432,128]{1,0:T(8,128)S(1)}, u32[]{:S(2)}, u32[]{:S(2)}) %collective-permute-start.14) | collective-permute-done | bytes 221216 | tf_op jit(solution)/shard_map/ppermute | solution.py:36
  102.7 6.6 %collective-permute-done.16.in_y = f32[432,128]{1,0:T(8,128)S(1)} collective-permute-done((f32[432,128]{1,0:T(8,128)S(1)}, f32[432,128]{1,0:T(8,128)S(1)}, u32[]{:S(2)}, u32[]{:S(2)}) %collective-permute-start.16) | collective-permute-done | bytes 221216 | tf_op jit(solution)/shard_map/ppermute | solution.py:36
  109.9 2.6 %collective-permute-start.22 = (f32[1,24,256]{2,1,0:T(8,128)S(1)}, f32[1,24,256]{2,1,0:T(8,128)S(1)}, u32[]{:S(2)}, u32[]{:S(2)}) collective-permute-start(f32[1,24,256]{2,1,0:T(8,128)S(1)} %get-tuple-element.117.refs_0_), channel_id=1, source_target_pairs={{0,96},{32,0},{64,32},{96,64},{1,97},{33,1},{65,33},{97,65},{2,98}... | collective-permute-start | bytes 73736 | tf_op jit(solution)/shard_map/ppermute | solution.py:31
  114.0 3.8 %collective-permute-done.21.refs_2_ = f32[1,24,256]{2,1,0:T(8,128)S(1)} collective-permute-done((f32[1,24,256]{2,1,0:T(8,128)S(1)}, f32[1,24,256]{2,1,0:T(8,128)S(1)}, u32[]{:S(2)}, u32[]{:S(2)}) %collective-permute-start.21) | collective-permute-done | bytes 24608 | tf_op jit(solution)/shard_map/ppermute | solution.py:31
  118.6 3.3 %shard_map.95 = (f32[128,176]{1,0:T(8,128)S(1)}, f32[1024,176]{1,0:T(8,128)S(1)}, f32[128,176]{1,0:T(8,128)S(1)}, f32[1024,176]{1,0:T(8,128)S(1)}, f32[1,176]{1,...) custom-call(bf16[1152,176]{1,0:T(8,128)(2,1)S(1)} %get-tuple-element.102.balanced, ...), custom_call_target="tpu_custom_call" | custom-call | tf_op jit(solution)/shard_map/pallas_call | solution.py:49
  122.6 17.5 %all_to_all.32.terms = f32[16,24,256]{2,1,0:T(8,128)S(1)} all-to-all(f32[16,24,256]{2,1,0:T(8,128)S(1)} %shard_map.98), channel_id=1, replica_groups=mesh['y'=4,'c'=2,'x'=4,'z'=4] {'x','z'}, dimensions={0} | all-to-all | bytes 786432 | tf_op jit(solution)/shard_map/all_to_all | solution.py:40
  141.0 2.3 %collective-permute-start.28 = (f32[432,128]{1,0:T(8,128)S(1)}, f32[432,128]{1,0:T(8,128)S(1)}, u32[]{:S(2)}, u32[]{:S(2)}) collective-permute-start(f32[432,128]{1,0:T(8,128)S(1)} %get-tuple-element.124), channel_id=1, source_target_pairs={{0,15},{1,2},{2,1},{3,4},{4,3},{5,6},{6,5},{7,8},{8,7},{9,10},{10,... | collective-permute-start | bytes 663560 | tf_op jit(solution)/shard_map/ppermute | solution.py:36
  144.2 2.6 %collective-permute-done.27.in_a = f32[432,128]{1,0:T(8,128)S(1)} collective-permute-done((f32[432,128]{1,0:T(8,128)S(1)}, f32[432,128]{1,0:T(8,128)S(1)}, u32[]{:S(2)}, u32[]{:S(2)}) %collective-permute-start.27) | collective-permute-done | bytes 221216 | tf_op jit(solution)/shard_map/ppermute | solution.py:36
  146.8 3.8 %collective-permute-done.28.in_b = f32[432,128]{1,0:T(8,128)S(1)} collective-permute-done((f32[432,128]{1,0:T(8,128)S(1)}, f32[432,128]{1,0:T(8,128)S(1)}, u32[]{:S(2)}, u32[]{:S(2)}) %collective-permute-start.28) | collective-permute-done | bytes 221216 | tf_op jit(solution)/shard_map/ppermute | solution.py:36
  162.8 3.6 %all-to-all-start.4 = ((f32[16,24,256]{2,1,0:T(8,128)}), f32[16,24,256]{2,1,0:T(8,128)S(1)}, u32[]{:S(2)}, u32[]{:S(2)}) async-start(f32[16,24,256]{2,1,0:T(8,128)} %shard_map.103), calls=%async_computation.4 | async-start | bytes 786432 | tf_op jit(solution)/shard_map/all_to_all | solution.py:40
  167.9 9.3 %all-to-all-done.4.terms = f32[16,24,256]{2,1,0:T(8,128)S(1)} async-done(((f32[16,24,256]{2,1,0:T(8,128)}), f32[16,24,256]{2,1,0:T(8,128)S(1)}, u32[]{:S(2)}, u32[]{:S(2)}) %all-to-all-start.4) | async-done | bytes 393248 | tf_op jit(solution)/shard_map/all_to_all | solution.py:40
  178.0 5.0 %all-to-all-start.5 = ((f32[128,1,256]{2,1,0:T(1,128)}), f32[128,1,256]{2,1,0:T(1,128)S(1)}, u32[]{:S(2)}, u32[]{:S(2)}) async-start(f32[128,1,256]{2,1,0:T(1,128)} %get-tuple-element.146), calls=%async_computation.5 | async-start | bytes 262144 | tf_op jit(solution)/shard_map/all_to_all | solution.py:40
  184.1 2.5 %copy.13 = f32[1,1,176,1152]{3,2,1,0:T(8,128)} copy(f32[1,1,176,1152]{2,3,1,0:T(8,128)} %maximum_bitcast_fusion.1) | data formatting | bytes 1622016
  186.8 5.8 %all-to-all-done.5 = f32[128,1,256]{2,1,0:T(1,128)S(1)} async-done(((f32[128,1,256]{2,1,0:T(1,128)}), f32[128,1,256]{2,1,0:T(1,128)S(1)}, u32[]{:S(2)}, u32[]{:S(2)}) %all-to-all-start.5) | async-done | bytes 131104 | tf_op jit(solution)/shard_map/all_to_all | solution.py:40
  (122 shorter events, 55.8 us)
Async XLA Ops:
  19.5 9.3 %collective-permute-start.1 = (f32[432,128]{1,0:T(8,128)S(1)}, f32[432,128]{1,0:T(8,128)S(1)}, u32[]{:S(2)}, u32[]{:S(2)}) collective-permute-start(f32[432,128]{1,0:T(8,128)S(1)} %get-tuple-element.80), channel_id=1, source_target_pairs={{0,15},{1,2},{2,1},{3,4},{4,3},{5,6},{6,5},{7,8},{8,7},{9,10},{10,... | collective-permute-start | bytes 663560 | tf_op jit(solution)/shard_map/ppermute | solution.py:36
  21.3 9.0 %collective-permute-start.2 = (f32[432,128]{1,0:T(8,128)S(1)}, f32[432,128]{1,0:T(8,128)S(1)}, u32[]{:S(2)}, u32[]{:S(2)}) collective-permute-start(f32[432,128]{1,0:T(8,128)S(1)} %get-tuple-element.81), channel_id=1, source_target_pairs={{0,16},{16,0},{32,48},{48,32},{64,80},{80,64},{96,112},{112,96},{1... | collective-permute-start | bytes 663560 | tf_op jit(solution)/shard_map/ppermute | solution.py:36
  21.3 9.0 %collective-permute-start.3 = (f32[432,128]{1,0:T(8,128)S(1)}, f32[432,128]{1,0:T(8,128)S(1)}, u32[]{:S(2)}, u32[]{:S(2)}) collective-permute-start(f32[432,128]{1,0:T(8,128)S(1)} %get-tuple-element.82), channel_id=1, source_target_pairs={{0,112},{16,32},{32,16},{48,64},{64,48},{80,96},{96,80},{112,0},{1... | collective-permute-start | bytes 663560 | tf_op jit(solution)/shard_map/ppermute | solution.py:36
  24.5 16.7 %collective-permute-start.8 = (f32[192,384]{1,0:T(8,128)}, f32[192,384]{1,0:T(8,128)}, u32[]{:S(2)}, u32[]{:S(2)}) collective-permute-start(f32[192,384]{1,0:T(8,128)} %bitcast.6.refs_0_), channel_id=1, source_target_pairs={{0,96},{32,0},{64,32},{96,64},{1,97},{33,1},{65,33},{97,65},{2,98}... | collective-permute-start | bytes 884744 | tf_op jit(solution)/shard_map/ppermute | solution.py:31
  25.2 15.9 %collective-permute-start.7 = (f32[192,384]{1,0:T(8,128)}, f32[192,384]{1,0:T(8,128)}, u32[]{:S(2)}, u32[]{:S(2)}) collective-permute-start(f32[192,384]{1,0:T(8,128)} %bitcast.6.refs_0_), channel_id=1, source_target_pairs={{0,64},{32,96},{64,0},{96,32},{1,65},{33,97},{65,1},{97,33},{2,66}... | collective-permute-start | bytes 884744 | tf_op jit(solution)/shard_map/ppermute | solution.py:31
  28.8 13.1 %collective-permute-start.6 = (f32[192,384]{1,0:T(8,128)}, f32[192,384]{1,0:T(8,128)}, u32[]{:S(2)}, u32[]{:S(2)}) collective-permute-start(f32[192,384]{1,0:T(8,128)} %bitcast.6.refs_0_), channel_id=1, source_target_pairs={{0,32},{32,64},{64,96},{96,0},{1,33},{33,65},{65,97},{97,1},{2,34}... | collective-permute-start | bytes 884744 | tf_op jit(solution)/shard_map/ppermute | solution.py:31
  32.6 15.8 %all-to-all-start.1 = ((f32[16,24,256]{2,1,0:T(8,128)}), f32[16,24,256]{2,1,0:T(8,128)}, u32[]{:S(2)}, u32[]{:S(2)}) async-start(f32[16,24,256]{2,1,0:T(8,128)} %copy-done.11), calls=%async_computation.1 | async-start | bytes 786432 | tf_op jit(solution)/shard_map/all_to_all | solution.py:40
  48.3 19.4 %collective-permute-start.4 = (f32[16,24,256]{2,1,0:T(8,128)}, f32[16,24,256]{2,1,0:T(8,128)S(1)}, u32[]{:S(2)}, u32[]{:S(2)}) collective-permute-start(f32[16,24,256]{2,1,0:T(8,128)} %all-to-all-done.1.after.own.values), channel_id=1, source_target_pairs={{0,16},{16,0},{1,17},{17,1},{2,18},{18,2},{3,19},{19,3},{4,20},{20... | collective-permute-start | bytes 1179656 | tf_op jit(solution)/shard_map/ppermute | solution.py:31
  49.6 10.0 %collective-permute-start.12 = (f32[192,384]{1,0:T(8,128)S(1)}, f32[192,384]{1,0:T(8,128)S(1)}, u32[]{:S(2)}, u32[]{:S(2)}) collective-permute-start(f32[192,384]{1,0:T(8,128)S(1)} %add.3.refs_0_), channel_id=1, source_target_pairs={{0,3},{1,0},{2,1},{3,2},{4,7},{5,4},{6,5},{7,6},{8,11},{9,8},{10,9... | collective-permute-start | bytes 884744 | tf_op jit(solution)/shard_map/ppermute | solution.py:31
  51.2 11.4 %collective-permute-start.11 = (f32[192,384]{1,0:T(8,128)S(1)}, f32[192,384]{1,0:T(8,128)S(1)}, u32[]{:S(2)}, u32[]{:S(2)}) collective-permute-start(f32[192,384]{1,0:T(8,128)S(1)} %add.3.refs_0_), channel_id=1, source_target_pairs={{0,2},{1,3},{2,0},{3,1},{4,6},{5,7},{6,4},{7,5},{8,10},{9,11},{10,... | collective-permute-start | bytes 884744 | tf_op jit(solution)/shard_map/ppermute | solution.py:31
  52.1 15.7 %collective-permute-start.10 = (f32[192,384]{1,0:T(8,128)S(1)}, f32[192,384]{1,0:T(8,128)S(1)}, u32[]{:S(2)}, u32[]{:S(2)}) collective-permute-start(f32[192,384]{1,0:T(8,128)S(1)} %add.3.refs_0_), channel_id=1, source_target_pairs={{0,1},{1,2},{2,3},{3,0},{4,5},{5,6},{6,7},{7,4},{8,9},{9,10},{10,1... | collective-permute-start | bytes 884744 | tf_op jit(solution)/shard_map/ppermute | solution.py:31
  89.7 13.0 %collective-permute-start.14 = (f32[432,128]{1,0:T(8,128)S(1)}, f32[432,128]{1,0:T(8,128)S(1)}, u32[]{:S(2)}, u32[]{:S(2)}) collective-permute-start(f32[432,128]{1,0:T(8,128)S(1)} %get-tuple-element.98), channel_id=1, source_target_pairs={{0,15},{1,2},{2,1},{3,4},{4,3},{5,6},{6,5},{7,8},{8,7},{9,10},{10,... | collective-permute-start | bytes 663560 | tf_op jit(solution)/shard_map/ppermute | solution.py:36
  91.9 20.5 %collective-permute-start.17 = (f32[192,384]{1,0:T(8,128)S(1)}, f32[192,384]{1,0:T(8,128)S(1)}, u32[]{:S(2)}, u32[]{:S(2)}) collective-permute-start(f32[192,384]{1,0:T(8,128)S(1)} %get-tuple-element.110), channel_id=1, source_target_pairs={{0,4},{4,8},{8,12},{12,0},{1,5},{5,9},{9,13},{13,1},{2,6},{6,10},{... | collective-permute-start | bytes 884744 | tf_op jit(solution)/shard_map/ppermute | solution.py:31
  92.9 20.5 %collective-permute-start.18 = (f32[192,384]{1,0:T(8,128)S(1)}, f32[192,384]{1,0:T(8,128)S(1)}, u32[]{:S(2)}, u32[]{:S(2)}) collective-permute-start(f32[192,384]{1,0:T(8,128)S(1)} %get-tuple-element.111), channel_id=1, source_target_pairs={{0,8},{4,12},{8,0},{12,4},{1,9},{5,13},{9,1},{13,5},{2,10},{6,14},... | collective-permute-start | bytes 884744 | tf_op jit(solution)/shard_map/ppermute | solution.py:31
  94.3 24.0 %collective-permute-start.19 = (f32[192,384]{1,0:T(8,128)S(1)}, f32[192,384]{1,0:T(8,128)S(1)}, u32[]{:S(2)}, u32[]{:S(2)}) collective-permute-start(f32[192,384]{1,0:T(8,128)S(1)} %get-tuple-element.112), channel_id=1, source_target_pairs={{0,12},{4,0},{8,4},{12,8},{1,13},{5,1},{9,5},{13,9},{2,14},{6,2},{... | collective-permute-start | bytes 884744 | tf_op jit(solution)/shard_map/ppermute | solution.py:31
  95.9 6.9 %collective-permute-start.15 = (f32[432,128]{1,0:T(8,128)S(1)}, f32[432,128]{1,0:T(8,128)S(1)}, u32[]{:S(2)}, u32[]{:S(2)}) collective-permute-start(f32[432,128]{1,0:T(8,128)S(1)} %get-tuple-element.99), channel_id=1, source_target_pairs={{0,16},{16,0},{32,48},{48,32},{64,80},{80,64},{96,112},{112,96},{1... | collective-permute-start | bytes 663560 | tf_op jit(solution)/shard_map/ppermute | solution.py:36
  113.4 8.8 %collective-permute-start.23 = (f32[1,24,256]{2,1,0:T(8,128)S(1)}, f32[1,24,256]{2,1,0:T(8,128)S(1)}, u32[]{:S(2)}, u32[]{:S(2)}) collective-permute-start(f32[1,24,256]{2,1,0:T(8,128)S(1)} %get-tuple-element.117.refs_0_), channel_id=1, source_target_pairs={{0,16},{16,0},{1,17},{17,1},{2,18},{18,2},{3,19},{19,3},{4,20},{20... | collective-permute-start | bytes 73736 | tf_op jit(solution)/shard_map/ppermute | solution.py:31
  114.0 8.2 %collective-permute-start.26 = (f32[1,24,256]{2,1,0:T(8,128)S(1)}, f32[1,24,256]{2,1,0:T(8,128)S(1)}, u32[]{:S(2)}, u32[]{:S(2)}) collective-permute-start(f32[1,24,256]{2,1,0:T(8,128)S(1)} %collective-permute-done.22.refs_3_), channel_id=1, source_target_pairs={{0,16},{16,0},{1,17},{17,1},{2,18},{18,2},{3,19},{19,3},{4,20},{20... | collective-permute-start | bytes 73736 | tf_op jit(solution)/shard_map/ppermute | solution.py:31
  141.0 9.5 %collective-permute-start.28 = (f32[432,128]{1,0:T(8,128)S(1)}, f32[432,128]{1,0:T(8,128)S(1)}, u32[]{:S(2)}, u32[]{:S(2)}) collective-permute-start(f32[432,128]{1,0:T(8,128)S(1)} %get-tuple-element.124), channel_id=1, source_target_pairs={{0,15},{1,2},{2,1},{3,4},{4,3},{5,6},{6,5},{7,8},{8,7},{9,10},{10,... | collective-permute-start | bytes 663560 | tf_op jit(solution)/shard_map/ppermute | solution.py:36
  143.3 7.3 %collective-permute-start.29 = (f32[432,128]{1,0:T(8,128)S(1)}, f32[432,128]{1,0:T(8,128)S(1)}, u32[]{:S(2)}, u32[]{:S(2)}) collective-permute-start(f32[432,128]{1,0:T(8,128)S(1)} %get-tuple-element.125), channel_id=1, source_target_pairs={{0,16},{16,0},{32,48},{48,32},{64,80},{80,64},{96,112},{112,96},{1... | collective-permute-start | bytes 663560 | tf_op jit(solution)/shard_map/ppermute | solution.py:36
  143.3 7.3 %collective-permute-start.30 = (f32[432,128]{1,0:T(8,128)S(1)}, f32[432,128]{1,0:T(8,128)S(1)}, u32[]{:S(2)}, u32[]{:S(2)}) collective-permute-start(f32[432,128]{1,0:T(8,128)S(1)} %get-tuple-element.126), channel_id=1, source_target_pairs={{0,112},{16,32},{32,16},{48,64},{64,48},{80,96},{96,80},{112,0},{1... | collective-permute-start | bytes 663560 | tf_op jit(solution)/shard_map/ppermute | solution.py:36
  154.6 7.1 %collective-permute-start.34 = (f32[1,24,256]{2,1,0:T(8,128)S(1)}, f32[1,24,256]{2,1,0:T(8,128)S(1)}, u32[]{:S(2)}, u32[]{:S(2)}) collective-permute-start(f32[1,24,256]{2,1,0:T(8,128)S(1)} %get-tuple-element.138.refs_0_), channel_id=1, source_target_pairs={{0,16},{16,0},{1,17},{17,1},{2,18},{18,2},{3,19},{19,3},{4,20},{20... | collective-permute-start | bytes 73736 | tf_op jit(solution)/shard_map/ppermute | solution.py:31
  162.8 14.4 %all-to-all-start.4 = ((f32[16,24,256]{2,1,0:T(8,128)}), f32[16,24,256]{2,1,0:T(8,128)S(1)}, u32[]{:S(2)}, u32[]{:S(2)}) async-start(f32[16,24,256]{2,1,0:T(8,128)} %shard_map.103), calls=%async_computation.4 | async-start | bytes 786432 | tf_op jit(solution)/shard_map/all_to_all | solution.py:40
  178.0 14.6 %all-to-all-start.5 = ((f32[128,1,256]{2,1,0:T(1,128)}), f32[128,1,256]{2,1,0:T(1,128)S(1)}, u32[]{:S(2)}, u32[]{:S(2)}) async-start(f32[128,1,256]{2,1,0:T(1,128)} %get-tuple-element.146), calls=%async_computation.5 | async-start | bytes 262144 | tf_op jit(solution)/shard_map/all_to_all | solution.py:40
  (32 other events, 179.9 us)

commit v6 on v5

--- a/solution.py
+++ b/solution.py
@@ -145,16 +145,28 @@
     return (1 - odd_b, odd_b, 3 - odd_a, 2 + odd_a)
 
 
-def ids_kernel(ids, side_rows, right, flex, told, line, counts):
+def ids_kernel(ids, right, flex, line):
     line[...] = jnp.zeros_like(line)
     line[:, 0 : ids.shape[1]] = ids[...].astype(F32)
-    told[...] = jnp.broadcast_to(line[...][None], told.shape)
+
+
+def line_kernel(*refs):
+    for k, line in enumerate(refs[:-1]):
+        refs[-1][k : k + 1, :] = line[...]
+
+
+def table_kernel(*refs):
+    my_x, my_z = lax.axis_index("x"), lax.axis_index("z")
+    for j, lines in enumerate(refs[:-1]):
+        for k in range(NZ):
+            at = ((my_x + NX - j) % NX) * NZ + (my_z + NZ - k) % NZ
+            refs[-1][pl.ds(at, 1), :] = lines[k : k + 1, :]
+
+
+def first_kernel(ids, side_rows, right, flex, flexed, extra, counts, *sends):
     live = side_rows[...].astype(F32)
     which = lax.broadcasted_iota(jnp.int32, counts.shape, 0)
     counts[...] = jnp.where(which == 0, live[:, 0:1], live[:, 1:2])
-
-
-def first_kernel(after, ids, counts, right, flex, flexed, extra, *sends):
     direction = (right[...] / cheb_center).astype(BF16)
     flexed[...] = dot(flex[...], direction, ((1,), (1,)))
     send_sides(counts, flexed, *sends)
@@ -215,12 +227,10 @@
         told[k] = told[0]
 
 
-def step_on(steps, flex, dir_low, low, new_dir_low, flex_base, rounded):
+def step_on(steps, flex, dir_low, low, new_dir_low, flex_base):
     new_dir = steps[0] * dir_low + steps[1] * low
     new_dir_low[...] = new_dir
-    rounded[0:TOP, :] = jnp.zeros((TOP, rounded.shape[1]), BF16)
-    rounded[TOP:, :] = new_dir.astype(BF16)
-    flex_base[...] = dot(flex[...], rounded[...])
+    flex_base[...] = dot(flex[:, TOP:], new_dir.astype(BF16))
 
 
 def first_bulk_kernel(steps, after, balanced, stiff, flex, right, *outs):
@@ -350,22 +360,27 @@
     corners = corner_map.shape[2]
     rows_held, cols_held = coarse_inv.shape
     half = N_GY * corners
+    (ids_line,) = call(ids_kernel, [shape(1, LANES)], unread=(right, flex_block))(corner_map[0])
+    lines = [ids_line]
+    for k in range(1, NZ):
+        lines.append(turned(ids_line, "z", NZ, k))
+    (line,) = call(line_kernel, [shape(NZ, LANES)])(*lines)
+    tables = [line]
+    for k in range(1, NX):
+        tables.append(turned(line, "x", NX, k))
+    (own_ids,) = call(table_kernel, [shape(N_GY, LANES)])(*tables)
+    other_ids = turned(own_ids, "c", NC, 1)
+
     inv_t = coarse_inv.T
     inv_blocks = [inv_t]
     for k in range(1, NY):
         inv_blocks.append(turned(inv_t, "y", NY, k))
 
-    own_ids, ids_line, counts = call(
-        ids_kernel, [shape(N_GY, 1, LANES), shape(1, LANES), shape(TILE, LANES)], unread=(right, flex_block)
-    )(corner_map[0], side_rows[0])
-    own_ids = to_all(own_ids, GY).reshape(N_GY, LANES)
-
     sides = [shape(side + side // 2, LANES)] * SIDES
-    flexed, extra, *sends = call(
-        first_kernel, [shape(order, loads), shape(corners, width)] + sides
-    )(own_ids, ids_line, counts, right, flex_block)
-
-    other_ids = turned(own_ids, "c", NC, 1)
+    flexed, extra, counts, *sends = call(
+        first_kernel, [shape(order, loads), shape(corners, width), shape(TILE, LANES)] + sides
+    )(ids_line, side_rows[0], right, flex_block)
+
     own_rows, other_rows = call(
         rows_kernel, [shape(cols_held, half)] * 2, scratch=[pltpu.VMEM((2 * half, rows_held), BF16)]
     )(own_ids, other_ids, *inv_blocks)
@@ -407,7 +422,6 @@
         outs = call(
             functools.partial(kernel, steps),
             [tops, lows, tops, lows, shape(1, loads)] + ([] if last else [lows, shape(order, loads)]),
-            scratch=[] if last else [pltpu.VMEM((order, loads), BF16)],
         )(*order_after, balanced, stiff_block, flex_block, *state)
         res_top, res_low, sol_top, sol_low, squares = outs[:5]
         if iteration == 0:

time: 195 us -> 196 us (level)
  blocking collectives: 49 us -> 31.2 us
  waiting for transfers between devices: 58.1 us -> 69.2 us
  starting transfers between devices: 46.1 us -> 53.8 us
    all_to_all x3 -> x2, blocking collectives: 49 us -> 31.2 us  [to_all(): return lax.all_to_all(copies, axes, split_axis=0, concat_axis=0, tiled=True)]
    ppermute x26 -> x32, waiting for transfers between devices: 20.7 us -> 31.5 us  [turned(): lax.ppermute(array, axes, [(i, (i + by) % count) for i in range(count)])]
    ppermute x12, starting transfers between devices: 11.8 us -> 16.5 us  [swapped(): return lax.ppermute(array, axes, pairs)]
    ppermute x26 -> x32, starting transfers between devices: 21.4 us -> 24.4 us  [turned(): lax.ppermute(array, axes, [(i, (i + by) % count) for i in range(count)])]
    ppermute x12, waiting for transfers between devices: 20.5 us -> 22.6 us  [swapped(): return lax.ppermute(array, axes, pairs)]
    pallas_call x20 -> x22, Pallas kernels: 24.7 us -> 24.1 us  [run(): pl.pallas_call(body, out_shape=outs, in_specs=[vm() for _ in operands] +...]
  transfers between devices with their start and end apart: 41 -> 47, of which waited for: 20 -> 24; matrix products, arithmetic and copies ran while one was open for 3% -> 3% of each run, Pallas kernels for 8% -> 7%
where the time goes in v6:
time: 196 us; the launch traced here: 195 us
  waiting for transfers between devices  69.2 us (35%)
  starting transfers between devices  53.8 us (27%)
  blocking collectives  31.2 us (16%)
  Pallas kernels  24.1 us (12%)
  local copies, waits for them, and re-layouts  12.6 us (6%)
  other arithmetic  3.03 us (2%)
    ppermute x32, waiting for transfers between devices, turned(): lax.ppermute(array, axes, [(i, (i + by) % count) for i in range(count)])  31.5 us
    all_to_all x2, blocking collectives, to_all(): return lax.all_to_all(copies, axes, split_axis=0, concat_axis=0, tiled=True)  31.2 us
    ppermute x32, starting transfers between devices, turned(): lax.ppermute(array, axes, [(i, (i + by) % count) for i in range(count)])  24.4 us
    pallas_call x22, Pallas kernels, run(): pl.pallas_call(body, out_shape=outs, in_specs=[vm() for _ in operands] +...  24.1 us
    ppermute x12, waiting for transfers between devices, swapped(): return lax.ppermute(array, axes, pairs)  22.6 us
    ppermute x12, starting transfers between devices, swapped(): return lax.ppermute(array, axes, pairs)  16.5 us
    all_to_all x3, waiting for transfers between devices, to_all(): return lax.all_to_all(copies, axes, split_axis=0, concat_axis=0, tiled=True)  15.1 us
    all_to_all x3, starting transfers between devices, to_all(): return lax.all_to_all(copies, axes, split_axis=0, concat_axis=0, tiled=True)  12.9 us
  transfers between devices with their start and end apart: 47, of which 24 were waited for; matrix products, arithmetic and copies ran while one was open for 3% of the time, Pallas kernels for 7%

profile of v6, /device:TPU:0, one launch (start us, length us, event | category | flops | bytes accessed | tf_op | source)
XLA Modules:
  0.0 194.9 jit_solution(3102896806429721410)
XLA Ops:
  6.6 4.7 %collective-permute-start.1 = (f32[432,128]{1,0:T(8,128)S(1)}, f32[432,128]{1,0:T(8,128)S(1)}, u32[]{:S(2)}, u32[]{:S(2)}) collective-permute-start(f32[432,128]{1,0:T(8,128)S(1)} %get-tuple-element.76), channel_id=1, source_target_pairs={{0,15},{1,2},{2,1},{3,4},{4,3},{5,6},{6,5},{7,8},{8,7},{9,10},{10,... | collective-permute-start | bytes 663560 | tf_op jit(solution)/shard_map/ppermute | solution.py:36
  11.3 3.1 %collective-permute-start.3 = (f32[432,128]{1,0:T(8,128)S(1)}, f32[432,128]{1,0:T(8,128)S(1)}, u32[]{:S(2)}, u32[]{:S(2)}) collective-permute-start(f32[432,128]{1,0:T(8,128)S(1)} %get-tuple-element.78), channel_id=1, source_target_pairs={{0,112},{16,32},{32,16},{48,64},{64,48},{80,96},{96,80},{112,0},{1... | collective-permute-start | bytes 663560 | tf_op jit(solution)/shard_map/ppermute | solution.py:36
  22.4 4.2 %all-to-all-start = ((f32[16,24,256]{2,1,0:T(8,128)}), f32[16,24,256]{2,1,0:T(8,128)}, u32[]{:S(2)}, u32[]{:S(2)}) async-start(f32[16,24,256]{2,1,0:T(8,128)} %copy-done.11), calls=%async_computation | async-start | bytes 786432 | tf_op jit(solution)/shard_map/all_to_all | solution.py:40
  26.7 3.0 %collective-permute-start.7 = (f32[1,128]{1,0:T(1,128)S(1)}, f32[1,128]{1,0:T(1,128)S(1)}, u32[]{:S(2)}, u32[]{:S(2)}) collective-permute-start(f32[1,128]{1,0:T(1,128)S(1)} %shard_map.85.ids.refs_0_), channel_id=1, source_target_pairs={{0,3},{1,0},{2,1},{3,2},{4,7},{5,4},{6,5},{7,6},{8,11},{9,8},{10,9... | collective-permute-start | bytes 1544 | tf_op jit(solution)/shard_map/ppermute | solution.py:31
  31.0 3.8 %collective-permute-done.6.refs_2_ = f32[1,128]{1,0:T(1,128)S(1)} collective-permute-done((f32[1,128]{1,0:T(1,128)S(1)}, f32[1,128]{1,0:T(1,128)S(1)}, u32[]{:S(2)}, u32[]{:S(2)}) %collective-permute-start.6) | collective-permute-done | bytes 544 | tf_op jit(solution)/shard_map/ppermute | solution.py:31
  36.0 3.0 %collective-permute-start.10 = (f32[4,128]{1,0:T(4,128)S(1)}, f32[4,128]{1,0:T(4,128)S(1)}, u32[]{:S(2)}, u32[]{:S(2)}) collective-permute-start(f32[4,128]{1,0:T(4,128)S(1)} %shard_map.89.refs_0_), channel_id=1, source_target_pairs={{0,12},{4,0},{8,4},{12,8},{1,13},{5,1},{9,5},{13,9},{2,14},{6,2},{... | collective-permute-start | bytes 6152 | tf_op jit(solution)/shard_map/ppermute | solution.py:31
  41.4 2.7 %collective-permute-done.9.refs_2_ = f32[4,128]{1,0:T(4,128)S(1)} collective-permute-done((f32[4,128]{1,0:T(4,128)S(1)}, f32[4,128]{1,0:T(4,128)S(1)}, u32[]{:S(2)}, u32[]{:S(2)}) %collective-permute-start.9) | collective-permute-done | bytes 2080 | tf_op jit(solution)/shard_map/ppermute | solution.py:31
  46.7 4.0 %shard_map.91 = (f32[192,384]{1,0:T(8,128)S(1)}, f32[192,384]{1,0:T(8,128)}) custom-call(f32[16,128]{1,0:T(8,128)S(1)} %shard_map.90.ids_own, f32[16,128]{1,0:T(8,128)S(1)} %collective-permute-done.11.ids_other, f32[192,384]{1,0:T(8,128)} %bitcast.5.refs_0_, f32[192,384]{1,0:T(8,128)} %collective-permute-done.12.refs_1_, ...), custom_call_target="tpu_custom_call" | custom-call | tf_op jit(solution)/shard_map/pallas_call | solution.py:49
  59.2 3.9 %shard_map.88 = (f32[128,176]{1,0:T(8,128)S(1)}, f32[1024,176]{1,0:T(8,128)S(1)}, f32[128,176]{1,0:T(8,128)S(1)}, f32[1024,176]{1,0:T(8,128)S(1)}, f32[1,176]{1,...) custom-call(f32[16,24,256]{2,1,0:T(8,128)} %all-to-all-done.after.own.values, ...), custom_call_target="tpu_custom_call" | custom-call | tf_op jit(solution)/shard_map/pallas_call | solution.py:49
  63.1 6.3 %collective-permute-done.18.refs_3_ = f32[192,384]{1,0:T(8,128)S(1)} collective-permute-done((f32[192,384]{1,0:T(8,128)S(1)}, f32[192,384]{1,0:T(8,128)S(1)}, u32[]{:S(2)}, u32[]{:S(2)}) %collective-permute-start.18) | collective-permute-done | bytes 294944 | tf_op jit(solution)/shard_map/ppermute | solution.py:31
  69.4 3.4 %collective-permute-done.16.refs_1_ = f32[192,384]{1,0:T(8,128)S(1)} collective-permute-done((f32[192,384]{1,0:T(8,128)S(1)}, f32[192,384]{1,0:T(8,128)S(1)}, u32[]{:S(2)}, u32[]{:S(2)}) %collective-permute-start.16) | collective-permute-done | bytes 294944 | tf_op jit(solution)/shard_map/ppermute | solution.py:31
  72.8 3.1 %shard_map.92 = (bf16[384,384]{1,0:T(8,128)(2,1)S(1)}, bf16[384,384]{1,0:T(8,128)(2,1)S(1)}, bf16[384,384]{1,0:T(8,128)(2,1)S(1)}, bf16[384,384]{1,0:T(8,128)(2,...) custom-call(f32[16,24,256]{2,1,0:T(8,128)} %all-to-all-done.after.own, ...), custom_call_target="tpu_custom_call" | custom-call | tf_op jit(solution)/shard_map/pallas_call | solution.py:49
  77.8 13.2 %all_to_all.25.terms = f32[16,24,256]{2,1,0:T(8,128)S(1)} all-to-all(f32[16,24,256]{2,1,0:T(8,128)S(1)} %shard_map.94), channel_id=1, replica_groups=mesh['y'=4,'c'=2,'x'=4,'z'=4] {'x','z'}, dimensions={0} | all-to-all | bytes 786432 | tf_op jit(solution)/shard_map/all_to_all | solution.py:40
  98.2 6.9 %collective-permute-done.20.in_b = f32[432,128]{1,0:T(8,128)S(1)} collective-permute-done((f32[432,128]{1,0:T(8,128)S(1)}, f32[432,128]{1,0:T(8,128)S(1)}, u32[]{:S(2)}, u32[]{:S(2)}) %collective-permute-start.20) | collective-permute-done | bytes 221216 | tf_op jit(solution)/shard_map/ppermute | solution.py:36
  105.1 6.6 %collective-permute-done.22.in_y = f32[432,128]{1,0:T(8,128)S(1)} collective-permute-done((f32[432,128]{1,0:T(8,128)S(1)}, f32[432,128]{1,0:T(8,128)S(1)}, u32[]{:S(2)}, u32[]{:S(2)}) %collective-permute-start.22) | collective-permute-done | bytes 221216 | tf_op jit(solution)/shard_map/ppermute | solution.py:36
  116.2 3.0 %collective-permute-done.27.refs_2_ = f32[1,24,256]{2,1,0:T(8,128)S(1)} collective-permute-done((f32[1,24,256]{2,1,0:T(8,128)S(1)}, f32[1,24,256]{2,1,0:T(8,128)S(1)}, u32[]{:S(2)}, u32[]{:S(2)}) %collective-permute-start.27) | collective-permute-done | bytes 24608 | tf_op jit(solution)/shard_map/ppermute | solution.py:31
  120.0 3.0 %shard_map.97 = (f32[128,176]{1,0:T(8,128)S(1)}, f32[1024,176]{1,0:T(8,128)S(1)}, f32[128,176]{1,0:T(8,128)S(1)}, f32[1024,176]{1,0:T(8,128)S(1)}, f32[1,176]{1,...) custom-call(bf16[1152,176]{1,0:T(8,128)(2,1)S(1)} %get-tuple-element.98.balanced, ...), custom_call_target="tpu_custom_call" | custom-call | tf_op jit(solution)/shard_map/pallas_call | solution.py:49
  123.7 18.0 %all_to_all.26.terms = f32[16,24,256]{2,1,0:T(8,128)S(1)} all-to-all(f32[16,24,256]{2,1,0:T(8,128)S(1)} %shard_map.100), channel_id=1, replica_groups=mesh['y'=4,'c'=2,'x'=4,'z'=4] {'x','z'}, dimensions={0} | all-to-all | bytes 786432 | tf_op jit(solution)/shard_map/all_to_all | solution.py:40
  148.4 3.8 %collective-permute-done.34.in_b = f32[432,128]{1,0:T(8,128)S(1)} collective-permute-done((f32[432,128]{1,0:T(8,128)S(1)}, f32[432,128]{1,0:T(8,128)S(1)}, u32[]{:S(2)}, u32[]{:S(2)}) %collective-permute-start.34) | collective-permute-done | bytes 221216 | tf_op jit(solution)/shard_map/ppermute | solution.py:36
  156.6 2.7 %collective-permute-done.38.refs_2_ = f32[1,24,256]{2,1,0:T(8,128)S(1)} collective-permute-done((f32[1,24,256]{2,1,0:T(8,128)S(1)}, f32[1,24,256]{2,1,0:T(8,128)S(1)}, u32[]{:S(2)}, u32[]{:S(2)}) %collective-permute-start.38) | collective-permute-done | bytes 24608 | tf_op jit(solution)/shard_map/ppermute | solution.py:31
  164.4 3.6 %all-to-all-start.3 = ((f32[16,24,256]{2,1,0:T(8,128)}), f32[16,24,256]{2,1,0:T(8,128)S(1)}, u32[]{:S(2)}, u32[]{:S(2)}) async-start(f32[16,24,256]{2,1,0:T(8,128)} %shard_map.105), calls=%async_computation.3 | async-start | bytes 786432 | tf_op jit(solution)/shard_map/all_to_all | solution.py:40
  169.4 9.3 %all-to-all-done.3.terms = f32[16,24,256]{2,1,0:T(8,128)S(1)} async-done(((f32[16,24,256]{2,1,0:T(8,128)}), f32[16,24,256]{2,1,0:T(8,128)S(1)}, u32[]{:S(2)}, u32[]{:S(2)}) %all-to-all-start.3) | async-done | bytes 393248 | tf_op jit(solution)/shard_map/all_to_all | solution.py:40
  179.4 5.1 %all-to-all-start.4 = ((f32[128,1,256]{2,1,0:T(1,128)}), f32[128,1,256]{2,1,0:T(1,128)S(1)}, u32[]{:S(2)}, u32[]{:S(2)}) async-start(f32[128,1,256]{2,1,0:T(1,128)} %get-tuple-element.142), calls=%async_computation.4 | async-start | bytes 262144 | tf_op jit(solution)/shard_map/all_to_all | solution.py:40
  188.4 5.8 %all-to-all-done.4 = f32[128,1,256]{2,1,0:T(1,128)S(1)} async-done(((f32[128,1,256]{2,1,0:T(1,128)}), f32[128,1,256]{2,1,0:T(1,128)S(1)}, u32[]{:S(2)}, u32[]{:S(2)}) %all-to-all-start.4) | async-done | bytes 131104 | tf_op jit(solution)/shard_map/all_to_all | solution.py:40
  (135 shorter events, 67.9 us)
Async XLA Ops:
  4.5 10.7 %collective-permute-start = (f32[432,128]{1,0:T(8,128)S(1)}, f32[432,128]{1,0:T(8,128)S(1)}, u32[]{:S(2)}, u32[]{:S(2)}) collective-permute-start(f32[432,128]{1,0:T(8,128)S(1)} %get-tuple-element.75), channel_id=1, source_target_pairs={{0,1},{1,0},{2,3},{3,2},{4,5},{5,4},{6,7},{7,6},{8,9},{9,8},{10,11... | collective-permute-start | bytes 663560 | tf_op jit(solution)/shard_map/ppermute | solution.py:36
  6.6 10.2 %collective-permute-start.1 = (f32[432,128]{1,0:T(8,128)S(1)}, f32[432,128]{1,0:T(8,128)S(1)}, u32[]{:S(2)}, u32[]{:S(2)}) collective-permute-start(f32[432,128]{1,0:T(8,128)S(1)} %get-tuple-element.76), channel_id=1, source_target_pairs={{0,15},{1,2},{2,1},{3,4},{4,3},{5,6},{6,5},{7,8},{8,7},{9,10},{10,... | collective-permute-start | bytes 663560 | tf_op jit(solution)/shard_map/ppermute | solution.py:36
  11.3 7.1 %collective-permute-start.2 = (f32[432,128]{1,0:T(8,128)S(1)}, f32[432,128]{1,0:T(8,128)S(1)}, u32[]{:S(2)}, u32[]{:S(2)}) collective-permute-start(f32[432,128]{1,0:T(8,128)S(1)} %get-tuple-element.77), channel_id=1, source_target_pairs={{0,16},{16,0},{32,48},{48,32},{64,80},{80,64},{96,112},{112,96},{1... | collective-permute-start | bytes 663560 | tf_op jit(solution)/shard_map/ppermute | solution.py:36
  11.3 8.9 %collective-permute-start.3 = (f32[432,128]{1,0:T(8,128)S(1)}, f32[432,128]{1,0:T(8,128)S(1)}, u32[]{:S(2)}, u32[]{:S(2)}) collective-permute-start(f32[432,128]{1,0:T(8,128)S(1)} %get-tuple-element.78), channel_id=1, source_target_pairs={{0,112},{16,32},{32,16},{48,64},{64,48},{80,96},{96,80},{112,0},{1... | collective-permute-start | bytes 663560 | tf_op jit(solution)/shard_map/ppermute | solution.py:36
  14.4 32.2 %collective-permute-start.14 = (f32[192,384]{1,0:T(8,128)}, f32[192,384]{1,0:T(8,128)}, u32[]{:S(2)}, u32[]{:S(2)}) collective-permute-start(f32[192,384]{1,0:T(8,128)} %bitcast.5.refs_0_), channel_id=1, source_target_pairs={{0,96},{32,0},{64,32},{96,64},{1,97},{33,1},{65,33},{97,65},{2,98}... | collective-permute-start | bytes 884744 | tf_op jit(solution)/shard_map/ppermute | solution.py:31
  15.2 31.5 %collective-permute-start.13 = (f32[192,384]{1,0:T(8,128)}, f32[192,384]{1,0:T(8,128)}, u32[]{:S(2)}, u32[]{:S(2)}) collective-permute-start(f32[192,384]{1,0:T(8,128)} %bitcast.5.refs_0_), channel_id=1, source_target_pairs={{0,64},{32,96},{64,0},{96,32},{1,65},{33,97},{65,1},{97,33},{2,66}... | collective-permute-start | bytes 884744 | tf_op jit(solution)/shard_map/ppermute | solution.py:31
  16.8 29.9 %collective-permute-start.12 = (f32[192,384]{1,0:T(8,128)}, f32[192,384]{1,0:T(8,128)}, u32[]{:S(2)}, u32[]{:S(2)}) collective-permute-start(f32[192,384]{1,0:T(8,128)} %bitcast.5.refs_0_), channel_id=1, source_target_pairs={{0,32},{32,64},{64,96},{96,0},{1,33},{33,65},{65,97},{97,1},{2,34}... | collective-permute-start | bytes 884744 | tf_op jit(solution)/shard_map/ppermute | solution.py:31
  22.4 29.1 %all-to-all-start = ((f32[16,24,256]{2,1,0:T(8,128)}), f32[16,24,256]{2,1,0:T(8,128)}, u32[]{:S(2)}, u32[]{:S(2)}) async-start(f32[16,24,256]{2,1,0:T(8,128)} %copy-done.11), calls=%async_computation | async-start | bytes 786432 | tf_op jit(solution)/shard_map/all_to_all | solution.py:40
  51.5 21.3 %collective-permute-start.4 = (f32[16,24,256]{2,1,0:T(8,128)}, f32[16,24,256]{2,1,0:T(8,128)S(1)}, u32[]{:S(2)}, u32[]{:S(2)}) collective-permute-start(f32[16,24,256]{2,1,0:T(8,128)} %all-to-all-done.after.own.values), channel_id=1, source_target_pairs={{0,16},{16,0},{1,17},{17,1},{2,18},{18,2},{3,19},{19,3},{4,20},{20... | collective-permute-start | bytes 1179656 | tf_op jit(solution)/shard_map/ppermute | solution.py:31
  54.4 15.0 %collective-permute-start.18 = (f32[192,384]{1,0:T(8,128)S(1)}, f32[192,384]{1,0:T(8,128)S(1)}, u32[]{:S(2)}, u32[]{:S(2)}) collective-permute-start(f32[192,384]{1,0:T(8,128)S(1)} %add.3.refs_0_), channel_id=1, source_target_pairs={{0,3},{1,0},{2,1},{3,2},{4,7},{5,4},{6,5},{7,6},{8,11},{9,8},{10,9... | collective-permute-start | bytes 884744 | tf_op jit(solution)/shard_map/ppermute | solution.py:31
  56.5 13.0 %collective-permute-start.17 = (f32[192,384]{1,0:T(8,128)S(1)}, f32[192,384]{1,0:T(8,128)S(1)}, u32[]{:S(2)}, u32[]{:S(2)}) collective-permute-start(f32[192,384]{1,0:T(8,128)S(1)} %add.3.refs_0_), channel_id=1, source_target_pairs={{0,2},{1,3},{2,0},{3,1},{4,6},{5,7},{6,4},{7,5},{8,10},{9,11},{10,... | collective-permute-start | bytes 884744 | tf_op jit(solution)/shard_map/ppermute | solution.py:31
  56.5 16.3 %collective-permute-start.16 = (f32[192,384]{1,0:T(8,128)S(1)}, f32[192,384]{1,0:T(8,128)S(1)}, u32[]{:S(2)}, u32[]{:S(2)}) collective-permute-start(f32[192,384]{1,0:T(8,128)S(1)} %add.3.refs_0_), channel_id=1, source_target_pairs={{0,1},{1,2},{2,3},{3,0},{4,5},{5,6},{6,7},{7,4},{8,9},{9,10},{10,1... | collective-permute-start | bytes 884744 | tf_op jit(solution)/shard_map/ppermute | solution.py:31
  92.1 13.1 %collective-permute-start.20 = (f32[432,128]{1,0:T(8,128)S(1)}, f32[432,128]{1,0:T(8,128)S(1)}, u32[]{:S(2)}, u32[]{:S(2)}) collective-permute-start(f32[432,128]{1,0:T(8,128)S(1)} %get-tuple-element.94), channel_id=1, source_target_pairs={{0,15},{1,2},{2,1},{3,4},{4,3},{5,6},{6,5},{7,8},{8,7},{9,10},{10,... | collective-permute-start | bytes 663560 | tf_op jit(solution)/shard_map/ppermute | solution.py:36
  94.3 20.3 %collective-permute-start.23 = (f32[192,384]{1,0:T(8,128)S(1)}, f32[192,384]{1,0:T(8,128)S(1)}, u32[]{:S(2)}, u32[]{:S(2)}) collective-permute-start(f32[192,384]{1,0:T(8,128)S(1)} %get-tuple-element.106), channel_id=1, source_target_pairs={{0,4},{4,8},{8,12},{12,0},{1,5},{5,9},{9,13},{13,1},{2,6},{6,10},{... | collective-permute-start | bytes 884744 | tf_op jit(solution)/shard_map/ppermute | solution.py:31
  95.2 20.3 %collective-permute-start.24 = (f32[192,384]{1,0:T(8,128)S(1)}, f32[192,384]{1,0:T(8,128)S(1)}, u32[]{:S(2)}, u32[]{:S(2)}) collective-permute-start(f32[192,384]{1,0:T(8,128)S(1)} %get-tuple-element.107), channel_id=1, source_target_pairs={{0,8},{4,12},{8,0},{12,4},{1,9},{5,13},{9,1},{13,5},{2,10},{6,14},... | collective-permute-start | bytes 884744 | tf_op jit(solution)/shard_map/ppermute | solution.py:31
  96.7 23.0 %collective-permute-start.25 = (f32[192,384]{1,0:T(8,128)S(1)}, f32[192,384]{1,0:T(8,128)S(1)}, u32[]{:S(2)}, u32[]{:S(2)}) collective-permute-start(f32[192,384]{1,0:T(8,128)S(1)} %get-tuple-element.108), channel_id=1, source_target_pairs={{0,12},{4,0},{8,4},{12,8},{1,13},{5,1},{9,5},{13,9},{2,14},{6,2},{... | collective-permute-start | bytes 884744 | tf_op jit(solution)/shard_map/ppermute | solution.py:31
  115.5 7.8 %collective-permute-start.29 = (f32[1,24,256]{2,1,0:T(8,128)S(1)}, f32[1,24,256]{2,1,0:T(8,128)S(1)}, u32[]{:S(2)}, u32[]{:S(2)}) collective-permute-start(f32[1,24,256]{2,1,0:T(8,128)S(1)} %get-tuple-element.113.refs_0_), channel_id=1, source_target_pairs={{0,16},{16,0},{1,17},{17,1},{2,18},{18,2},{3,19},{19,3},{4,20},{20... | collective-permute-start | bytes 73736 | tf_op jit(solution)/shard_map/ppermute | solution.py:31
  116.2 7.2 %collective-permute-start.32 = (f32[1,24,256]{2,1,0:T(8,128)S(1)}, f32[1,24,256]{2,1,0:T(8,128)S(1)}, u32[]{:S(2)}, u32[]{:S(2)}) collective-permute-start(f32[1,24,256]{2,1,0:T(8,128)S(1)} %collective-permute-done.28.refs_3_), channel_id=1, source_target_pairs={{0,16},{16,0},{1,17},{17,1},{2,18},{18,2},{3,19},{19,3},{4,20},{20... | collective-permute-start | bytes 73736 | tf_op jit(solution)/shard_map/ppermute | solution.py:31
  142.7 9.4 %collective-permute-start.34 = (f32[432,128]{1,0:T(8,128)S(1)}, f32[432,128]{1,0:T(8,128)S(1)}, u32[]{:S(2)}, u32[]{:S(2)}) collective-permute-start(f32[432,128]{1,0:T(8,128)S(1)} %get-tuple-element.120), channel_id=1, source_target_pairs={{0,15},{1,2},{2,1},{3,4},{4,3},{5,6},{6,5},{7,8},{8,7},{9,10},{10,... | collective-permute-start | bytes 663560 | tf_op jit(solution)/shard_map/ppermute | solution.py:36
  144.9 7.3 %collective-permute-start.35 = (f32[432,128]{1,0:T(8,128)S(1)}, f32[432,128]{1,0:T(8,128)S(1)}, u32[]{:S(2)}, u32[]{:S(2)}) collective-permute-start(f32[432,128]{1,0:T(8,128)S(1)} %get-tuple-element.121), channel_id=1, source_target_pairs={{0,16},{16,0},{32,48},{48,32},{64,80},{80,64},{96,112},{112,96},{1... | collective-permute-start | bytes 663560 | tf_op jit(solution)/shard_map/ppermute | solution.py:36
  144.9 7.3 %collective-permute-start.36 = (f32[432,128]{1,0:T(8,128)S(1)}, f32[432,128]{1,0:T(8,128)S(1)}, u32[]{:S(2)}, u32[]{:S(2)}) collective-permute-start(f32[432,128]{1,0:T(8,128)S(1)} %get-tuple-element.122), channel_id=1, source_target_pairs={{0,112},{16,32},{32,16},{48,64},{64,48},{80,96},{96,80},{112,0},{1... | collective-permute-start | bytes 663560 | tf_op jit(solution)/shard_map/ppermute | solution.py:36
  155.7 7.6 %collective-permute-start.40 = (f32[1,24,256]{2,1,0:T(8,128)S(1)}, f32[1,24,256]{2,1,0:T(8,128)S(1)}, u32[]{:S(2)}, u32[]{:S(2)}) collective-permute-start(f32[1,24,256]{2,1,0:T(8,128)S(1)} %get-tuple-element.134.refs_0_), channel_id=1, source_target_pairs={{0,16},{16,0},{1,17},{17,1},{2,18},{18,2},{3,19},{19,3},{4,20},{20... | collective-permute-start | bytes 73736 | tf_op jit(solution)/shard_map/ppermute | solution.py:31
  164.4 14.3 %all-to-all-start.3 = ((f32[16,24,256]{2,1,0:T(8,128)}), f32[16,24,256]{2,1,0:T(8,128)S(1)}, u32[]{:S(2)}, u32[]{:S(2)}) async-start(f32[16,24,256]{2,1,0:T(8,128)} %shard_map.105), calls=%async_computation.3 | async-start | bytes 786432 | tf_op jit(solution)/shard_map/all_to_all | solution.py:40
  179.4 14.7 %all-to-all-start.4 = ((f32[128,1,256]{2,1,0:T(1,128)}), f32[128,1,256]{2,1,0:T(1,128)S(1)}, u32[]{:S(2)}, u32[]{:S(2)}) async-start(f32[128,1,256]{2,1,0:T(1,128)} %get-tuple-element.142), calls=%async_computation.4 | async-start | bytes 262144 | tf_op jit(solution)/shard_map/all_to_all | solution.py:40
  (38 other events, 185.8 us)

commit v7 on v6

--- a/solution.py
+++ b/solution.py
@@ -100,14 +100,15 @@
     other[...] = total[:, half:]
 
 
-def cols_kernel(own, other, *refs):
+def cols_kernel(*refs):
+    values, refs = refs[: NC * NX], refs[NC * NX :]
     blocks, outs, sends, pick, total = refs[:NZ], refs[NZ : NZ + 4], refs[NZ + 4 : -2], refs[-2], refs[-1]
     my_x, my_z = lax.axis_index("x"), lax.axis_index("z")
     held = blocks[0].shape[0]
     half = outs[0].shape[1]
-    last = own.shape[2] - 1
-    corners = own.shape[1]
-    columns = [v[n, :, last:] for v in (own, other) for n in range(v.shape[0])]
+    share = half // NX
+    last = values[0].shape[2] - 1
+    columns = [v[n, :, last:] for v in values for n in range(NY)]
     summed = 0.0
     for k, block in enumerate(blocks):
         base = ((my_x * NZ + (my_z + NZ - k) % NZ) * held).astype(F32)
@@ -118,9 +119,9 @@
     for n in range(2):
         outs[2 * n][...], outs[2 * n + 1][...] = split(summed[n * half : (n + 1) * half].T)
     for k, send in enumerate(sends):
-        for n in range(NC * NY):
-            start = pl.multiple_of((n * NX + (my_x + k) % NX) * corners, TILE)
-            send[n * corners : (n + 1) * corners, :] = total[pl.ds(start, corners), :]
+        for n in range(NC):
+            start = n * half + ((NX - k) % NX) * share
+            send[n * share : (n + 1) * share, :] = total[start : start + share, :]
 
 
 def block_kernel(*refs):
@@ -223,8 +224,6 @@
     corners = told.shape[1]
     told[0] = extra[...]
     told[0, :, 0:loads] = dot(stiff[0:32, :], balanced[...])[:corners]
-    for k in range(1, told.shape[0]):
-        told[k] = told[0]
 
 
 def step_on(steps, flex, dir_low, low, new_dir_low, flex_base):
@@ -233,7 +232,7 @@
     flex_base[...] = dot(flex[:, TOP:], new_dir.astype(BF16))
 
 
-def first_bulk_kernel(steps, after, balanced, stiff, flex, right, *outs):
+def first_bulk_kernel(steps, balanced, stiff, flex, right, *outs):
     right = right[...].T
     res_top, res_low, sol_top, sol_low, squares = outs[:5]
     stiffed = dot(stiff[...], balanced[...])
@@ -271,21 +270,28 @@
     return parts[0]
 
 
-def first_half_kernel(high, low, values, total):
-    total[...] = split_dot(high, low, values[...].reshape(-1, values.shape[2]))
-
-
-def first_product_kernel(after, high, low, values, half, total):
-    more = split_dot(high, low, values[...].reshape(-1, values.shape[2]))
-    total[...] = (half[...] + more).reshape(total.shape)
+def rows_of(values):
+    return jnp.concatenate([v[...].reshape(-1, v.shape[2]) for v in values], axis=0)
+
+
+def stack_kernel(*refs):
+    for k, block in enumerate(refs[:-1]):
+        refs[-1][k] = block[0]
+
+
+def first_half_kernel(high, low, *refs):
+    refs[-1][...] = split_dot(high, low, rows_of(refs[:-1]))
+
+
+def first_product_kernel(high, low, half, *refs):
+    total = refs[-1]
+    total[...] = (half[...] + split_dot(high, low, rows_of(refs[:-1]))).reshape(total.shape)
 
 
 def gathered(blocks, stack):
-    my_y = lax.axis_index("y")
     corners = blocks[0].shape[1]
     for k, block in enumerate(blocks):
-        at = pl.multiple_of(((my_y + NY - k) % NY) * corners, TILE)
-        stack[pl.ds(at, corners), :] = block[0]
+        stack[k * corners : (k + 1) * corners, :] = block[0]
     b = [block[0, 0:TILE, :] for block in blocks]
     return (b[0] + b[2]) + (b[1] + b[3])
 
@@ -402,47 +408,47 @@
             axes, count = (GY, N_GY) if k < 2 else (GX, N_GX)
             ins.append(swapped(sends[k], axes, count, k % 2))
         balanced, told = call(
-            balance_kernel, [shape(order, loads, dtype=BF16), shape(NY * NX if iteration == 0 else 1, corners, width)]
+            balance_kernel, [shape(order, loads, dtype=BF16), shape(1, corners, width)]
         )(counts, flexed, *ins, stiff_block, extra)
         steps = None
         if not last:
             rho_next = 1.0 / (2.0 * cheb_sigma - rho_prev)
             steps = (rho_next * rho_prev, 2.0 * rho_next / cheb_half)
             rho_prev = rho_next
+        values = [told]
+        for k in range(1, NY):
+            values.append(turned(told, "y", NY, k))
         if iteration == 0:
-            values = to_all(told, ("y", "x"))
+            (stacked,) = call(stack_kernel, [shape(NY, corners, width)])(*values)
+            values = [stacked]
+            for k in range(1, NX):
+                values.append(turned(stacked, "x", NX, k))
             kernel, state = first_bulk_kernel, (right,)
-            order_after = (values,)
         else:
-            values = [told]
-            for k in range(1, NY):
-                values.append(turned(told, "y", NY, k))
             kernel, state = bulk_kernel, (res_top, res_low, dir_top, dir_low, sol_top, sol_low)
-            order_after = ()
         outs = call(
             functools.partial(kernel, steps),
             [tops, lows, tops, lows, shape(1, loads)] + ([] if last else [lows, shape(order, loads)]),
-        )(*order_after, balanced, stiff_block, flex_block, *state)
+        )(balanced, stiff_block, flex_block, *state)
         res_top, res_low, sol_top, sol_low, squares = outs[:5]
+        others = []
+        for value in values:
+            others.append(turned(value, "c", NC, 1))
         if iteration == 0:
             dir_top = sol_top
-            values_other = turned(values, "c", NC, 1)
             own_high, own_low, other_high, other_low, *shares = call(
                 cols_kernel,
                 [shape(half, half, dtype=BF16)] * 4 + [shape(half // NX * 2, half)] * NX,
                 scratch=[pltpu.VMEM((2 * half, cols_held), BF16), pltpu.VMEM((2 * half, half), F32)],
-            )(values, values_other, *row_parts)
-            (partial,) = call(first_half_kernel, [shape(half, width)])(own_high, own_low, values)
+            )(*values, *others, *row_parts)
+            (partial,) = call(first_half_kernel, [shape(half, width)])(own_high, own_low, *values)
             (partial,) = call(first_product_kernel, [shape(N_GY, corners, width)])(
-                squares, other_high, other_low, values_other, partial
+                other_high, other_low, partial, *others
             )
             for k in range(1, NX):
                 shares[k] = turned(shares[k], "x", NX, k)
             block = call(block_kernel, [shape(half, NY * corners, dtype=BF16)] * 4)(*shares)
         else:
-            others = []
-            for k in range(NY):
-                others.append(turned(values[k], "c", NC, 1))
             partial, ride = call(
                 half_product_kernel, [shape(half, width), ride_shape], scratch=corner_scratch
             )(*block[:2], *values)

time: 196 us -> 204 us (1.041)
  blocking collectives: 31.2 us -> 17.6 us
  starting transfers between devices: 53.8 us -> 63.1 us
  waiting for transfers between devices: 69.2 us -> 77.9 us
  local copies, waits for them, and re-layouts: 12.6 us -> 20.4 us
  Pallas kernels: 24.1 us -> 20.3 us
    all_to_all x2 -> x1, blocking collectives: 31.2 us -> 17.6 us  [to_all(): return lax.all_to_all(copies, axes, split_axis=0, concat_axis=0, tiled=True)]
    ppermute x32 -> x41, waiting for transfers between devices: 31.5 us -> 39.7 us  [turned(): lax.ppermute(array, axes, [(i, (i + by) % count) for i in range(count)])]
    ppermute x32 -> x41, starting transfers between devices: 24.4 us -> 32.6 us  [turned(): lax.ppermute(array, axes, [(i, (i + by) % count) for i in range(count)])]
    unnamed x32 -> x72, local copies, waits for them, and re-layouts: 12.3 us -> 20.1 us
    pallas_call x22 -> x23, Pallas kernels: 24.1 us -> 20.3 us  [run(): pl.pallas_call(body, out_shape=outs, in_specs=[vm() for _ in operands] +...]
  transfers between devices with their start and end apart: 47 -> 56, of which waited for: 24 -> 29; matrix products, arithmetic and copies ran while one was open for 3% -> 3% of each run, Pallas kernels for 7% -> 6%
where the time goes in v7:
time: 204 us; the launch traced here: 202 us
  waiting for transfers between devices  77.9 us (38%)
  starting transfers between devices  63.1 us (31%)
  local copies, waits for them, and re-layouts  20.4 us (10%)
  Pallas kernels  20.3 us (10%)
  blocking collectives  17.6 us (9%)
    ppermute x41, waiting for transfers between devices, turned(): lax.ppermute(array, axes, [(i, (i + by) % count) for i in range(count)])  39.7 us
    ppermute x41, starting transfers between devices, turned(): lax.ppermute(array, axes, [(i, (i + by) % count) for i in range(count)])  32.6 us
    ppermute x12, waiting for transfers between devices, swapped(): return lax.ppermute(array, axes, pairs)  23.1 us
    pallas_call x23, Pallas kernels, run(): pl.pallas_call(body, out_shape=outs, in_specs=[vm() for _ in operands] +...  20.3 us
    unnamed x72, local copies, waits for them, and re-layouts  20.1 us
    all_to_all x1, blocking collectives, to_all(): return lax.all_to_all(copies, axes, split_axis=0, concat_axis=0, tiled=True)  17.6 us
    ppermute x12, starting transfers between devices, swapped(): return lax.ppermute(array, axes, pairs)  16.9 us
    all_to_all x3, waiting for transfers between devices, to_all(): return lax.all_to_all(copies, axes, split_axis=0, concat_axis=0, tiled=True)  15.1 us
  transfers between devices with their start and end apart: 56, of which 29 were waited for; matrix products, arithmetic and copies ran while one was open for 3% of the time, Pallas kernels for 6%

profile of v7, /device:TPU:0, one launch (start us, length us, event | category | flops | bytes accessed | tf_op | source)
XLA Modules:
  0.0 202.4 jit_solution(6016354992078669130)
XLA Ops:
  0.6 3.2 %collective-permute-start.23 = (f32[192,384]{1,0:T(8,128)}, f32[192,384]{1,0:T(8,128)S(1)}, u32[]{:S(2)}, u32[]{:S(2)}) collective-permute-start(f32[192,384]{1,0:T(8,128)} %bitcast.36), channel_id=1, source_target_pairs={{0,96},{32,0},{64,32},{96,64},{1,97},{33,1},{65,33},{97,65},{2,98}... | collective-permute-start | bytes 884744 | tf_op jit(solution)/shard_map/ppermute | solution.py:31
  6.1 4.1 %collective-permute-start.16 = (f32[1,128]{1,0:T(1,128)S(1)}, f32[1,128]{1,0:T(1,128)S(1)}, u32[]{:S(2)}, u32[]{:S(2)}) collective-permute-start(f32[1,128]{1,0:T(1,128)S(1)} %shard_map.85.ids.refs_0_), channel_id=1, source_target_pairs={{0,3},{1,0},{2,1},{3,2},{4,7},{5,4},{6,5},{7,6},{8,11},{9,8},{10,9... | collective-permute-start | bytes 1544 | tf_op jit(solution)/shard_map/ppermute | solution.py:31
  11.7 3.6 %collective-permute-done.15.refs_2_ = f32[1,128]{1,0:T(1,128)S(1)} collective-permute-done((f32[1,128]{1,0:T(1,128)S(1)}, f32[1,128]{1,0:T(1,128)S(1)}, u32[]{:S(2)}, u32[]{:S(2)}) %collective-permute-start.15) | collective-permute-done | bytes 544 | tf_op jit(solution)/shard_map/ppermute | solution.py:31
  21.6 2.8 %collective-permute-done.18.refs_2_ = f32[4,128]{1,0:T(4,128)S(1)} collective-permute-done((f32[4,128]{1,0:T(4,128)S(1)}, f32[4,128]{1,0:T(4,128)S(1)}, u32[]{:S(2)}, u32[]{:S(2)}) %collective-permute-start.18) | collective-permute-done | bytes 2080 | tf_op jit(solution)/shard_map/ppermute | solution.py:31
  27.2 3.6 %collective-permute-start.1 = (f32[432,128]{1,0:T(8,128)S(1)}, f32[432,128]{1,0:T(8,128)S(1)}, u32[]{:S(2)}, u32[]{:S(2)}) collective-permute-start(f32[432,128]{1,0:T(8,128)S(1)} %get-tuple-element.76), channel_id=1, source_target_pairs={{0,15},{1,2},{2,1},{3,4},{4,3},{5,6},{6,5},{7,8},{8,7},{9,10},{10,... | collective-permute-start | bytes 663560 | tf_op jit(solution)/shard_map/ppermute | solution.py:36
  35.3 3.1 %collective-permute-done.1.in_b = f32[432,128]{1,0:T(8,128)S(1)} collective-permute-done((f32[432,128]{1,0:T(8,128)S(1)}, f32[432,128]{1,0:T(8,128)S(1)}, u32[]{:S(2)}, u32[]{:S(2)}) %collective-permute-start.1) | collective-permute-done | bytes 221216 | tf_op jit(solution)/shard_map/ppermute | solution.py:36
  43.0 3.6 %collective-permute-done.5.refs_2_ = f32[1,24,256]{2,1,0:T(8,128)S(1)} collective-permute-done((f32[1,24,256]{2,1,0:T(8,128)S(1)}, f32[1,24,256]{2,1,0:T(8,128)S(1)}, u32[]{:S(2)}, u32[]{:S(2)}) %collective-permute-start.5) | collective-permute-done | bytes 24608 | tf_op jit(solution)/shard_map/ppermute | solution.py:31
  49.0 3.3 %collective-permute-start.27 = (f32[192,384]{1,0:T(8,128)S(1)}, f32[192,384]{1,0:T(8,128)S(1)}, u32[]{:S(2)}, u32[]{:S(2)}) collective-permute-start(f32[192,384]{1,0:T(8,128)S(1)} %add.3.refs_8_), channel_id=1, source_target_pairs={{0,3},{1,0},{2,1},{3,2},{4,7},{5,4},{6,5},{7,6},{8,11},{9,8},{10,9... | collective-permute-start | bytes 884744 | tf_op jit(solution)/shard_map/ppermute | solution.py:31
  55.3 4.3 %collective-permute-done.7.refs_1_ = f32[4,24,256]{2,1,0:T(8,128)S(1)} collective-permute-done((f32[4,24,256]{2,1,0:T(8,128)S(1)}, f32[4,24,256]{2,1,0:T(8,128)S(1)}, u32[]{:S(2)}, u32[]{:S(2)}) %collective-permute-start.7) | collective-permute-done | bytes 98336 | tf_op jit(solution)/shard_map/ppermute | solution.py:31
  61.1 4.1 %collective-permute-done.27.refs_11_ = f32[192,384]{1,0:T(8,128)S(1)} collective-permute-done((f32[192,384]{1,0:T(8,128)S(1)}, f32[192,384]{1,0:T(8,128)S(1)}, u32[]{:S(2)}, u32[]{:S(2)}) %collective-permute-start.27) | collective-permute-done | bytes 294944 | tf_op jit(solution)/shard_map/ppermute | solution.py:31
  65.2 3.4 %collective-permute-done.25.refs_9_ = f32[192,384]{1,0:T(8,128)S(1)} collective-permute-done((f32[192,384]{1,0:T(8,128)S(1)}, f32[192,384]{1,0:T(8,128)S(1)}, u32[]{:S(2)}, u32[]{:S(2)}) %collective-permute-start.25) | collective-permute-done | bytes 294944 | tf_op jit(solution)/shard_map/ppermute | solution.py:31
  74.1 5.0 %all-to-all-start = ((f32[16,24,256]{2,1,0:T(8,128)}), f32[16,24,256]{2,1,0:T(8,128)}, u32[]{:S(2)}, u32[]{:S(2)}) async-start(f32[16,24,256]{2,1,0:T(8,128)} %copy-done.5), calls=%async_computation | async-start | bytes 786432 | tf_op jit(solution)/shard_map/all_to_all | solution.py:40
  82.0 2.9 %shard_map.95 = (f32[128,176]{1,0:T(8,128)S(1)}, f32[1024,176]{1,0:T(8,128)S(1)}, f32[128,176]{1,0:T(8,128)S(1)}, f32[1024,176]{1,0:T(8,128)S(1)}, f32[1,176]{1,...) custom-call(bf16[1152,176]{1,0:T(8,128)(2,1)S(1)} %copy-done.19, bf16[1152,1152]{1,0:T(8,128)(2,1)S(1)} %bitcast.28, ...), custom_call_target="tpu_custom_call" | custom-call | tf_op jit(solution)/shard_map/pallas_call | solution.py:49
  97.0 4.2 %collective-permute-start.29 = (f32[432,128]{1,0:T(8,128)S(1)}, f32[432,128]{1,0:T(8,128)S(1)}, u32[]{:S(2)}, u32[]{:S(2)}) collective-permute-start(f32[432,128]{1,0:T(8,128)S(1)} %get-tuple-element.94), channel_id=1, source_target_pairs={{0,15},{1,2},{2,1},{3,4},{4,3},{5,6},{6,5},{7,8},{8,7},{9,10},{10,... | collective-permute-start | bytes 663560 | tf_op jit(solution)/shard_map/ppermute | solution.py:36
  104.7 8.4 %collective-permute-done.29.in_b = f32[432,128]{1,0:T(8,128)S(1)} collective-permute-done((f32[432,128]{1,0:T(8,128)S(1)}, f32[432,128]{1,0:T(8,128)S(1)}, u32[]{:S(2)}, u32[]{:S(2)}) %collective-permute-start.29) | collective-permute-done | bytes 221216 | tf_op jit(solution)/shard_map/ppermute | solution.py:36
  113.0 6.6 %collective-permute-done.31.in_y = f32[432,128]{1,0:T(8,128)S(1)} collective-permute-done((f32[432,128]{1,0:T(8,128)S(1)}, f32[432,128]{1,0:T(8,128)S(1)}, u32[]{:S(2)}, u32[]{:S(2)}) %collective-permute-start.31) | collective-permute-done | bytes 221216 | tf_op jit(solution)/shard_map/ppermute | solution.py:36
  127.1 3.0 %shard_map.98 = (f32[128,176]{1,0:T(8,128)S(1)}, f32[1024,176]{1,0:T(8,128)S(1)}, f32[128,176]{1,0:T(8,128)S(1)}, f32[1024,176]{1,0:T(8,128)S(1)}, f32[1,176]{1,...) custom-call(bf16[1152,176]{1,0:T(8,128)(2,1)S(1)} %get-tuple-element.98.balanced, ...), custom_call_target="tpu_custom_call" | custom-call | tf_op jit(solution)/shard_map/pallas_call | solution.py:49
  130.8 17.6 %all_to_all.20.terms = f32[16,24,256]{2,1,0:T(8,128)S(1)} all-to-all(f32[16,24,256]{2,1,0:T(8,128)S(1)} %shard_map.101), channel_id=1, replica_groups=mesh['y'=4,'c'=2,'x'=4,'z'=4] {'x','z'}, dimensions={0} | all-to-all | bytes 786432 | tf_op jit(solution)/shard_map/all_to_all | solution.py:40
  155.2 3.7 %collective-permute-done.43.in_b = f32[432,128]{1,0:T(8,128)S(1)} collective-permute-done((f32[432,128]{1,0:T(8,128)S(1)}, f32[432,128]{1,0:T(8,128)S(1)}, u32[]{:S(2)}, u32[]{:S(2)}) %collective-permute-start.43) | collective-permute-done | bytes 221216 | tf_op jit(solution)/shard_map/ppermute | solution.py:36
  163.6 3.3 %collective-permute-done.47.refs_2_ = f32[1,24,256]{2,1,0:T(8,128)S(1)} collective-permute-done((f32[1,24,256]{2,1,0:T(8,128)S(1)}, f32[1,24,256]{2,1,0:T(8,128)S(1)}, u32[]{:S(2)}, u32[]{:S(2)}) %collective-permute-start.47) | collective-permute-done | bytes 24608 | tf_op jit(solution)/shard_map/ppermute | solution.py:31
  171.9 3.6 %all-to-all-start.2 = ((f32[16,24,256]{2,1,0:T(8,128)}), f32[16,24,256]{2,1,0:T(8,128)S(1)}, u32[]{:S(2)}, u32[]{:S(2)}) async-start(f32[16,24,256]{2,1,0:T(8,128)} %shard_map.106), calls=%async_computation.2 | async-start | bytes 786432 | tf_op jit(solution)/shard_map/all_to_all | solution.py:40
  177.0 9.3 %all-to-all-done.2.terms = f32[16,24,256]{2,1,0:T(8,128)S(1)} async-done(((f32[16,24,256]{2,1,0:T(8,128)}), f32[16,24,256]{2,1,0:T(8,128)S(1)}, u32[]{:S(2)}, u32[]{:S(2)}) %all-to-all-start.2) | async-done | bytes 393248 | tf_op jit(solution)/shard_map/all_to_all | solution.py:40
  187.1 5.0 %all-to-all-start.3 = ((f32[128,1,256]{2,1,0:T(1,128)}), f32[128,1,256]{2,1,0:T(1,128)S(1)}, u32[]{:S(2)}, u32[]{:S(2)}) async-start(f32[128,1,256]{2,1,0:T(1,128)} %get-tuple-element.142), calls=%async_computation.3 | async-start | bytes 262144 | tf_op jit(solution)/shard_map/all_to_all | solution.py:40
  195.9 5.8 %all-to-all-done.3 = f32[128,1,256]{2,1,0:T(1,128)S(1)} async-done(((f32[128,1,256]{2,1,0:T(1,128)}), f32[128,1,256]{2,1,0:T(1,128)S(1)}, u32[]{:S(2)}, u32[]{:S(2)}) %all-to-all-start.3) | async-done | bytes 131104 | tf_op jit(solution)/shard_map/all_to_all | solution.py:40
  (193 shorter events, 83.9 us)
Async XLA Ops:
  0.6 30.1 %collective-permute-start.23 = (f32[192,384]{1,0:T(8,128)}, f32[192,384]{1,0:T(8,128)S(1)}, u32[]{:S(2)}, u32[]{:S(2)}) collective-permute-start(f32[192,384]{1,0:T(8,128)} %bitcast.36), channel_id=1, source_target_pairs={{0,96},{32,0},{64,32},{96,64},{1,97},{33,1},{65,33},{97,65},{2,98}... | collective-permute-start | bytes 884744 | tf_op jit(solution)/shard_map/ppermute | solution.py:31
  3.8 27.1 %collective-permute-start.22 = (f32[192,384]{1,0:T(8,128)}, f32[192,384]{1,0:T(8,128)S(1)}, u32[]{:S(2)}, u32[]{:S(2)}) collective-permute-start(f32[192,384]{1,0:T(8,128)} %bitcast.37), channel_id=1, source_target_pairs={{0,64},{32,96},{64,0},{96,32},{1,65},{33,97},{65,1},{97,33},{2,66}... | collective-permute-start | bytes 884744 | tf_op jit(solution)/shard_map/ppermute | solution.py:31
  4.5 28.6 %collective-permute-start.21 = (f32[192,384]{1,0:T(8,128)}, f32[192,384]{1,0:T(8,128)S(1)}, u32[]{:S(2)}, u32[]{:S(2)}) collective-permute-start(f32[192,384]{1,0:T(8,128)} %bitcast.38), channel_id=1, source_target_pairs={{0,32},{32,64},{64,96},{96,0},{1,33},{33,65},{65,97},{97,1},{2,34}... | collective-permute-start | bytes 884744 | tf_op jit(solution)/shard_map/ppermute | solution.py:31
  27.1 8.2 %collective-permute-start = (f32[432,128]{1,0:T(8,128)S(1)}, f32[432,128]{1,0:T(8,128)S(1)}, u32[]{:S(2)}, u32[]{:S(2)}) collective-permute-start(f32[432,128]{1,0:T(8,128)S(1)} %get-tuple-element.75), channel_id=1, source_target_pairs={{0,1},{1,0},{2,3},{3,2},{4,5},{5,4},{6,7},{7,6},{8,9},{9,8},{10,11... | collective-permute-start | bytes 663560 | tf_op jit(solution)/shard_map/ppermute | solution.py:36
  27.2 11.2 %collective-permute-start.1 = (f32[432,128]{1,0:T(8,128)S(1)}, f32[432,128]{1,0:T(8,128)S(1)}, u32[]{:S(2)}, u32[]{:S(2)}) collective-permute-start(f32[432,128]{1,0:T(8,128)S(1)} %get-tuple-element.76), channel_id=1, source_target_pairs={{0,15},{1,2},{2,1},{3,4},{4,3},{5,6},{6,5},{7,8},{8,7},{9,10},{10,... | collective-permute-start | bytes 663560 | tf_op jit(solution)/shard_map/ppermute | solution.py:36
  30.7 7.6 %collective-permute-start.2 = (f32[432,128]{1,0:T(8,128)S(1)}, f32[432,128]{1,0:T(8,128)S(1)}, u32[]{:S(2)}, u32[]{:S(2)}) collective-permute-start(f32[432,128]{1,0:T(8,128)S(1)} %get-tuple-element.77), channel_id=1, source_target_pairs={{0,16},{16,0},{32,48},{48,32},{64,80},{80,64},{96,112},{112,96},{1... | collective-permute-start | bytes 663560 | tf_op jit(solution)/shard_map/ppermute | solution.py:36
  30.9 7.5 %collective-permute-start.3 = (f32[432,128]{1,0:T(8,128)S(1)}, f32[432,128]{1,0:T(8,128)S(1)}, u32[]{:S(2)}, u32[]{:S(2)}) collective-permute-start(f32[432,128]{1,0:T(8,128)S(1)} %get-tuple-element.78), channel_id=1, source_target_pairs={{0,112},{16,32},{32,16},{48,64},{64,48},{80,96},{96,80},{112,0},{1... | collective-permute-start | bytes 663560 | tf_op jit(solution)/shard_map/ppermute | solution.py:36
  35.2 13.8 %collective-permute-start.24 = (f32[192,384]{1,0:T(8,128)S(1)}, f32[192,384]{1,0:T(8,128)S(1)}, u32[]{:S(2)}, u32[]{:S(2)}) collective-permute-start(f32[192,384]{1,0:T(8,128)S(1)} %get-tuple-element.82), channel_id=1, source_target_pairs={{0,16},{16,0},{1,17},{17,1},{2,18},{18,2},{3,19},{19,3},{4,20},{20... | collective-permute-start | bytes 884744 | tf_op jit(solution)/shard_map/ppermute | solution.py:31
  49.0 16.2 %collective-permute-start.27 = (f32[192,384]{1,0:T(8,128)S(1)}, f32[192,384]{1,0:T(8,128)S(1)}, u32[]{:S(2)}, u32[]{:S(2)}) collective-permute-start(f32[192,384]{1,0:T(8,128)S(1)} %add.3.refs_8_), channel_id=1, source_target_pairs={{0,3},{1,0},{2,1},{3,2},{4,7},{5,4},{6,5},{7,6},{8,11},{9,8},{10,9... | collective-permute-start | bytes 884744 | tf_op jit(solution)/shard_map/ppermute | solution.py:31
  52.3 12.9 %collective-permute-start.26 = (f32[192,384]{1,0:T(8,128)S(1)}, f32[192,384]{1,0:T(8,128)S(1)}, u32[]{:S(2)}, u32[]{:S(2)}) collective-permute-start(f32[192,384]{1,0:T(8,128)S(1)} %add.3.refs_8_), channel_id=1, source_target_pairs={{0,2},{1,3},{2,0},{3,1},{4,6},{5,7},{6,4},{7,5},{8,10},{9,11},{10,... | collective-permute-start | bytes 884744 | tf_op jit(solution)/shard_map/ppermute | solution.py:31
  52.3 16.3 %collective-permute-start.25 = (f32[192,384]{1,0:T(8,128)S(1)}, f32[192,384]{1,0:T(8,128)S(1)}, u32[]{:S(2)}, u32[]{:S(2)}) collective-permute-start(f32[192,384]{1,0:T(8,128)S(1)} %add.3.refs_8_), channel_id=1, source_target_pairs={{0,1},{1,2},{2,3},{3,0},{4,5},{5,6},{6,7},{7,4},{8,9},{9,10},{10,1... | collective-permute-start | bytes 884744 | tf_op jit(solution)/shard_map/ppermute | solution.py:31
  74.1 16.0 %all-to-all-start = ((f32[16,24,256]{2,1,0:T(8,128)}), f32[16,24,256]{2,1,0:T(8,128)}, u32[]{:S(2)}, u32[]{:S(2)}) async-start(f32[16,24,256]{2,1,0:T(8,128)} %copy-done.5), calls=%async_computation | async-start | bytes 786432 | tf_op jit(solution)/shard_map/all_to_all | solution.py:40
  95.0 9.6 %collective-permute-start.28 = (f32[432,128]{1,0:T(8,128)S(1)}, f32[432,128]{1,0:T(8,128)S(1)}, u32[]{:S(2)}, u32[]{:S(2)}) collective-permute-start(f32[432,128]{1,0:T(8,128)S(1)} %get-tuple-element.93), channel_id=1, source_target_pairs={{0,1},{1,0},{2,3},{3,2},{4,5},{5,4},{6,7},{7,6},{8,9},{9,8},{10,11... | collective-permute-start | bytes 663560 | tf_op jit(solution)/shard_map/ppermute | solution.py:36
  97.0 16.0 %collective-permute-start.29 = (f32[432,128]{1,0:T(8,128)S(1)}, f32[432,128]{1,0:T(8,128)S(1)}, u32[]{:S(2)}, u32[]{:S(2)}) collective-permute-start(f32[432,128]{1,0:T(8,128)S(1)} %get-tuple-element.94), channel_id=1, source_target_pairs={{0,15},{1,2},{2,1},{3,4},{4,3},{5,6},{6,5},{7,8},{8,7},{9,10},{10,... | collective-permute-start | bytes 663560 | tf_op jit(solution)/shard_map/ppermute | solution.py:36
  101.2 19.2 %collective-permute-start.32 = (f32[192,384]{1,0:T(8,128)S(1)}, f32[192,384]{1,0:T(8,128)S(1)}, u32[]{:S(2)}, u32[]{:S(2)}) collective-permute-start(f32[192,384]{1,0:T(8,128)S(1)} %copy-done.34), channel_id=1, source_target_pairs={{0,4},{4,8},{8,12},{12,0},{1,5},{5,9},{9,13},{13,1},{2,6},{6,10},{... | collective-permute-start | bytes 884744 | tf_op jit(solution)/shard_map/ppermute | solution.py:31
  101.2 21.1 %collective-permute-start.33 = (f32[192,384]{1,0:T(8,128)S(1)}, f32[192,384]{1,0:T(8,128)S(1)}, u32[]{:S(2)}, u32[]{:S(2)}) collective-permute-start(f32[192,384]{1,0:T(8,128)S(1)} %copy-done.32), channel_id=1, source_target_pairs={{0,8},{4,12},{8,0},{12,4},{1,9},{5,13},{9,1},{13,5},{2,10},{6,14},... | collective-permute-start | bytes 884744 | tf_op jit(solution)/shard_map/ppermute | solution.py:31
  103.5 23.3 %collective-permute-start.34 = (f32[192,384]{1,0:T(8,128)S(1)}, f32[192,384]{1,0:T(8,128)S(1)}, u32[]{:S(2)}, u32[]{:S(2)}) collective-permute-start(f32[192,384]{1,0:T(8,128)S(1)} %copy-done.30), channel_id=1, source_target_pairs={{0,12},{4,0},{8,4},{12,8},{1,13},{5,1},{9,5},{13,9},{2,14},{6,2},{... | collective-permute-start | bytes 884744 | tf_op jit(solution)/shard_map/ppermute | solution.py:31
  104.7 8.4 %collective-permute-start.30 = (f32[432,128]{1,0:T(8,128)S(1)}, f32[432,128]{1,0:T(8,128)S(1)}, u32[]{:S(2)}, u32[]{:S(2)}) collective-permute-start(f32[432,128]{1,0:T(8,128)S(1)} %get-tuple-element.95), channel_id=1, source_target_pairs={{0,16},{16,0},{32,48},{48,32},{64,80},{80,64},{96,112},{112,96},{1... | collective-permute-start | bytes 663560 | tf_op jit(solution)/shard_map/ppermute | solution.py:36
  122.3 8.1 %collective-permute-start.38 = (f32[1,24,256]{2,1,0:T(8,128)S(1)}, f32[1,24,256]{2,1,0:T(8,128)S(1)}, u32[]{:S(2)}, u32[]{:S(2)}) collective-permute-start(f32[1,24,256]{2,1,0:T(8,128)S(1)} %get-tuple-element.113.refs_0_), channel_id=1, source_target_pairs={{0,16},{16,0},{1,17},{17,1},{2,18},{18,2},{3,19},{19,3},{4,20},{20... | collective-permute-start | bytes 73736 | tf_op jit(solution)/shard_map/ppermute | solution.py:31
  149.5 9.4 %collective-permute-start.43 = (f32[432,128]{1,0:T(8,128)S(1)}, f32[432,128]{1,0:T(8,128)S(1)}, u32[]{:S(2)}, u32[]{:S(2)}) collective-permute-start(f32[432,128]{1,0:T(8,128)S(1)} %get-tuple-element.120), channel_id=1, source_target_pairs={{0,15},{1,2},{2,1},{3,4},{4,3},{5,6},{6,5},{7,8},{8,7},{9,10},{10,... | collective-permute-start | bytes 663560 | tf_op jit(solution)/shard_map/ppermute | solution.py:36
  162.5 8.4 %collective-permute-start.49 = (f32[1,24,256]{2,1,0:T(8,128)S(1)}, f32[1,24,256]{2,1,0:T(8,128)S(1)}, u32[]{:S(2)}, u32[]{:S(2)}) collective-permute-start(f32[1,24,256]{2,1,0:T(8,128)S(1)} %get-tuple-element.134.refs_0_), channel_id=1, source_target_pairs={{0,16},{16,0},{1,17},{17,1},{2,18},{18,2},{3,19},{19,3},{4,20},{20... | collective-permute-start | bytes 73736 | tf_op jit(solution)/shard_map/ppermute | solution.py:31
  163.6 7.3 %collective-permute-start.52 = (f32[1,24,256]{2,1,0:T(8,128)S(1)}, f32[1,24,256]{2,1,0:T(8,128)S(1)}, u32[]{:S(2)}, u32[]{:S(2)}) collective-permute-start(f32[1,24,256]{2,1,0:T(8,128)S(1)} %collective-permute-done.48.refs_3_), channel_id=1, source_target_pairs={{0,16},{16,0},{1,17},{17,1},{2,18},{18,2},{3,19},{19,3},{4,20},{20... | collective-permute-start | bytes 73736 | tf_op jit(solution)/shard_map/ppermute | solution.py:31
  171.9 14.4 %all-to-all-start.2 = ((f32[16,24,256]{2,1,0:T(8,128)}), f32[16,24,256]{2,1,0:T(8,128)S(1)}, u32[]{:S(2)}, u32[]{:S(2)}) async-start(f32[16,24,256]{2,1,0:T(8,128)} %shard_map.106), calls=%async_computation.2 | async-start | bytes 786432 | tf_op jit(solution)/shard_map/all_to_all | solution.py:40
  187.1 14.6 %all-to-all-start.3 = ((f32[128,1,256]{2,1,0:T(1,128)}), f32[128,1,256]{2,1,0:T(1,128)S(1)}, u32[]{:S(2)}, u32[]{:S(2)}) async-start(f32[128,1,256]{2,1,0:T(1,128)} %get-tuple-element.142), calls=%async_computation.3 | async-start | bytes 262144 | tf_op jit(solution)/shard_map/all_to_all | solution.py:40
  (67 other events, 380.1 us)

commit v8 on v5

--- a/solution.py
+++ b/solution.py
@@ -145,18 +145,18 @@
     return (1 - odd_b, odd_b, 3 - odd_a, 2 + odd_a)
 
 
-def ids_kernel(ids, side_rows, right, flex, told, line, counts):
+def ids_kernel(ids, right, flex, told, line):
     line[...] = jnp.zeros_like(line)
     line[:, 0 : ids.shape[1]] = ids[...].astype(F32)
     told[...] = jnp.broadcast_to(line[...][None], told.shape)
+
+
+def first_kernel(after, ids, side_rows, right, flex, flexed, extra, counts, *sends):
+    direction = (right[...] / cheb_center).astype(BF16)
+    flexed[...] = dot(flex[...], direction, ((1,), (1,)))
     live = side_rows[...].astype(F32)
     which = lax.broadcasted_iota(jnp.int32, counts.shape, 0)
     counts[...] = jnp.where(which == 0, live[:, 0:1], live[:, 1:2])
-
-
-def first_kernel(after, ids, counts, right, flex, flexed, extra, *sends):
-    direction = (right[...] / cheb_center).astype(BF16)
-    flexed[...] = dot(flex[...], direction, ((1,), (1,)))
     send_sides(counts, flexed, *sends)
     column = jnp.broadcast_to(ids[...], (LANES, LANES)).T
     extra[...] = jnp.zeros_like(extra)
@@ -215,12 +215,10 @@
         told[k] = told[0]
 
 
-def step_on(steps, flex, dir_low, low, new_dir_low, flex_base, rounded):
+def step_on(steps, flex, dir_low, low, new_dir_low, flex_base):
     new_dir = steps[0] * dir_low + steps[1] * low
     new_dir_low[...] = new_dir
-    rounded[0:TOP, :] = jnp.zeros((TOP, rounded.shape[1]), BF16)
-    rounded[TOP:, :] = new_dir.astype(BF16)
-    flex_base[...] = dot(flex[...], rounded[...])
+    flex_base[...] = dot(flex[:, TOP:], new_dir.astype(BF16))
 
 
 def first_bulk_kernel(steps, after, balanced, stiff, flex, right, *outs):
@@ -355,15 +353,15 @@
     for k in range(1, NY):
         inv_blocks.append(turned(inv_t, "y", NY, k))
 
-    own_ids, ids_line, counts = call(
-        ids_kernel, [shape(N_GY, 1, LANES), shape(1, LANES), shape(TILE, LANES)], unread=(right, flex_block)
-    )(corner_map[0], side_rows[0])
+    own_ids, ids_line = call(
+        ids_kernel, [shape(N_GY, 1, LANES), shape(1, LANES)], unread=(right, flex_block)
+    )(corner_map[0])
     own_ids = to_all(own_ids, GY).reshape(N_GY, LANES)
 
     sides = [shape(side + side // 2, LANES)] * SIDES
-    flexed, extra, *sends = call(
-        first_kernel, [shape(order, loads), shape(corners, width)] + sides
-    )(own_ids, ids_line, counts, right, flex_block)
+    flexed, extra, counts, *sends = call(
+        first_kernel, [shape(order, loads), shape(corners, width), shape(TILE, LANES)] + sides
+    )(own_ids, ids_line, side_rows[0], right, flex_block)
 
     other_ids = turned(own_ids, "c", NC, 1)
     own_rows, other_rows = call(
@@ -407,7 +405,6 @@
         outs = call(
             functools.partial(kernel, steps),
             [tops, lows, tops, lows, shape(1, loads)] + ([] if last else [lows, shape(order, loads)]),
-            scratch=[] if last else [pltpu.VMEM((order, loads), BF16)],
         )(*order_after, balanced, stiff_block, flex_block, *state)
         res_top, res_low, sol_top, sol_low, squares = outs[:5]
         if iteration == 0:

time: 195 us -> 194 us (level)
  transfers between devices with their start and end apart: 41 -> 41, of which waited for: 20 -> 20; matrix products, arithmetic and copies ran while one was open for 3% -> 3% of each run, Pallas kernels for 8% -> 7%
where the time goes in v8:
time: 194 us; the launch traced here: 192 us
  waiting for transfers between devices  58.4 us (30%)
  blocking collectives  49 us (25%)
  starting transfers between devices  46.1 us (24%)
  Pallas kernels  24.2 us (12%)
  local copies, waits for them, and re-layouts  10.8 us (6%)
  other arithmetic  3.05 us (2%)
    all_to_all x3, blocking collectives, to_all(): return lax.all_to_all(copies, axes, split_axis=0, concat_axis=0, tiled=True)  49 us
    pallas_call x20, Pallas kernels, run(): pl.pallas_call(body, out_shape=outs, in_specs=[vm() for _ in operands] +...  24.2 us
    ppermute x26, starting transfers between devices, turned(): lax.ppermute(array, axes, [(i, (i + by) % count) for i in range(count)])  21.4 us
    ppermute x26, waiting for transfers between devices, turned(): lax.ppermute(array, axes, [(i, (i + by) % count) for i in range(count)])  21 us
    ppermute x12, waiting for transfers between devices, swapped(): return lax.ppermute(array, axes, pairs)  20.6 us
    all_to_all x3, waiting for transfers between devices, to_all(): return lax.all_to_all(copies, axes, split_axis=0, concat_axis=0, tiled=True)  16.8 us
    all_to_all x3, starting transfers between devices, to_all(): return lax.all_to_all(copies, axes, split_axis=0, concat_axis=0, tiled=True)  12.9 us
    ppermute x12, starting transfers between devices, swapped(): return lax.ppermute(array, axes, pairs)  11.8 us
  transfers between devices with their start and end apart: 41, of which 20 were waited for; matrix products, arithmetic and copies ran while one was open for 3% of the time, Pallas kernels for 7%

profile of v8, /device:TPU:0, one launch (start us, length us, event | category | flops | bytes accessed | tf_op | source)
XLA Modules:
  0.0 192.4 jit_solution(7101564686045170257)
XLA Ops:
  1.3 15.6 %all_to_all.30 = f32[16,1,128]{2,1,0:T(1,128)S(1)} all-to-all(f32[16,1,128]{2,1,0:T(1,128)S(1)} %get-tuple-element.75), channel_id=1, replica_groups=mesh['y'=4,'c'=2,'x'=4,'z'=4] {'x','z'}, dimensions={0} | all-to-all | bytes 16384 | tf_op jit(solution)/shard_map/all_to_all | solution.py:40
  20.6 3.1 %collective-permute-start.3 = (f32[432,128]{1,0:T(8,128)S(1)}, f32[432,128]{1,0:T(8,128)S(1)}, u32[]{:S(2)}, u32[]{:S(2)}) collective-permute-start(f32[432,128]{1,0:T(8,128)S(1)} %get-tuple-element.82), channel_id=1, source_target_pairs={{0,112},{16,32},{32,16},{48,64},{64,48},{80,96},{96,80},{112,0},{1... | collective-permute-start | bytes 663560 | tf_op jit(solution)/shard_map/ppermute | solution.py:36
  24.5 2.9 %collective-permute-start.7 = (f32[192,384]{1,0:T(8,128)}, f32[192,384]{1,0:T(8,128)}, u32[]{:S(2)}, u32[]{:S(2)}) collective-permute-start(f32[192,384]{1,0:T(8,128)} %bitcast.6.refs_0_), channel_id=1, source_target_pairs={{0,64},{32,96},{64,0},{96,32},{1,65},{33,97},{65,1},{97,33},{2,66}... | collective-permute-start | bytes 884744 | tf_op jit(solution)/shard_map/ppermute | solution.py:31
  31.9 4.3 %all-to-all-start.1 = ((f32[16,24,256]{2,1,0:T(8,128)}), f32[16,24,256]{2,1,0:T(8,128)}, u32[]{:S(2)}, u32[]{:S(2)}) async-start(f32[16,24,256]{2,1,0:T(8,128)} %copy-done.11), calls=%async_computation.1 | async-start | bytes 786432 | tf_op jit(solution)/shard_map/all_to_all | solution.py:40
  41.2 4.0 %shard_map.89 = (f32[192,384]{1,0:T(8,128)S(1)}, f32[192,384]{1,0:T(8,128)}) custom-call(f32[16,128]{1,0:T(8,128)S(1)} %bitcast.39, f32[16,128]{1,0:T(8,128)S(1)} %collective-permute-done.5.ids_other, f32[192,384]{1,0:T(8,128)} %bitcast.6.refs_0_, f32[192,384]{1,0:T(8,128)} %collective-permute-done.6.refs_1_, f32[192,384]{1,0:T(8,128)} %collective-permute-done.7.refs_2_, ...), custom_call_target="tpu_custom_call" | custom-call | tf_op jit(solution)/shard_map/pallas_call | solution.py:49
  54.0 3.9 %shard_map.88 = (f32[128,176]{1,0:T(8,128)S(1)}, f32[1024,176]{1,0:T(8,128)S(1)}, f32[128,176]{1,0:T(8,128)S(1)}, f32[1024,176]{1,0:T(8,128)S(1)}, f32[1,176]{1,...) custom-call(f32[16,24,256]{2,1,0:T(8,128)} %all-to-all-done.1.after.own.values, ...), custom_call_target="tpu_custom_call" | custom-call | tf_op jit(solution)/shard_map/pallas_call | solution.py:49
  58.9 3.1 %collective-permute-done.11.refs_2_ = f32[192,384]{1,0:T(8,128)S(1)} collective-permute-done((f32[192,384]{1,0:T(8,128)S(1)}, f32[192,384]{1,0:T(8,128)S(1)}, u32[]{:S(2)}, u32[]{:S(2)}) %collective-permute-start.11) | collective-permute-done | bytes 294944 | tf_op jit(solution)/shard_map/ppermute | solution.py:31
  62.0 5.1 %collective-permute-done.10.refs_1_ = f32[192,384]{1,0:T(8,128)S(1)} collective-permute-done((f32[192,384]{1,0:T(8,128)S(1)}, f32[192,384]{1,0:T(8,128)S(1)}, u32[]{:S(2)}, u32[]{:S(2)}) %collective-permute-start.10) | collective-permute-done | bytes 294944 | tf_op jit(solution)/shard_map/ppermute | solution.py:31
  67.1 3.1 %shard_map.90 = (bf16[384,384]{1,0:T(8,128)(2,1)S(1)}, bf16[384,384]{1,0:T(8,128)(2,1)S(1)}, bf16[384,384]{1,0:T(8,128)(2,1)S(1)}, bf16[384,384]{1,0:T(8,128)(2,...) custom-call(f32[16,24,256]{2,1,0:T(8,128)} %all-to-all-done.1.after.o, ...), custom_call_target="tpu_custom_call" | custom-call | tf_op jit(solution)/shard_map/pallas_call | solution.py:49
  72.1 15.9 %all_to_all.31.terms = f32[16,24,256]{2,1,0:T(8,128)S(1)} all-to-all(f32[16,24,256]{2,1,0:T(8,128)S(1)} %shard_map.92), channel_id=1, replica_groups=mesh['y'=4,'c'=2,'x'=4,'z'=4] {'x','z'}, dimensions={0} | all-to-all | bytes 786432 | tf_op jit(solution)/shard_map/all_to_all | solution.py:40
  95.2 6.9 %collective-permute-done.14.in_b = f32[432,128]{1,0:T(8,128)S(1)} collective-permute-done((f32[432,128]{1,0:T(8,128)S(1)}, f32[432,128]{1,0:T(8,128)S(1)}, u32[]{:S(2)}, u32[]{:S(2)}) %collective-permute-start.14) | collective-permute-done | bytes 221216 | tf_op jit(solution)/shard_map/ppermute | solution.py:36
  102.1 6.6 %collective-permute-done.16.in_y = f32[432,128]{1,0:T(8,128)S(1)} collective-permute-done((f32[432,128]{1,0:T(8,128)S(1)}, f32[432,128]{1,0:T(8,128)S(1)}, u32[]{:S(2)}, u32[]{:S(2)}) %collective-permute-start.16) | collective-permute-done | bytes 221216 | tf_op jit(solution)/shard_map/ppermute | solution.py:36
  109.3 2.5 %collective-permute-start.22 = (f32[1,24,256]{2,1,0:T(8,128)S(1)}, f32[1,24,256]{2,1,0:T(8,128)S(1)}, u32[]{:S(2)}, u32[]{:S(2)}) collective-permute-start(f32[1,24,256]{2,1,0:T(8,128)S(1)} %get-tuple-element.117.refs_0_), channel_id=1, source_target_pairs={{0,96},{32,0},{64,32},{96,64},{1,97},{33,1},{65,33},{97,65},{2,98}... | collective-permute-start | bytes 73736 | tf_op jit(solution)/shard_map/ppermute | solution.py:31
  113.3 3.8 %collective-permute-done.21.refs_2_ = f32[1,24,256]{2,1,0:T(8,128)S(1)} collective-permute-done((f32[1,24,256]{2,1,0:T(8,128)S(1)}, f32[1,24,256]{2,1,0:T(8,128)S(1)}, u32[]{:S(2)}, u32[]{:S(2)}) %collective-permute-start.21) | collective-permute-done | bytes 24608 | tf_op jit(solution)/shard_map/ppermute | solution.py:31
  117.9 3.0 %shard_map.95 = (f32[128,176]{1,0:T(8,128)S(1)}, f32[1024,176]{1,0:T(8,128)S(1)}, f32[128,176]{1,0:T(8,128)S(1)}, f32[1024,176]{1,0:T(8,128)S(1)}, f32[1,176]{1,...) custom-call(bf16[1152,176]{1,0:T(8,128)(2,1)S(1)} %get-tuple-element.102.balanced, ...), custom_call_target="tpu_custom_call" | custom-call | tf_op jit(solution)/shard_map/pallas_call | solution.py:49
  121.6 17.5 %all_to_all.32.terms = f32[16,24,256]{2,1,0:T(8,128)S(1)} all-to-all(f32[16,24,256]{2,1,0:T(8,128)S(1)} %shard_map.98), channel_id=1, replica_groups=mesh['y'=4,'c'=2,'x'=4,'z'=4] {'x','z'}, dimensions={0} | all-to-all | bytes 786432 | tf_op jit(solution)/shard_map/all_to_all | solution.py:40
  140.1 2.2 %collective-permute-start.28 = (f32[432,128]{1,0:T(8,128)S(1)}, f32[432,128]{1,0:T(8,128)S(1)}, u32[]{:S(2)}, u32[]{:S(2)}) collective-permute-start(f32[432,128]{1,0:T(8,128)S(1)} %get-tuple-element.124), channel_id=1, source_target_pairs={{0,15},{1,2},{2,1},{3,4},{4,3},{5,6},{6,5},{7,8},{8,7},{9,10},{10,... | collective-permute-start | bytes 663560 | tf_op jit(solution)/shard_map/ppermute | solution.py:36
  143.2 2.6 %collective-permute-done.27.in_a = f32[432,128]{1,0:T(8,128)S(1)} collective-permute-done((f32[432,128]{1,0:T(8,128)S(1)}, f32[432,128]{1,0:T(8,128)S(1)}, u32[]{:S(2)}, u32[]{:S(2)}) %collective-permute-start.27) | collective-permute-done | bytes 221216 | tf_op jit(solution)/shard_map/ppermute | solution.py:36
  145.8 3.8 %collective-permute-done.28.in_b = f32[432,128]{1,0:T(8,128)S(1)} collective-permute-done((f32[432,128]{1,0:T(8,128)S(1)}, f32[432,128]{1,0:T(8,128)S(1)}, u32[]{:S(2)}, u32[]{:S(2)}) %collective-permute-start.28) | collective-permute-done | bytes 221216 | tf_op jit(solution)/shard_map/ppermute | solution.py:36
  161.9 3.6 %all-to-all-start.4 = ((f32[16,24,256]{2,1,0:T(8,128)}), f32[16,24,256]{2,1,0:T(8,128)S(1)}, u32[]{:S(2)}, u32[]{:S(2)}) async-start(f32[16,24,256]{2,1,0:T(8,128)} %shard_map.103), calls=%async_computation.4 | async-start | bytes 786432 | tf_op jit(solution)/shard_map/all_to_all | solution.py:40
  166.9 9.3 %all-to-all-done.4.terms = f32[16,24,256]{2,1,0:T(8,128)S(1)} async-done(((f32[16,24,256]{2,1,0:T(8,128)}), f32[16,24,256]{2,1,0:T(8,128)S(1)}, u32[]{:S(2)}, u32[]{:S(2)}) %all-to-all-start.4) | async-done | bytes 393248 | tf_op jit(solution)/shard_map/all_to_all | solution.py:40
  176.9 5.0 %all-to-all-start.5 = ((f32[128,1,256]{2,1,0:T(1,128)}), f32[128,1,256]{2,1,0:T(1,128)S(1)}, u32[]{:S(2)}, u32[]{:S(2)}) async-start(f32[128,1,256]{2,1,0:T(1,128)} %get-tuple-element.146), calls=%async_computation.5 | async-start | bytes 262144 | tf_op jit(solution)/shard_map/all_to_all | solution.py:40
  183.1 2.5 %copy.13 = f32[1,1,176,1152]{3,2,1,0:T(8,128)} copy(f32[1,1,176,1152]{2,3,1,0:T(8,128)} %maximum_bitcast_fusion.1) | data formatting | bytes 1622016
  185.8 5.8 %all-to-all-done.5 = f32[128,1,256]{2,1,0:T(1,128)S(1)} async-done(((f32[128,1,256]{2,1,0:T(1,128)}), f32[128,1,256]{2,1,0:T(1,128)S(1)}, u32[]{:S(2)}, u32[]{:S(2)}) %all-to-all-start.5) | async-done | bytes 131104 | tf_op jit(solution)/shard_map/all_to_all | solution.py:40
  (122 shorter events, 55.3 us)
Async XLA Ops:
  18.8 9.3 %collective-permute-start.1 = (f32[432,128]{1,0:T(8,128)S(1)}, f32[432,128]{1,0:T(8,128)S(1)}, u32[]{:S(2)}, u32[]{:S(2)}) collective-permute-start(f32[432,128]{1,0:T(8,128)S(1)} %get-tuple-element.80), channel_id=1, source_target_pairs={{0,15},{1,2},{2,1},{3,4},{4,3},{5,6},{6,5},{7,8},{8,7},{9,10},{10,... | collective-permute-start | bytes 663560 | tf_op jit(solution)/shard_map/ppermute | solution.py:36
  20.6 9.0 %collective-permute-start.2 = (f32[432,128]{1,0:T(8,128)S(1)}, f32[432,128]{1,0:T(8,128)S(1)}, u32[]{:S(2)}, u32[]{:S(2)}) collective-permute-start(f32[432,128]{1,0:T(8,128)S(1)} %get-tuple-element.81), channel_id=1, source_target_pairs={{0,16},{16,0},{32,48},{48,32},{64,80},{80,64},{96,112},{112,96},{1... | collective-permute-start | bytes 663560 | tf_op jit(solution)/shard_map/ppermute | solution.py:36
  20.6 9.0 %collective-permute-start.3 = (f32[432,128]{1,0:T(8,128)S(1)}, f32[432,128]{1,0:T(8,128)S(1)}, u32[]{:S(2)}, u32[]{:S(2)}) collective-permute-start(f32[432,128]{1,0:T(8,128)S(1)} %get-tuple-element.82), channel_id=1, source_target_pairs={{0,112},{16,32},{32,16},{48,64},{64,48},{80,96},{96,80},{112,0},{1... | collective-permute-start | bytes 663560 | tf_op jit(solution)/shard_map/ppermute | solution.py:36
  23.8 16.7 %collective-permute-start.8 = (f32[192,384]{1,0:T(8,128)}, f32[192,384]{1,0:T(8,128)}, u32[]{:S(2)}, u32[]{:S(2)}) collective-permute-start(f32[192,384]{1,0:T(8,128)} %bitcast.6.refs_0_), channel_id=1, source_target_pairs={{0,96},{32,0},{64,32},{96,64},{1,97},{33,1},{65,33},{97,65},{2,98}... | collective-permute-start | bytes 884744 | tf_op jit(solution)/shard_map/ppermute | solution.py:31
  24.5 15.9 %collective-permute-start.7 = (f32[192,384]{1,0:T(8,128)}, f32[192,384]{1,0:T(8,128)}, u32[]{:S(2)}, u32[]{:S(2)}) collective-permute-start(f32[192,384]{1,0:T(8,128)} %bitcast.6.refs_0_), channel_id=1, source_target_pairs={{0,64},{32,96},{64,0},{96,32},{1,65},{33,97},{65,1},{97,33},{2,66}... | collective-permute-start | bytes 884744 | tf_op jit(solution)/shard_map/ppermute | solution.py:31
  28.1 13.1 %collective-permute-start.6 = (f32[192,384]{1,0:T(8,128)}, f32[192,384]{1,0:T(8,128)}, u32[]{:S(2)}, u32[]{:S(2)}) collective-permute-start(f32[192,384]{1,0:T(8,128)} %bitcast.6.refs_0_), channel_id=1, source_target_pairs={{0,32},{32,64},{64,96},{96,0},{1,33},{33,65},{65,97},{97,1},{2,34}... | collective-permute-start | bytes 884744 | tf_op jit(solution)/shard_map/ppermute | solution.py:31
  31.9 15.8 %all-to-all-start.1 = ((f32[16,24,256]{2,1,0:T(8,128)}), f32[16,24,256]{2,1,0:T(8,128)}, u32[]{:S(2)}, u32[]{:S(2)}) async-start(f32[16,24,256]{2,1,0:T(8,128)} %copy-done.11), calls=%async_computation.1 | async-start | bytes 786432 | tf_op jit(solution)/shard_map/all_to_all | solution.py:40
  47.6 19.4 %collective-permute-start.4 = (f32[16,24,256]{2,1,0:T(8,128)}, f32[16,24,256]{2,1,0:T(8,128)S(1)}, u32[]{:S(2)}, u32[]{:S(2)}) collective-permute-start(f32[16,24,256]{2,1,0:T(8,128)} %all-to-all-done.1.after.own.values), channel_id=1, source_target_pairs={{0,16},{16,0},{1,17},{17,1},{2,18},{18,2},{3,19},{19,3},{4,20},{20... | collective-permute-start | bytes 1179656 | tf_op jit(solution)/shard_map/ppermute | solution.py:31
  48.9 9.9 %collective-permute-start.12 = (f32[192,384]{1,0:T(8,128)S(1)}, f32[192,384]{1,0:T(8,128)S(1)}, u32[]{:S(2)}, u32[]{:S(2)}) collective-permute-start(f32[192,384]{1,0:T(8,128)S(1)} %add.3.refs_0_), channel_id=1, source_target_pairs={{0,3},{1,0},{2,1},{3,2},{4,7},{5,4},{6,5},{7,6},{8,11},{9,8},{10,9... | collective-permute-start | bytes 884744 | tf_op jit(solution)/shard_map/ppermute | solution.py:31
  50.5 11.4 %collective-permute-start.11 = (f32[192,384]{1,0:T(8,128)S(1)}, f32[192,384]{1,0:T(8,128)S(1)}, u32[]{:S(2)}, u32[]{:S(2)}) collective-permute-start(f32[192,384]{1,0:T(8,128)S(1)} %add.3.refs_0_), channel_id=1, source_target_pairs={{0,2},{1,3},{2,0},{3,1},{4,6},{5,7},{6,4},{7,5},{8,10},{9,11},{10,... | collective-permute-start | bytes 884744 | tf_op jit(solution)/shard_map/ppermute | solution.py:31
  51.4 15.7 %collective-permute-start.10 = (f32[192,384]{1,0:T(8,128)S(1)}, f32[192,384]{1,0:T(8,128)S(1)}, u32[]{:S(2)}, u32[]{:S(2)}) collective-permute-start(f32[192,384]{1,0:T(8,128)S(1)} %add.3.refs_0_), channel_id=1, source_target_pairs={{0,1},{1,2},{2,3},{3,0},{4,5},{5,6},{6,7},{7,4},{8,9},{9,10},{10,1... | collective-permute-start | bytes 884744 | tf_op jit(solution)/shard_map/ppermute | solution.py:31
  89.0 13.1 %collective-permute-start.14 = (f32[432,128]{1,0:T(8,128)S(1)}, f32[432,128]{1,0:T(8,128)S(1)}, u32[]{:S(2)}, u32[]{:S(2)}) collective-permute-start(f32[432,128]{1,0:T(8,128)S(1)} %get-tuple-element.98), channel_id=1, source_target_pairs={{0,15},{1,2},{2,1},{3,4},{4,3},{5,6},{6,5},{7,8},{8,7},{9,10},{10,... | collective-permute-start | bytes 663560 | tf_op jit(solution)/shard_map/ppermute | solution.py:36
  91.3 20.5 %collective-permute-start.17 = (f32[192,384]{1,0:T(8,128)S(1)}, f32[192,384]{1,0:T(8,128)S(1)}, u32[]{:S(2)}, u32[]{:S(2)}) collective-permute-start(f32[192,384]{1,0:T(8,128)S(1)} %get-tuple-element.110), channel_id=1, source_target_pairs={{0,4},{4,8},{8,12},{12,0},{1,5},{5,9},{9,13},{13,1},{2,6},{6,10},{... | collective-permute-start | bytes 884744 | tf_op jit(solution)/shard_map/ppermute | solution.py:31
  92.2 20.5 %collective-permute-start.18 = (f32[192,384]{1,0:T(8,128)S(1)}, f32[192,384]{1,0:T(8,128)S(1)}, u32[]{:S(2)}, u32[]{:S(2)}) collective-permute-start(f32[192,384]{1,0:T(8,128)S(1)} %get-tuple-element.111), channel_id=1, source_target_pairs={{0,8},{4,12},{8,0},{12,4},{1,9},{5,13},{9,1},{13,5},{2,10},{6,14},... | collective-permute-start | bytes 884744 | tf_op jit(solution)/shard_map/ppermute | solution.py:31
  93.6 24.0 %collective-permute-start.19 = (f32[192,384]{1,0:T(8,128)S(1)}, f32[192,384]{1,0:T(8,128)S(1)}, u32[]{:S(2)}, u32[]{:S(2)}) collective-permute-start(f32[192,384]{1,0:T(8,128)S(1)} %get-tuple-element.112), channel_id=1, source_target_pairs={{0,12},{4,0},{8,4},{12,8},{1,13},{5,1},{9,5},{13,9},{2,14},{6,2},{... | collective-permute-start | bytes 884744 | tf_op jit(solution)/shard_map/ppermute | solution.py:31
  95.2 7.0 %collective-permute-start.15 = (f32[432,128]{1,0:T(8,128)S(1)}, f32[432,128]{1,0:T(8,128)S(1)}, u32[]{:S(2)}, u32[]{:S(2)}) collective-permute-start(f32[432,128]{1,0:T(8,128)S(1)} %get-tuple-element.99), channel_id=1, source_target_pairs={{0,16},{16,0},{32,48},{48,32},{64,80},{80,64},{96,112},{112,96},{1... | collective-permute-start | bytes 663560 | tf_op jit(solution)/shard_map/ppermute | solution.py:36
  112.7 8.5 %collective-permute-start.23 = (f32[1,24,256]{2,1,0:T(8,128)S(1)}, f32[1,24,256]{2,1,0:T(8,128)S(1)}, u32[]{:S(2)}, u32[]{:S(2)}) collective-permute-start(f32[1,24,256]{2,1,0:T(8,128)S(1)} %get-tuple-element.117.refs_0_), channel_id=1, source_target_pairs={{0,16},{16,0},{1,17},{17,1},{2,18},{18,2},{3,19},{19,3},{4,20},{20... | collective-permute-start | bytes 73736 | tf_op jit(solution)/shard_map/ppermute | solution.py:31
  113.3 8.0 %collective-permute-start.26 = (f32[1,24,256]{2,1,0:T(8,128)S(1)}, f32[1,24,256]{2,1,0:T(8,128)S(1)}, u32[]{:S(2)}, u32[]{:S(2)}) collective-permute-start(f32[1,24,256]{2,1,0:T(8,128)S(1)} %collective-permute-done.22.refs_3_), channel_id=1, source_target_pairs={{0,16},{16,0},{1,17},{17,1},{2,18},{18,2},{3,19},{19,3},{4,20},{20... | collective-permute-start | bytes 73736 | tf_op jit(solution)/shard_map/ppermute | solution.py:31
  140.1 9.5 %collective-permute-start.28 = (f32[432,128]{1,0:T(8,128)S(1)}, f32[432,128]{1,0:T(8,128)S(1)}, u32[]{:S(2)}, u32[]{:S(2)}) collective-permute-start(f32[432,128]{1,0:T(8,128)S(1)} %get-tuple-element.124), channel_id=1, source_target_pairs={{0,15},{1,2},{2,1},{3,4},{4,3},{5,6},{6,5},{7,8},{8,7},{9,10},{10,... | collective-permute-start | bytes 663560 | tf_op jit(solution)/shard_map/ppermute | solution.py:36
  142.3 7.3 %collective-permute-start.29 = (f32[432,128]{1,0:T(8,128)S(1)}, f32[432,128]{1,0:T(8,128)S(1)}, u32[]{:S(2)}, u32[]{:S(2)}) collective-permute-start(f32[432,128]{1,0:T(8,128)S(1)} %get-tuple-element.125), channel_id=1, source_target_pairs={{0,16},{16,0},{32,48},{48,32},{64,80},{80,64},{96,112},{112,96},{1... | collective-permute-start | bytes 663560 | tf_op jit(solution)/shard_map/ppermute | solution.py:36
  142.3 7.3 %collective-permute-start.30 = (f32[432,128]{1,0:T(8,128)S(1)}, f32[432,128]{1,0:T(8,128)S(1)}, u32[]{:S(2)}, u32[]{:S(2)}) collective-permute-start(f32[432,128]{1,0:T(8,128)S(1)} %get-tuple-element.126), channel_id=1, source_target_pairs={{0,112},{16,32},{32,16},{48,64},{64,48},{80,96},{96,80},{112,0},{1... | collective-permute-start | bytes 663560 | tf_op jit(solution)/shard_map/ppermute | solution.py:36
  153.6 7.1 %collective-permute-start.34 = (f32[1,24,256]{2,1,0:T(8,128)S(1)}, f32[1,24,256]{2,1,0:T(8,128)S(1)}, u32[]{:S(2)}, u32[]{:S(2)}) collective-permute-start(f32[1,24,256]{2,1,0:T(8,128)S(1)} %get-tuple-element.138.refs_0_), channel_id=1, source_target_pairs={{0,16},{16,0},{1,17},{17,1},{2,18},{18,2},{3,19},{19,3},{4,20},{20... | collective-permute-start | bytes 73736 | tf_op jit(solution)/shard_map/ppermute | solution.py:31
  161.9 14.3 %all-to-all-start.4 = ((f32[16,24,256]{2,1,0:T(8,128)}), f32[16,24,256]{2,1,0:T(8,128)S(1)}, u32[]{:S(2)}, u32[]{:S(2)}) async-start(f32[16,24,256]{2,1,0:T(8,128)} %shard_map.103), calls=%async_computation.4 | async-start | bytes 786432 | tf_op jit(solution)/shard_map/all_to_all | solution.py:40
  176.9 14.6 %all-to-all-start.5 = ((f32[128,1,256]{2,1,0:T(1,128)}), f32[128,1,256]{2,1,0:T(1,128)S(1)}, u32[]{:S(2)}, u32[]{:S(2)}) async-start(f32[128,1,256]{2,1,0:T(1,128)} %get-tuple-element.146), calls=%async_computation.5 | async-start | bytes 262144 | tf_op jit(solution)/shard_map/all_to_all | solution.py:40
  (32 other events, 194.2 us)
